TPU v7x, 128 devices: a whole 4x4x4 slice. The times are simulated.
128 devices in a mesh: gx: 8 (over x_hi, z), gy: 16 (over x_lo, y, core).
Axes of the slice: x: 4 (x_hi: 2, x_lo: 2; x = x_hi * 2 + x_lo), y: 4, z: 4, core: 2. Of those that a mesh axis runs over, the one named last changes fastest.
Arguments:
- velocity: float32 [3, 4, 1024, 1024], P(None, None, 'gy', 'gx'), may hold values from -6 to 6
- stress: float32 [3, 3, 4, 1024, 1024], P(None, None, None, 'gy', 'gx'), may hold values from -2.4 to 2.4
- face_mask: int32 [3, 4, 1024, 1024], P(None, None, 'gy', 'gx'), may hold values 0 or 1
- zones: int32 [4, 1024, 1024], P(None, 'gy', 'gx'), may hold values from 0 to 7
- zone_table: float32 [3, 8], replicated, may hold values from 0.5 to 2
- impedance: float32 [2, 3, 1024, 1024], P(None, None, ('gx', 'gy')), may hold values from 0.5 to 2
- memory: float32 [2, 31, 1024, 1024], P(None, None, ('gx', 'gy')), may hold values from -0.9 to 0.9
- history: float32 [2, 3, 31, 2, 1024, 1024], P(None, None, None, None, ('gx', 'gy')), may hold values from -6 to 6
Outputs:
- new_velocity: float32 [3, 4, 1024, 1024], P(None, None, 'gy', 'gx')
- new_stress: float32 [3, 3, 4, 1024, 1024], P(None, None, None, 'gy', 'gx')
All inputs are finite; a program needn't handle non-finite values. No bound on the sum of `face_mask` on one device may be relied on, other than what follows from the above.
Results may differ from a plain program's by a relative error of at most 0.0001.
Values sent between devices are 32-bit elements; how exact they have to be, the bound alone decides.
No kernel may reach another device: no remote copies, remote signals or barrier semaphores. Data moves between devices by JAX's collectives and lax.ppermute only.
A program may use at most 128 MiB of HBM per device.

v0:
```python
import math

import jax
import jax.numpy as jnp
from jax import lax
from jax.sharding import PartitionSpec as P

STEPS = 2


time_step = 0.2
highest = lax.Precision.HIGHEST


def split_up(value, dim, peers):
    lengths = value.shape
    blocks = value.reshape(*lengths[:dim], peers, lengths[dim] // peers, *lengths[dim + 1 :])
    return jnp.moveaxis(blocks, dim, 0)


def laid_out(blocks, dim):
    lengths = list(blocks.shape[1:])
    lengths[dim] *= blocks.shape[0]
    return jnp.moveaxis(blocks, 0, dim).reshape(lengths)


def one_exchange(value, axis, axes, splits, concats):
    sizes = [lax.axis_size(a) for a in axes]
    blocks = split_up(value, splits[0], sizes[0])
    blocks = jnp.moveaxis(split_up(blocks, splits[1] + 1, sizes[1]), 0, 1)
    inside = blocks.shape[2:]
    blocks = blocks.reshape(-1, *inside)
    blocks = lax.all_to_all(blocks, axis, split_axis=0, concat_axis=0, tiled=True)
    blocks = laid_out(blocks.reshape(*sizes, *inside), concats[0] + 1)
    return laid_out(blocks, concats[1])


def shifted(value, axis, steps):
    count = lax.axis_size(axis)
    pairs = [(source, (source + steps) % count) for source in range(count)]
    return lax.ppermute(value, axis, pairs)


def split_point(length):
    for candidate in range(math.isqrt(length), 0, -1):
        return candidate
    return 1


def phase_pair(rows, cols, period):
    first = jnp.arange(rows, dtype=jnp.int32)[:, None]
    second = jnp.arange(cols, dtype=jnp.int32)[None, :]
    turns = first * second % period
    angles = turns.astype(jnp.float32) * (2.0 * math.pi / period)
    return (jnp.cos(angles), jnp.sin(angles))


def first_section(values, table):
    return jnp.einsum("...ab,ak->...kb", values, table, precision=highest)


def second_section(values, table):
    return jnp.einsum("...kb,bq->...qk", values, table, precision=highest)


def transform_last(real, imag, inverse):
    length = real.shape[-1]
    outer = split_point(length)
    inner = length // outer
    sign = 1.0 if inverse else -1.0
    lead = real.shape[:-1]
    cos_outer, sin_outer = phase_pair(outer, outer, outer)
    cos_inner, sin_inner = phase_pair(inner, inner, inner)
    cos_twist, sin_twist = phase_pair(outer, inner, length)
    real_in = real.reshape(lead + (outer, inner))
    imag_in = imag.reshape(lead + (outer, inner))
    mid_real = first_section(real_in, cos_outer) - sign * first_section(imag_in, sin_outer)
    mid_imag = first_section(imag_in, cos_outer) + sign * first_section(real_in, sin_outer)
    turn_real = mid_real * cos_twist - sign * mid_imag * sin_twist
    turn_imag = mid_imag * cos_twist + sign * mid_real * sin_twist
    out_real = second_section(turn_real, cos_inner) - sign * second_section(turn_imag, sin_inner)
    out_imag = second_section(turn_imag, cos_inner) + sign * second_section(turn_real, sin_inner)
    scale = 1.0 / math.sqrt(length)
    return (out_real.reshape(lead + (length,)) * scale, out_imag.reshape(lead + (length,)) * scale)


def body(velocity, stress, face_mask, zones, zone_table, impedance, memory, history):
    strike_count = lax.axis_size("gx")
    dip_count = lax.axis_size("gy")
    components, layers, rows_local, cols_local = velocity.shape
    width_x = cols_local * strike_count
    width_y = rows_local * dip_count
    sub_rows = rows_local // strike_count
    wave_local = history.shape[4]
    lag_count = history.shape[2]
    plane_count = 2 * components
    rigidity = jnp.zeros(zones.shape, jnp.float32)
    buoyancy = jnp.zeros(zones.shape, jnp.float32)
    cohesion = jnp.zeros(zones.shape, jnp.float32)
    for zone_index in range(zone_table.shape[1]):
        matched = zones == zone_index
        rigidity = jnp.where(matched, zone_table[0, zone_index], rigidity)
        buoyancy = jnp.where(matched, zone_table[1, zone_index], buoyancy)
        cohesion = jnp.where(matched, zone_table[2, zone_index], cohesion)
    cohesive = face_mask.astype(jnp.float32)
    recent = []
    for step_index in range(STEPS):
        along_x, along_y, along_z = (stress[:, 0], stress[:, 1], stress[:, 2])
        west_rim = shifted(along_x[..., cols_local - 1], "gx", 1)
        south_rim = shifted(along_y[:, :, rows_local - 1, :], "gy", 1)
        planes = jnp.stack([velocity[:, 0], velocity[:, layers - 1]])
        forward_pieces = planes.reshape(plane_count, strike_count, sub_rows, cols_local)
        strike_rows = lax.all_to_all(
            forward_pieces, "gx", split_axis=1, concat_axis=3, tiled=True
        ).reshape(plane_count, sub_rows, width_x)
        real_x, imag_x = transform_last(strike_rows, jnp.zeros_like(strike_rows), False)
        forward_packed = jnp.stack([real_x, imag_x], axis=1)
        outgoing = forward_packed.reshape(
            plane_count, 2, sub_rows, strike_count, dip_count, wave_local
        )
        forward_incoming = lax.all_to_all(
            lax.all_to_all(outgoing, "gx", split_axis=3, concat_axis=2, tiled=True),
            "gy",
            split_axis=4,
            concat_axis=2,
            tiled=True,
        )
        lines = forward_incoming.reshape(plane_count, 2, width_y, wave_local).transpose(0, 1, 3, 2)
        spec_real, spec_imag = transform_last(lines[:, 0], lines[:, 1], False)
        spectrum = jnp.stack([spec_real, spec_imag], axis=1).reshape(
            2, components, 2, wave_local, width_y
        )
        response = -impedance[:, :, None] * spectrum
        for offset in range(1, step_index + 1):
            response = response + memory[:, offset - 1][:, None, None] * recent[step_index - offset]
        tail_count = lag_count - step_index
        response = response + jnp.sum(
            memory[:, None, step_index:, None] * history[:, :, :tail_count], axis=2
        )
        recent.append(spectrum)
        spectra = response.reshape(plane_count, 2, wave_local, width_y)
        line_real, line_imag = transform_last(spectra[:, 0], spectra[:, 1], True)
        packed = jnp.stack([line_real, line_imag], axis=1)
        packed = packed.reshape(
            plane_count, 2, wave_local, dip_count, strike_count, sub_rows
        ).transpose(0, 1, 2, 4, 3, 5)
        incoming = one_exchange(packed, ("gx", "gy"), ("gx", "gy"), (3, 4), (2, 2))
        incoming = incoming.reshape(plane_count, 2, dip_count, strike_count, wave_local, sub_rows)
        incoming = incoming.transpose(0, 1, 3, 2, 4, 5).reshape(plane_count, 2, width_x, sub_rows)
        ordered = incoming.transpose(0, 1, 3, 2)
        plane_field, unused_imag = transform_last(ordered[:, 0], ordered[:, 1], True)
        pieces = plane_field.reshape(plane_count, sub_rows, strike_count, cols_local)
        restored = lax.all_to_all(pieces, "gx", split_axis=2, concat_axis=1, tiled=True)
        traction = restored.reshape(2, components, rows_local, cols_local)
        behind_x = jnp.concatenate([west_rim[..., None], along_x[..., :-1]], axis=3)
        behind_y = jnp.concatenate([south_rim[:, :, None], along_y[:, :, :-1]], axis=2)
        face_top = jnp.concatenate([along_z[:, :-1], traction[1][:, None]], axis=1)
        face_low = jnp.concatenate([traction[0][:, None], face_top[:, :-1]], axis=1)
        velocity = velocity + time_step * buoyancy * (
            along_x - behind_x + along_y - behind_y + face_top - face_low
        )
        east_rim = shifted(velocity[..., 0], "gx", -1)
        north_rim = shifted(velocity[:, :, 0, :], "gy", -1)
        ahead_x = jnp.concatenate([velocity[..., 1:], east_rim[..., None]], axis=3)
        ahead_y = jnp.concatenate([velocity[:, :, 1:], north_rim[:, :, None]], axis=2)
        new_x = cohesive[0] * (along_x + time_step * rigidity * (ahead_x - velocity))
        new_y = cohesive[1] * (along_y + time_step * rigidity * (ahead_y - velocity))
        inner_z = along_z[:, :-1] + time_step * rigidity[:-1] * (velocity[:, 1:] - velocity[:, :-1])
        new_z = cohesive[2] * jnp.concatenate([inner_z, traction[1][:, None]], axis=1)
        squares = jnp.sum(new_x * new_x + new_y * new_y + new_z * new_z, axis=0)
        factor = cohesion / jnp.maximum(jnp.sqrt(squares), cohesion)
        stress = jnp.stack([new_x, new_y, new_z], axis=1) * factor
    return (velocity, stress)


def solution(mesh):
    in_specs = (
        P(None, None, "gy", "gx"),
        P(None, None, None, "gy", "gx"),
        P(None, None, "gy", "gx"),
        P(None, "gy", "gx"),
        P(),
        P(None, None, ("gx", "gy"), None),
        P(None, None, ("gx", "gy"), None),
        P(None, None, None, None, ("gx", "gy"), None),
    )
    out_specs = (P(None, None, "gy", "gx"), P(None, None, None, "gy", "gx"))
    return jax.shard_map(body, mesh=mesh, in_specs=in_specs, out_specs=out_specs, check_vma=False)
```

profile of v0, /device:TPU:2, one launch (start us, length us, event | category | flops | bytes accessed | tf_op | source)
XLA Modules:
  0.0 528.3 jit_solution(9956004368002495465)
XLA Ops:
  2.3 6.9 %all-to-all-start = ((f32[6,8,8,128]{3,2,0,1:T(8,128)}), f32[6,8,8,128]{3,2,0,1:T(8,128)S(1)}, u32[]{:S(2)}, u32[]{:S(2)}) async-start(f32[6,8,8,128]{3,2,0,1:T(8,128)} %copy.261), calls=%async_computation | async-start | bytes 393216 | tf_op jit(solution)/shard_map/all_to_all | solution.py:113
  25.7 4.6 convolution_multiply_fusion.12
  30.3 4.6 fusion.4
  38.3 5.7 %fusion.2 = f32[6,8,32,32]{3,2,1,0:T(8,128)} fusion(f32[32,6,8,32]{3,0,2,1:T(8,128)} %convolution_multiply_fusion.12, f32[32,6,8,32]{3,0,2,1:T(8,128)S(1)} %fusion, f32[32,6,8,32]{3,0,2,1:T(8,128)S(1)} %convolution_subtract_fusion.15, f32[32,32]{1,0:T(8,128)S(1)} %copy.264, f32[32,32]{1,0:T(8,128)S(1)} %copy.263), kind=kOutput, calls=%fused_computation.51 | convolution fusion | flops 19134464 | bytes 794624 | tf_op jit(solution)/shard_map/...kb,bq->...qk/dot_general | solution.py:63
  47.2 6.5 %pad_maximum_fusion = f32[6,2,8,8,16,8]{5,4,3,2,0,1:T(8,128)} fusion(f32[6,1,8,8,16,8]{5,4,3,2,0,1:T(8,128)} %mul.1774, f32[6,1,8,8,16,8]{5,4,3,2,0,1:T(8,128)} %mul.1770), kind=kLoop, calls=%fused_computation.2 | loop fusion | flops 98304 | bytes 786432 | tf_op jit(solution)/shard_map/stack | solution.py:117
  53.7 6.2 %copy.265 = f32[6,2,8,8,16,8]{4,5,2,1,0,3:T(8,128)} copy(f32[6,2,8,8,16,8]{5,4,3,2,0,1:T(8,128)} %pad_maximum_fusion) | data formatting | bytes 786432 | tf_op jit(solution)/shard_map/stack | solution.py:117
  63.5 6.4 %all-to-all-start.1 = ((f32[8,1,12288]{2,1,0:T(1,128)}), f32[8,1,12288]{2,1,0:T(1,128)}, u32[]{:S(2)}, u32[]{:S(2)}) async-start(f32[8,1,12288]{2,1,0:T(1,128)} %reshape.406), calls=%async_computation.1 | async-start | bytes 786432 | tf_op jit(solution)/shard_map/all_to_all | solution.py:122
  69.8 7.2 %multiply_reduce_fusion.1 = f32[2,3,2,8,1024]{4,3,2,1,0:T(8,128)} fusion(f32[2,3,31,2,8,1024]{5,4,3,2,1,0:T(8,128)} %param.15, f32[2,30,8,1024]{3,2,1,0:T(8,128)S(1)} %slice-done), kind=kLoop, calls=%fused_computation.1 | loop fusion | flops 5799936 | bytes 14155776 | tf_op jit(solution)/shard_map/reduce_sum | solution.py:137
  93.7 6.7 %all-to-all-start.2 = ((f32[16,1,6144]{2,1,0:T(1,128)}), f32[16,1,6144]{2,1,0:T(1,128)S(1)}, u32[]{:S(2)}, u32[]{:S(2)}) async-start(f32[16,1,6144]{2,1,0:T(1,128)} %reshape.408), calls=%async_computation.2 | async-start | bytes 786432 | tf_op jit(solution)/shard_map/all_to_all | solution.py:121
  100.5 7.9 %multiply_reduce_fusion = f32[2,3,2,8,1024]{4,3,2,1,0:T(8,128)} fusion(f32[2,3,31,2,8,1024]{5,4,3,2,1,0:T(8,128)} %param.15, f32[2,31,8,1024]{3,2,1,0:T(8,128)} %param.14), kind=kLoop, calls=%fused_computation | loop fusion | flops 5996544 | bytes 14614528 | tf_op jit(solution)/shard_map/reduce_sum | solution.py:137
  124.6 4.6 convolution_multiply_fusion.7
  129.2 4.7 fusion.6
  137.7 5.7 %fusion.8 = f32[6,8,32,32]{3,2,1,0:T(8,128)} fusion(f32[32,6,8,32]{3,0,2,1:T(8,128)} %convolution_multiply_fusion.7, f32[32,6,8,32]{3,0,2,1:T(8,128)S(1)} %convolution_subtract_fusion.13, f32[32,6,8,32]{3,0,2,1:T(8,128)S(1)} %convolution_add_fusion.10, f32[32,32]{1,0:T(8,128)S(1)} %copy-done.12, f32[32,32]{1,0:T(8,128)S(1)} %copy.263), kind=kOutput, calls=%fused_computation.57 | convolution fusion | flops 19134464 | bytes 794624 | tf_op jit(solution)/shard_map/...kb,bq->...qk/dot_general | solution.py:63
  157.7 4.6 fusion.54
  162.2 4.8 fusion.12
  170.0 5.7 %fusion.10 = f32[6,8,32,32]{3,2,1,0:T(8,128)} fusion(f32[32,6,8,32]{3,0,2,1:T(8,128)} %fusion.54, f32[32,6,8,32]{3,0,2,1:T(8,128)S(1)} %convolution_subtract_fusion.11, f32[32,6,8,32]{3,0,2,1:T(8,128)S(1)} %convolution_add_fusion.8, f32[32,32]{1,0:T(8,128)S(1)} %copy.270, f32[32,32]{1,0:T(8,128)S(1)} %copy.263), kind=kOutput, calls=%fused_computation.59 | convolution fusion | flops 19134464 | bytes 794624 | tf_op jit(solution)/shard_map/...kb,bq->...qk/dot_general | solution.py:63
  182.2 6.3 %copy.307 = f32[8,16,6,2,8,1,1,8]{7,4,3,2,1,0,6,5:T(8,128)} copy(f32[8,16,6,2,8,1,1,8]{7,0,1,4,2,3,6,5:T(8,128)S(1)} %maximum_bitcast_fusion) | data formatting | bytes 786432 | tf_op jit(solution)/shard_map/reshape | solution.py:32
  188.5 6.2 %reshape.410 = f32[128,1,768]{2,1,0:T(1,128)} reshape(f32[128,1,1,6,2,8,8]{6,5,4,3,2,1,0:T(8,128)} %bitcast.560) | data formatting | bytes 786432
  194.7 7.7 %all-to-all-start.3 = ((f32[128,1,768]{2,1,0:T(1,128)}), f32[128,1,768]{2,1,0:T(1,128)S(1)}, u32[]{:S(2)}, u32[]{:S(2)}) async-start(f32[128,1,768]{2,1,0:T(1,128)} %reshape.410), calls=%async_computation.3 | async-start | bytes 786432 | tf_op jit(solution)/shard_map/all_to_all | solution.py:33
  203.8 5.9 %broadcast_multiply_fusion = (f32[4,64,128]{2,1,0:T(8,128)}, f32[4,64,128]{2,1,0:T(8,128)}, pred[4,64,128]{2,1,0:T(8,128)(4,1)S(1)}, pred[4,64,128]{2,1,0:T(8,12...) fusion(f32[]{:T(128)} %bitcast.76, f32[]{:T(128)} %bitcast.75, ...), kind=kLoop, calls=%fused_computation.234 | loop fusion | flops 557056 | bytes 655392 | tf_op jit(solution)/shard_map/mul | solution.py:166
  215.6 5.1 reshape.411
  220.7 7.7 %copy.274 = f32[6,2,8,16,8,8]{4,3,2,5,1,0:T(8,128)} copy(f32[6,2,8,16,8,8]{5,4,1,0,3,2:T(8,128)} %bitcast.561) | data formatting | bytes 786432 | tf_op jit(solution)/shard_map/transpose | solution.py:149
  228.4 5.6 %reshape.395 = f32[6,2,1024,8]{2,3,1,0:T(8,128)S(1)} reshape(f32[6,2,8,16,8,8]{4,3,2,5,1,0:T(8,128)} %copy.274) | data formatting | bytes 786432 | tf_op jit(solution)/shard_map/reshape | solution.py:149
  244.9 4.6 fusion.14
  255.7 6.3 %select_multiply_fusion = f32[4,64,128]{2,1,0:T(8,128)} fusion(pred[4,64,128]{2,1,0:T(8,128)(4,1)} %get-tuple-element.23, pred[4,64,128]{2,1,0:T(8,128)(4,1)} %get-tuple-element.22, pred[4,64,128]{2,1,0:T(8,128)(4,1)S(1)} %copy-done.58, pred[4,64,128]{2,1,0:T(8,128)(4,1)S(1)} %get-tuple-element.20, pred[4,64,128]{2,1,0:T(8,128)(4,1)S(1)} %get-tuple-element.19, ...), kind=kLoop, calls=%fused_computation.221 | loop fusion | flops 294912 | bytes 393248 | tf_op jit(solution)/shard_map/mul | solution.py:159
  269.9 7.3 %all-to-all-start.5 = ((f32[6,8,8,128]{3,2,0,1:T(8,128)}), f32[6,8,8,128]{3,2,0,1:T(8,128)S(1)}, u32[]{:S(2)}, u32[]{:S(2)}) async-start(f32[6,8,8,128]{3,2,0,1:T(8,128)} %copy.286), calls=%async_computation.5 | async-start | bytes 393216 | tf_op jit(solution)/shard_map/all_to_all | solution.py:113
  278.8 6.9 %all-to-all-done.5 = f32[6,8,8,128]{3,2,0,1:T(8,128)S(1)} async-done(((f32[6,8,8,128]{3,2,0,1:T(8,128)}), f32[6,8,8,128]{3,2,0,1:T(8,128)S(1)}, u32[]{:S(2)}, u32[]{:S(2)}) %all-to-all-start.5) | async-done | bytes 196640 | tf_op jit(solution)/shard_map/all_to_all | solution.py:113
  289.7 4.4 convolution_multiply_fusion.4
  297.8 4.6 fusion.19
  305.5 4.6 fusion.17
  313.3 6.5 %pad_maximum_fusion.1 = f32[6,2,8,8,16,8]{5,4,3,2,0,1:T(8,128)} fusion(f32[6,1,8,8,16,8]{5,4,3,2,0,1:T(8,128)} %mul.1846, f32[6,1,8,8,16,8]{5,4,3,2,0,1:T(8,128)} %mul.1842), kind=kLoop, calls=%fused_computation.4 | loop fusion | flops 98304 | bytes 786432 | tf_op jit(solution)/shard_map/stack | solution.py:117
  319.8 6.2 %copy.288 = f32[6,2,8,8,16,8]{4,5,2,1,0,3:T(8,128)} copy(f32[6,2,8,8,16,8]{5,4,3,2,0,1:T(8,128)} %pad_maximum_fusion.1) | data formatting | bytes 786432 | tf_op jit(solution)/shard_map/stack | solution.py:117
  334.4 5.6 %collective-permute-start.2 = (f32[3,4,64]{2,1,0:T(4,128)S(1)}, f32[3,4,64]{2,1,0:T(4,128)S(1)}, u32[]{:S(2)}, u32[]{:S(2)}) collective-permute-start(f32[3,4,64]{2,1,0:T(4,128)S(1)} %bitcast.605), channel_id=1, source_target_pairs={{0,112},{16,0},{32,16},{48,32},{64,48},{80,64},{96,80},{112,96},{1... | collective-permute-start | bytes 9224 | tf_op jit(solution)/shard_map/ppermute | solution.py:41
  354.6 5.5 %all-to-all-start.7 = ((f32[16,1,6144]{2,1,0:T(1,128)}), f32[16,1,6144]{2,1,0:T(1,128)}, u32[]{:S(2)}, u32[]{:S(2)}) async-start(f32[16,1,6144]{2,1,0:T(1,128)} %reshape.414), calls=%async_computation.7 | async-start | bytes 786432 | tf_op jit(solution)/shard_map/all_to_all | solution.py:121
  363.3 4.9 all-to-all-done.7
  385.3 4.6 fusion.23
  392.2 4.7 fusion.21
  417.1 4.6 fusion.25
  427.6 6.3 %copy.309 = f32[8,16,6,2,8,1,1,8]{7,4,3,2,1,0,6,5:T(8,128)} copy(f32[8,16,6,2,8,1,1,8]{7,0,1,4,2,3,6,5:T(8,128)S(1)} %maximum_bitcast_fusion.1) | data formatting | bytes 786432 | tf_op jit(solution)/shard_map/reshape | solution.py:32
  433.9 6.3 %reshape.416 = f32[128,1,768]{2,1,0:T(1,128)} reshape(f32[128,1,1,6,2,8,8]{6,5,4,3,2,1,0:T(8,128)} %bitcast.562) | data formatting | bytes 786432
  440.2 5.3 all-to-all-start.8
  445.6 5.1 maximum_divide_fusion.1
  450.9 6.4 %all-to-all-done.8 = f32[128,1,768]{2,1,0:T(1,128)S(1)} async-done(((f32[128,1,768]{2,1,0:T(1,128)}), f32[128,1,768]{2,1,0:T(1,128)S(1)}, u32[]{:S(2)}, u32[]{:S(2)}) %all-to-all-start.8) | async-done | bytes 393248 | tf_op jit(solution)/shard_map/all_to_all | solution.py:33
  458.8 5.1 reshape.417
  464.0 7.7 %copy.296 = f32[6,2,8,16,8,8]{4,3,2,5,1,0:T(8,128)} copy(f32[6,2,8,16,8,8]{5,4,1,0,3,2:T(8,128)} %bitcast.563) | data formatting | bytes 786432 | tf_op jit(solution)/shard_map/transpose | solution.py:149
  471.7 5.6 %reshape.403 = f32[6,2,1024,8]{2,3,1,0:T(8,128)S(1)} reshape(f32[6,2,8,16,8,8]{4,3,2,5,1,0:T(8,128)} %copy.296) | data formatting | bytes 786432 | tf_op jit(solution)/shard_map/reshape | solution.py:149
  500.8 5.4 %collective-permute-done.4 = f32[3,4,64]{2,1,0:T(4,128)S(1)} collective-permute-done((f32[3,4,64]{2,1,0:T(4,128)S(1)}, f32[3,4,64]{2,1,0:T(4,128)S(1)}, u32[]{:S(2)}, u32[]{:S(2)}) %collective-permute-start.4) | collective-permute-done | bytes 3104 | tf_op jit(solution)/shard_map/ppermute | solution.py:41
  521.5 5.1 maximum_divide_fusion
  (350 shorter events, 248.8 us)
Async XLA Ops:
  2.3 15.7 %all-to-all-start = ((f32[6,8,8,128]{3,2,0,1:T(8,128)}), f32[6,8,8,128]{3,2,0,1:T(8,128)S(1)}, u32[]{:S(2)}, u32[]{:S(2)}) async-start(f32[6,8,8,128]{3,2,0,1:T(8,128)} %copy.261), calls=%async_computation | async-start | bytes 393216 | tf_op jit(solution)/shard_map/all_to_all | solution.py:113
  13.8 249.1 %collective-permute-start = (f32[3,4,64]{2,1,0:T(4,128)}, f32[3,4,64]{2,1,0:T(4,128)}, u32[]{:S(2)}, u32[]{:S(2)}) collective-permute-start(f32[3,4,64]{2,1,0:T(4,128)} %bitcast.9), channel_id=1, source_target_pairs={{0,16},{16,32},{32,48},{48,64},{64,80},{80,96},{96,112},{112,0},{1... | collective-permute-start | bytes 9224 | tf_op jit(solution)/shard_map/ppermute | solution.py:41
  16.6 247.9 %collective-permute-start.1 = (f32[3,4,128]{2,1,0:T(4,128)}, f32[3,4,128]{2,1,0:T(4,128)}, u32[]{:S(2)}, u32[]{:S(2)}) collective-permute-start(f32[3,4,128]{2,1,0:T(4,128)} %bitcast.552), channel_id=1, source_target_pairs={{0,1},{1,2},{2,3},{3,4},{4,5},{5,6},{6,7},{7,8},{8,9},{9,10},{10,1... | collective-permute-start | bytes 18440 | tf_op jit(solution)/shard_map/ppermute | solution.py:41
  17.4 20.9 %copy-start.11 = (f32[32,32]{1,0:T(8,128)}, f32[32,32]{1,0:T(8,128)S(1)}, u32[]{:S(2)}) copy-start(f32[32,32]{1,0:T(8,128)S(1)} %copy.264) | copy-start | bytes 12292
  63.5 16.7 %all-to-all-start.1 = ((f32[8,1,12288]{2,1,0:T(1,128)}), f32[8,1,12288]{2,1,0:T(1,128)}, u32[]{:S(2)}, u32[]{:S(2)}) async-start(f32[8,1,12288]{2,1,0:T(1,128)} %reshape.406), calls=%async_computation.1 | async-start | bytes 786432 | tf_op jit(solution)/shard_map/all_to_all | solution.py:122
  93.7 15.7 %all-to-all-start.2 = ((f32[16,1,6144]{2,1,0:T(1,128)}), f32[16,1,6144]{2,1,0:T(1,128)S(1)}, u32[]{:S(2)}, u32[]{:S(2)}) async-start(f32[16,1,6144]{2,1,0:T(1,128)} %reshape.408), calls=%async_computation.2 | async-start | bytes 786432 | tf_op jit(solution)/shard_map/all_to_all | solution.py:121
  108.5 37.2 %copy-start.25 = (f32[2,3,8,1024]{3,2,1,0:T(8,128)}, f32[2,3,8,1024]{3,2,1,0:T(8,128)S(1)}, u32[]{:S(2)}) copy-start(f32[2,3,8,1024]{3,2,1,0:T(8,128)S(1)} %neg.5) | copy-start | bytes 589828
  108.6 136.2 %copy-start.19 = (f32[32,32]{1,0:T(8,128)}, f32[32,32]{1,0:T(8,128)S(1)}, u32[]{:S(2)}) copy-start(f32[32,32]{1,0:T(8,128)S(1)} %copy.270) | copy-start | bytes 12292
  188.5 13.9 %copy-start.70 = (f32[3,8]{1,0:T(4,128)S(1)}, f32[3,8]{1,0:T(4,128)}, u32[]{:S(2)}) copy-start(f32[3,8]{1,0:T(4,128)} %param.12) | copy-start | bytes 292
  188.5 15.3 %copy-start.69 = (s32[4,64,128]{2,1,0:T(8,128)S(1)}, s32[4,64,128]{2,1,0:T(8,128)}, u32[]{:S(2)}) copy-start(s32[4,64,128]{2,1,0:T(8,128)} %param.11) | copy-start | bytes 393220
  194.7 19.3 %all-to-all-start.3 = ((f32[128,1,768]{2,1,0:T(1,128)}), f32[128,1,768]{2,1,0:T(1,128)S(1)}, u32[]{:S(2)}, u32[]{:S(2)}) async-start(f32[128,1,768]{2,1,0:T(1,128)} %reshape.410), calls=%async_computation.3 | async-start | bytes 786432 | tf_op jit(solution)/shard_map/all_to_all | solution.py:33
  209.7 45.9 %copy-start.43 = (pred[4,64,128]{2,1,0:T(8,128)(4,1)}, pred[4,64,128]{2,1,0:T(8,128)(4,1)S(1)}, u32[]{:S(2)}) copy-start(pred[4,64,128]{2,1,0:T(8,128)(4,1)S(1)} %get-tuple-element.16) | copy-start | bytes 98308
  209.7 45.9 %copy-start.46 = (pred[4,64,128]{2,1,0:T(8,128)(4,1)}, pred[4,64,128]{2,1,0:T(8,128)(4,1)S(1)}, u32[]{:S(2)}) copy-start(pred[4,64,128]{2,1,0:T(8,128)(4,1)S(1)} %get-tuple-element.17) | copy-start | bytes 98308
  209.7 45.9 %copy-start.49 = (pred[4,64,128]{2,1,0:T(8,128)(4,1)}, pred[4,64,128]{2,1,0:T(8,128)(4,1)S(1)}, u32[]{:S(2)}) copy-start(pred[4,64,128]{2,1,0:T(8,128)(4,1)S(1)} %get-tuple-element.18) | copy-start | bytes 98308
  209.7 45.9 %copy-start.52 = (pred[4,64,128]{2,1,0:T(8,128)(4,1)}, pred[4,64,128]{2,1,0:T(8,128)(4,1)S(1)}, u32[]{:S(2)}) copy-start(pred[4,64,128]{2,1,0:T(8,128)(4,1)S(1)} %get-tuple-element.19) | copy-start | bytes 98308
  209.7 45.9 %copy-start.55 = (pred[4,64,128]{2,1,0:T(8,128)(4,1)}, pred[4,64,128]{2,1,0:T(8,128)(4,1)S(1)}, u32[]{:S(2)}) copy-start(pred[4,64,128]{2,1,0:T(8,128)(4,1)S(1)} %get-tuple-element.20) | copy-start | bytes 98308
  241.1 14.5 %copy-start.58 = (pred[4,64,128]{2,1,0:T(8,128)(4,1)S(1)}, pred[4,64,128]{2,1,0:T(8,128)(4,1)}, u32[]{:S(2)}) copy-start(pred[4,64,128]{2,1,0:T(8,128)(4,1)} %get-tuple-element.21) | copy-start | bytes 98308
  244.9 17.2 %copy-start.31 = (f32[3,1,4,64,128]{4,3,2,1,0:T(8,128)S(1)}, f32[3,1,4,64,128]{4,3,2,1,0:T(8,128)}, u32[]{:S(2)}) copy-start(f32[3,1,4,64,128]{4,3,2,1,0:T(8,128)} %get-tuple-element.27) | copy-start | bytes 1179652
  249.4 18.0 %copy-start.6 = (f32[3,1,4,64,128]{4,3,2,1,0:T(8,128)S(1)}, f32[3,1,4,64,128]{4,3,2,1,0:T(8,128)}, u32[]{:S(2)}) copy-start(f32[3,1,4,64,128]{4,3,2,1,0:T(8,128)} %copy-done.5) | copy-start | bytes 1179652
  249.5 18.0 %copy-start.9 = (f32[3,1,4,64,128]{4,3,2,1,0:T(8,128)S(1)}, f32[3,1,4,64,128]{4,3,2,1,0:T(8,128)}, u32[]{:S(2)}) copy-start(f32[3,1,4,64,128]{4,3,2,1,0:T(8,128)} %copy-done.8) | copy-start | bytes 1179652
  249.5 18.0 %copy-start.16 = (f32[3,1,4,64,128]{4,3,0,2,1:T(8,128)S(1)}, f32[3,1,4,64,128]{4,3,0,2,1:T(8,128)}, u32[]{:S(2)}) copy-start(f32[3,1,4,64,128]{4,3,0,2,1:T(8,128)} %copy-done.15) | copy-start | bytes 1179652
  251.6 14.2 %all-to-all-start.4 = ((f32[6,8,8,128]{3,1,0,2:T(8,128)}), f32[6,8,8,128]{3,1,0,2:T(8,128)}, u32[]{:S(2)}, u32[]{:S(2)}) async-start(f32[6,8,8,128]{3,1,0,2:T(8,128)} %copy.275), calls=%async_computation.4 | async-start | bytes 393216 | tf_op jit(solution)/shard_map/all_to_all | solution.py:153
  269.9 15.7 %all-to-all-start.5 = ((f32[6,8,8,128]{3,2,0,1:T(8,128)}), f32[6,8,8,128]{3,2,0,1:T(8,128)S(1)}, u32[]{:S(2)}, u32[]{:S(2)}) async-start(f32[6,8,8,128]{3,2,0,1:T(8,128)} %copy.286), calls=%async_computation.5 | async-start | bytes 393216 | tf_op jit(solution)/shard_map/all_to_all | solution.py:113
  326.0 14.0 %copy-start.23 = (f32[3,1,4,64,128]{4,3,0,2,1:T(8,128)S(1)}, f32[3,1,4,64,128]{4,3,0,2,1:T(8,128)}, u32[]{:S(2)}) copy-start(f32[3,1,4,64,128]{4,3,0,2,1:T(8,128)} %copy-done.22) | copy-start | bytes 1179652
  326.0 14.0 %copy-start.38 = (f32[3,64,128]{2,1,0:T(8,128)S(1)}, f32[3,64,128]{2,1,0:T(8,128)}, u32[]{:S(2)}) copy-start(f32[3,64,128]{2,1,0:T(8,128)} %slice_multiply_fusion) | copy-start | bytes 294916
  329.9 12.6 %all-to-all-start.6 = ((f32[8,1,12288]{2,1,0:T(1,128)}), f32[8,1,12288]{2,1,0:T(1,128)S(1)}, u32[]{:S(2)}, u32[]{:S(2)}) async-start(f32[8,1,12288]{2,1,0:T(1,128)} %reshape.412), calls=%async_computation.6 | async-start | bytes 786432 | tf_op jit(solution)/shard_map/all_to_all | solution.py:122
  334.4 26.7 %collective-permute-start.2 = (f32[3,4,64]{2,1,0:T(4,128)S(1)}, f32[3,4,64]{2,1,0:T(4,128)S(1)}, u32[]{:S(2)}, u32[]{:S(2)}) collective-permute-start(f32[3,4,64]{2,1,0:T(4,128)S(1)} %bitcast.605), channel_id=1, source_target_pairs={{0,112},{16,0},{32,16},{48,32},{64,48},{80,64},{96,80},{112,96},{1... | collective-permute-start | bytes 9224 | tf_op jit(solution)/shard_map/ppermute | solution.py:41
  340.0 21.3 %collective-permute-start.3 = (f32[3,4,128]{2,1,0:T(4,128)S(1)}, f32[3,4,128]{2,1,0:T(4,128)S(1)}, u32[]{:S(2)}, u32[]{:S(2)}) collective-permute-start(f32[3,4,128]{2,1,0:T(4,128)S(1)} %bitcast.598), channel_id=1, source_target_pairs={{0,15},{1,0},{2,1},{3,2},{4,3},{5,4},{6,5},{7,6},{8,7},{9,8},{10,9... | collective-permute-start | bytes 18440 | tf_op jit(solution)/shard_map/ppermute | solution.py:41
  354.6 13.6 %all-to-all-start.7 = ((f32[16,1,6144]{2,1,0:T(1,128)}), f32[16,1,6144]{2,1,0:T(1,128)}, u32[]{:S(2)}, u32[]{:S(2)}) async-start(f32[16,1,6144]{2,1,0:T(1,128)} %reshape.414), calls=%async_computation.7 | async-start | bytes 786432 | tf_op jit(solution)/shard_map/all_to_all | solution.py:121
  433.8 11.7 %copy-start.44 = (pred[4,64,128]{2,1,0:T(8,128)(4,1)S(1)}, pred[4,64,128]{2,1,0:T(8,128)(4,1)}, u32[]{:S(2)}) copy-start(pred[4,64,128]{2,1,0:T(8,128)(4,1)} %copy-done.43) | copy-start | bytes 98308
  433.8 11.7 %copy-start.47 = (pred[4,64,128]{2,1,0:T(8,128)(4,1)S(1)}, pred[4,64,128]{2,1,0:T(8,128)(4,1)}, u32[]{:S(2)}) copy-start(pred[4,64,128]{2,1,0:T(8,128)(4,1)} %copy-done.46) | copy-start | bytes 98308
  433.8 11.7 %copy-start.50 = (pred[4,64,128]{2,1,0:T(8,128)(4,1)S(1)}, pred[4,64,128]{2,1,0:T(8,128)(4,1)}, u32[]{:S(2)}) copy-start(pred[4,64,128]{2,1,0:T(8,128)(4,1)} %copy-done.49) | copy-start | bytes 98308
  433.8 11.7 %copy-start.53 = (pred[4,64,128]{2,1,0:T(8,128)(4,1)S(1)}, pred[4,64,128]{2,1,0:T(8,128)(4,1)}, u32[]{:S(2)}) copy-start(pred[4,64,128]{2,1,0:T(8,128)(4,1)} %copy-done.52) | copy-start | bytes 98308
  433.8 11.7 %copy-start.56 = (pred[4,64,128]{2,1,0:T(8,128)(4,1)S(1)}, pred[4,64,128]{2,1,0:T(8,128)(4,1)}, u32[]{:S(2)}) copy-start(pred[4,64,128]{2,1,0:T(8,128)(4,1)} %copy-done.55) | copy-start | bytes 98308
  433.8 11.7 %copy-start.59 = (pred[4,64,128]{2,1,0:T(8,128)(4,1)S(1)}, pred[4,64,128]{2,1,0:T(8,128)(4,1)}, u32[]{:S(2)}) copy-start(pred[4,64,128]{2,1,0:T(8,128)(4,1)} %get-tuple-element.21) | copy-start | bytes 98308
  433.8 11.7 %copy-start.61 = (pred[4,64,128]{2,1,0:T(8,128)(4,1)S(1)}, pred[4,64,128]{2,1,0:T(8,128)(4,1)}, u32[]{:S(2)}) copy-start(pred[4,64,128]{2,1,0:T(8,128)(4,1)} %get-tuple-element.22) | copy-start | bytes 98308
  433.9 11.7 %copy-start.63 = (pred[4,64,128]{2,1,0:T(8,128)(4,1)S(1)}, pred[4,64,128]{2,1,0:T(8,128)(4,1)}, u32[]{:S(2)}) copy-start(pred[4,64,128]{2,1,0:T(8,128)(4,1)} %get-tuple-element.23) | copy-start | bytes 98308
  433.9 11.7 %copy-start.65 = (f32[4,64,128]{2,1,0:T(8,128)S(1)}, f32[4,64,128]{2,1,0:T(8,128)}, u32[]{:S(2)}) copy-start(f32[4,64,128]{2,1,0:T(8,128)} %get-tuple-element.11) | copy-start | bytes 393220
  433.9 16.8 %copy-start.28 = (f32[3,1,4,64,128]{4,3,0,2,1:T(8,128)S(1)}, f32[3,1,4,64,128]{4,3,0,2,1:T(8,128)}, u32[]{:S(2)}) copy-start(f32[3,1,4,64,128]{4,3,0,2,1:T(8,128)} %maximum_multiply_fusion.2) | copy-start | bytes 1179652
  433.9 16.8 %copy-start.29 = (f32[3,4,64,128]{3,2,0,1:T(8,128)S(1)}, f32[3,4,64,128]{3,2,0,1:T(8,128)}, u32[]{:S(2)}) copy-start(f32[3,4,64,128]{3,2,0,1:T(8,128)} %get-tuple-element.12) | copy-start | bytes 1179652
  433.9 16.8 %copy-start.30 = (f32[3,4,64,128]{3,2,0,1:T(8,128)S(1)}, f32[3,4,64,128]{3,2,0,1:T(8,128)}, u32[]{:S(2)}) copy-start(f32[3,4,64,128]{3,2,0,1:T(8,128)} %get-tuple-element.13) | copy-start | bytes 1179652
  440.2 17.0 %all-to-all-start.8 = ((f32[128,1,768]{2,1,0:T(1,128)}), f32[128,1,768]{2,1,0:T(1,128)S(1)}, u32[]{:S(2)}, u32[]{:S(2)}) async-start(f32[128,1,768]{2,1,0:T(1,128)} %reshape.416), calls=%async_computation.8 | async-start | bytes 786432 | tf_op jit(solution)/shard_map/all_to_all | solution.py:33
  492.5 16.3 %copy-start.34 = (f32[4,64,128]{2,1,0:T(8,128)S(1)}, f32[4,64,128]{2,1,0:T(8,128)}, u32[]{:S(2)}) copy-start(f32[4,64,128]{2,1,0:T(8,128)} %select_multiply_fusion) | copy-start | bytes 393220
  493.2 14.0 %all-to-all-start.9 = ((f32[6,8,8,128]{3,1,0,2:T(8,128)}), f32[6,8,8,128]{3,1,0,2:T(8,128)}, u32[]{:S(2)}, u32[]{:S(2)}) async-start(f32[6,8,8,128]{3,1,0,2:T(8,128)} %copy.297), calls=%async_computation.9 | async-start | bytes 393216 | tf_op jit(solution)/shard_map/all_to_all | solution.py:153
  497.7 9.5 %collective-permute-start.5 = (f32[3,4,128]{2,1,0:T(4,128)S(1)}, f32[3,4,128]{2,1,0:T(4,128)S(1)}, u32[]{:S(2)}, u32[]{:S(2)}) collective-permute-start(f32[3,4,128]{2,1,0:T(4,128)S(1)} %bitcast.600), channel_id=1, source_target_pairs={{0,1},{1,2},{2,3},{3,4},{4,5},{5,6},{6,7},{7,8},{8,9},{9,10},{10,1... | collective-permute-start | bytes 18440 | tf_op jit(solution)/shard_map/ppermute | solution.py:41
  498.2 8.0 %collective-permute-start.4 = (f32[3,4,64]{2,1,0:T(4,128)S(1)}, f32[3,4,64]{2,1,0:T(4,128)S(1)}, u32[]{:S(2)}, u32[]{:S(2)}) collective-permute-start(f32[3,4,64]{2,1,0:T(4,128)S(1)} %bitcast.606), channel_id=1, source_target_pairs={{0,16},{16,32},{32,48},{48,64},{64,80},{80,96},{96,112},{112,0},{1... | collective-permute-start | bytes 9224 | tf_op jit(solution)/shard_map/ppermute | solution.py:41
  512.1 6.1 %collective-permute-start.6 = (f32[3,4,64]{2,1,0:T(4,128)}, f32[3,4,64]{2,1,0:T(4,128)}, u32[]{:S(2)}, u32[]{:S(2)}) collective-permute-start(f32[3,4,64]{2,1,0:T(4,128)} %bitcast.150), channel_id=1, source_target_pairs={{0,112},{16,0},{32,16},{48,32},{64,48},{80,64},{96,80},{112,96},{1... | collective-permute-start | bytes 9224 | tf_op jit(solution)/shard_map/ppermute | solution.py:41
  513.4 6.5 %collective-permute-start.7 = (f32[3,4,128]{2,1,0:T(4,128)S(1)}, f32[3,4,128]{2,1,0:T(4,128)S(1)}, u32[]{:S(2)}, u32[]{:S(2)}) collective-permute-start(f32[3,4,128]{2,1,0:T(4,128)S(1)} %bitcast.602), channel_id=1, source_target_pairs={{0,15},{1,0},{2,1},{3,2},{4,3},{5,4},{6,5},{7,6},{8,7},{9,8},{10,9... | collective-permute-start | bytes 18440 | tf_op jit(solution)/shard_map/ppermute | solution.py:41
  (42 other events, 214.5 us)
where the time goes:
time: 538 us; the launch traced here: 528 us
  local copies, waits for them, and re-layouts  176 us (33%)
  matrix products  161 us (30%)
  other arithmetic  83.1 us (15%)
  starting transfers between devices  71.3 us (13%)
  waiting for transfers between devices  33.5 us (6%)
    dot_general x28, matrix products, second_section(): return jnp.einsum('...kb,bq->...qk', values, table, precision=highest)  121 us
    unnamed x160, local copies, waits for them, and re-layouts  46.7 us
    dot_general x30, matrix products, first_section(): return jnp.einsum('...ab,ak->...kb', values, table, precision=highest)  40.1 us
    mul x10, local copies, waits for them, and re-layouts, transform_last(): out_real.reshape(lead + (length,)) * scale  18.6 us
    mul x6, local copies, waits for them, and re-layouts, transform_last(): out_imag.reshape(lead + (length,)) * scale  15.7 us
    transpose x2, local copies, waits for them, and re-layouts, body(): incoming.transpose(0, 1, 3, 2, 4, 5)  15.4 us
    reduce_sum x2, other arithmetic, body(): jnp.sum(memory[:, None, step_index:, None] * history[:, :, :tail_count],...  15.1 us
    all_to_all x2, starting transfers between devices, body(): lax.all_to_all(forward_pieces, 'gx', split_axis=1, concat_axis=3, tiled=T...  14.2 us
  transfers between devices with their start and end apart: 18, of which 7 were waited for; matrix products, arithmetic and copies ran while one was open for 47% of the time, Pallas kernels for 0%

commit v1 on v0

v1 whole, which is shorter than its diff:
```python
import functools
import math

import jax
import jax.numpy as jnp
import numpy as np
from jax import lax
from jax.experimental import pallas as pl
from jax.experimental.pallas import tpu as pltpu
from jax.sharding import PartitionSpec as P

time_step = 0.2
GX = 8
GY = 16
PEERS = 128
f32 = jnp.float32
bf16 = jnp.bfloat16
both = ("gx", "gy")
half_root = math.sqrt(0.5)


def halves(table):
    high = jnp.asarray(table, f32).astype(bf16)
    low = (jnp.asarray(table, f32) - high.astype(f32)).astype(bf16)
    return jnp.stack([high, low])


def tables():
    index = np.arange(PEERS)
    angle = 2.0 * np.pi * (np.outer(index, index) % PEERS) / PEERS
    c, s = np.cos(angle) / 32.0, np.sin(angle) / 32.0
    along_x = np.block([[c, s], [-s, c]])
    place = 8 * (index % GY) + index // GY
    angle = 2.0 * np.pi * (np.outer(place, index) % PEERS) / PEERS
    c, s = np.cos(angle) / 32.0, np.sin(angle) / 32.0
    along_y = np.block([[c, -s], [s, c]])
    turn = 2.0 * np.pi * np.outer(np.arange(8), index) / 1024.0
    twist = np.stack([np.cos(turn), np.sin(turn)])
    twist = np.broadcast_to(twist[:, :, None, :], (2, 8, 8, PEERS))
    return halves(along_x), halves(along_y), jnp.asarray(twist, f32)


def plus(a, b):
    imag = a[1] if b[1] is None else b[1] if a[1] is None else a[1] + b[1]
    return (a[0] + b[0], imag)


def minus(a, b):
    imag = a[1] if b[1] is None else -b[1] if a[1] is None else a[1] - b[1]
    return (a[0] - b[0], imag)


def turned(a, sign):
    if a[1] is None:
        return (jnp.zeros_like(a[0]), a[0] if sign > 0 else -a[0])
    return (-a[1], a[0]) if sign > 0 else (a[1], -a[0])


def four(x, sign):
    a, b = plus(x[0], x[2]), minus(x[0], x[2])
    c, d = plus(x[1], x[3]), turned(minus(x[1], x[3]), sign)
    return [plus(a, c), plus(b, d), minus(a, c), minus(b, d)]


def eight(x, sign):
    even, odd = four(x[0::2], sign), four(x[1::2], sign)
    o1, o3 = odd[1], odd[3]
    odd1 = ((o1[0] - sign * o1[1]) * half_root, (o1[1] + sign * o1[0]) * half_root)
    odd3 = ((-o3[0] - sign * o3[1]) * half_root, (sign * o3[0] - o3[1]) * half_root)
    odd = [odd[0], odd1, turned(odd[2], sign), odd3]
    return [plus(e, o) for e, o in zip(even, odd)] + [minus(e, o) for e, o in zip(even, odd)]


def split(x):
    high = x.astype(bf16)
    return high, (x - high.astype(f32)).astype(bf16)


def product(a, b, dims):
    dot = functools.partial(lax.dot_general, dimension_numbers=(dims, ((), ())), preferred_element_type=f32)
    return dot(a[0], b[0]) + (dot(a[1], b[0]) + dot(a[0], b[1]))


def from_peers(x_ref, pair, matrix, re_ref, im_ref, tiles):
    x = jnp.concatenate([x_ref[pl.ds(2 * pair + part, PEERS, stride=tiles), :] for part in range(2)], axis=0)
    y = product(split(x), matrix, ((0,), (0,)))
    re_ref[...] = y[:, :PEERS]
    im_ref[...] = y[:, PEERS:]


def to_peers(o_ref, pair, matrix, re_ref, im_ref, tiles):
    t = split(jnp.concatenate([re_ref[...], im_ref[...]], axis=1))
    out = product(matrix, t, ((1,), (1,)))
    for part in range(2):
        o_ref[pl.ds(2 * pair + part, PEERS, stride=tiles), :] = out[part * PEERS : (part + 1) * PEERS]


def twisted(value, twist_ref, index, sign):
    if index == 0:
        return value
    c, s = twist_ref[0, index], twist_ref[1, index]
    if sign < 0:
        return (value[0] * c + value[1] * s, value[1] * c - value[0] * s)
    return (value[0] * c - value[1] * s, value[1] * c + value[0] * s)


def strike_forward(take, twist_ref, matrix, o_ref, re_ref, im_ref):
    for pair in range(3):
        for member in range(2):
            plane = 2 * pair + member
            waves = eight([(take(plane, tile), None) for tile in range(GX)], -1.0)
            for k in range(8):
                re, im = waves[k]
                if im is None:
                    im = jnp.zeros_like(re)
                re, im = twisted((re, im), twist_ref, k, -1)
                rows = pl.ds(member * 64 + k * 8, 8)
                re_ref[rows, :] = re
                im_ref[rows, :] = im
        to_peers(o_ref, pair, matrix, re_ref, im_ref, 6)


def strike_inverse(x_ref, twist_ref, matrix, re_ref, im_ref, put):
    for pair in range(3):
        from_peers(x_ref, pair, matrix, re_ref, im_ref, 6)
        for member in range(2):
            values = []
            for k in range(8):
                rows = pl.ds(member * 64 + k, 8, stride=8)
                values.append(twisted((re_ref[rows, :], im_ref[rows, :]), twist_ref, k, 1))
            field = eight(values, 1.0)
            for tile in range(GX):
                put(2 * pair + member, tile, field[tile][0])


def forward_kernel(x_ref, mx_ref, twist_ref, o_ref, re_ref, im_ref):
    matrix = (mx_ref[0], mx_ref[1])
    take = lambda plane, tile: x_ref[tile, pl.ds(plane * 8, 8), :]
    strike_forward(take, twist_ref, matrix, o_ref, re_ref, im_ref)


def dip_kernel(carry, x_ref, impedance_ref, tail_ref, *refs):
    if carry:
        first_ref, later_ref, my_ref, twist_ref, o_ref, next_ref, re_ref, im_ref = refs
    else:
        my_ref, twist_ref, o_ref, re_ref, im_ref = refs
    matrix = (my_ref[0], my_ref[1])
    for pair in range(3):
        from_peers(x_ref, pair, matrix, re_ref, im_ref, 6)
        for member in range(2):
            plane = 2 * pair + member
            values = []
            for j in range(8):
                rows = pl.ds(member * 64 + j, 8, stride=8)
                values.append(twisted((re_ref[rows, :], im_ref[rows, :]), twist_ref, j, -1))
            spectrum = eight(values, -1.0)
            response = []
            for tile in range(8):
                lanes = pl.ds(tile * PEERS, PEERS)
                z = impedance_ref[plane, :, lanes]
                re, im = spectrum[tile]
                response.append(
                    (tail_ref[2 * plane, :, lanes] - z * re, tail_ref[2 * plane + 1, :, lanes] - z * im)
                )
                if carry:
                    first = first_ref[plane // 3, :, lanes]
                    next_ref[2 * plane, :, lanes] = later_ref[2 * plane, :, lanes] + first * re
                    next_ref[2 * plane + 1, :, lanes] = later_ref[2 * plane + 1, :, lanes] + first * im
            lines = eight(response, 1.0)
            for j in range(8):
                re, im = twisted(lines[j], twist_ref, j, 1)
                rows = pl.ds(member * 64 + j * 8, 8)
                re_ref[rows, :] = re
                im_ref[rows, :] = im
        to_peers(o_ref, pair, matrix, re_ref, im_ref, 6)


def turn_kernel(x_ref, early_ref, mx_ref, twist_ref, traction_ref, o_ref, re_ref, im_ref, plane_ref):
    matrix = (mx_ref[0], mx_ref[1])

    def put(plane, tile, value):
        traction_ref[tile, pl.ds(plane * 8, 8), :] = value
        gain = early_ref[tile, pl.ds(48 + (plane // 3) * 8, 8), :]
        plane_ref[tile, pl.ds(plane * 8, 8), :] = early_ref[tile, pl.ds(plane * 8, 8), :] + gain * value

    strike_inverse(x_ref, twist_ref, matrix, re_ref, im_ref, put)
    take = lambda plane, tile: plane_ref[tile, pl.ds(plane * 8, 8), :]
    strike_forward(take, twist_ref, matrix, o_ref, re_ref, im_ref)


def inverse_kernel(x_ref, mx_ref, twist_ref, traction_ref, re_ref, im_ref):
    matrix = (mx_ref[0], mx_ref[1])

    def put(plane, tile, value):
        traction_ref[tile, pl.ds(plane * 8, 8), :] = value

    strike_inverse(x_ref, twist_ref, matrix, re_ref, im_ref, put)


def history_kernel(history_ref, memory_ref, now_ref, next_ref):
    lags = history_ref.shape[2]
    for tile in range(8):
        lanes = pl.ds(tile * PEERS, PEERS)
        for part in range(2):
            now = jnp.zeros((8, PEERS), f32)
            later = jnp.zeros((8, PEERS), f32)
            for lag in range(lags):
                value = history_ref[0, 0, lag, part, :, lanes]
                now = now + memory_ref[0, lag, :, lanes] * value
                if lag + 1 < lags:
                    later = later + memory_ref[0, lag + 1, :, lanes] * value
            now_ref[0, 0, part, :, lanes] = now
            next_ref[0, 0, part, :, lanes] = later


def planes_kernel(low_ref, high_ref, o_ref):
    for plane in range(6):
        source = low_ref if plane < 3 else high_ref
        for tile in range(GX):
            o_ref[tile, pl.ds(plane * 8, 8), :] = source[plane % 3, 0, pl.ds(tile * 8, 8), :]


def lane_index(shape):
    return lax.broadcasted_iota(jnp.int32, shape, len(shape) - 1)


def packed_column(values, column, lane):
    out = jnp.zeros(values[0].shape, f32)
    for k, value in enumerate(values):
        shift = (k - column) % PEERS
        moved = pltpu.roll(value, shift, 1) if shift else value
        out = jnp.where(lane == k, moved, out)
    return out


def zones_kernel(table_ref, zones_ref, x_ref, y_ref, coef_ref, west_ref, south_ref):
    for z in range(4):
        zone = zones_ref[z]
        rows = [jnp.zeros(zone.shape, f32)] * 3
        for index in range(table_ref.shape[1]):
            matched = zone == index
            rows = [jnp.where(matched, table_ref[row, index], rows[row]) for row in range(3)]
        coef_ref[0, z] = rows[0] * time_step
        coef_ref[1, z] = rows[1] * time_step
        coef_ref[2, z] = rows[2]
    lane = lane_index((64, PEERS))
    west_ref[...] = packed_column([x_ref[k // 4, 0, k % 4] for k in range(12)], PEERS - 1, lane)
    for k in range(12):
        south_ref[pl.ds(k, 1), :] = y_ref[k // 4, 0, k % 4, pl.ds(7, 1), :]


def early_kernel(feed, velocity_ref, stress_ref, west_ref, south_ref, coef_ref, early_ref, *feed_refs):
    lane = lane_index((64, PEERS))
    row = lax.broadcasted_iota(jnp.int32, (64, PEERS), 0)
    west = west_ref[...]
    for c in range(3):
        for z in range(4):
            k = c * 4 + z
            x, y = stress_ref[c, 0, z], stress_ref[c, 1, z]
            edge = pltpu.roll(west, (PEERS - k) % PEERS, 1) if k else west
            behind_x = jnp.where(lane == 0, edge, pltpu.roll(x, 1, 1))
            behind_y = jnp.where(row == 0, south_ref[pl.ds(k, 1), :], pltpu.roll(y, 1, 0))
            force = x - behind_x + y - behind_y
            if z < 3:
                force = force + stress_ref[c, 2, z]
            if z > 0:
                force = force - stress_ref[c, 2, z - 1]
            early = velocity_ref[c, z] + coef_ref[1, z] * force
            early_ref[c, z] = early
            if feed and z in (0, 3):
                plane = c if z == 0 else 3 + c
                for tile in range(GX):
                    feed_refs[0][tile, pl.ds(plane * 8, 8), :] = early[tile * 8 : tile * 8 + 8]
    if feed:
        for tile in range(GX):
            rows = pl.ds(tile * 8, 8)
            feed_refs[0][tile, pl.ds(48, 8), :] = -coef_ref[1, 0, rows, :]
            feed_refs[0][tile, pl.ds(56, 8), :] = coef_ref[1, 3, rows, :]


def velocity_kernel(early_ref, traction_ref, coef_ref, velocity_ref, east_ref, north_ref):
    for c in range(3):
        for z in range(4):
            if z in (1, 2):
                velocity_ref[c, z] = early_ref[c, z]
                continue
            plane = c if z == 0 else 3 + c
            for tile in range(GX):
                rows = pl.ds(tile * 8, 8)
                push = coef_ref[1, z, rows, :] * traction_ref[tile, pl.ds(plane * 8, 8), :]
                base = early_ref[c, z, rows, :]
                velocity_ref[c, z, rows, :] = base - push if z == 0 else base + push
    lane = lane_index((64, PEERS))
    east_ref[...] = packed_column([velocity_ref[k // 4, k % 4] for k in range(12)], 0, lane)
    for k in range(12):
        north_ref[pl.ds(k, 1), :] = velocity_ref[k // 4, k % 4, pl.ds(0, 1), :]


def stress_kernel(rims, velocity_ref, east_ref, north_ref, stress_ref, mask_ref, coef_ref, traction_ref, o_ref, *rim_refs):
    lane = lane_index((64, PEERS))
    row = lax.broadcasted_iota(jnp.int32, (64, PEERS), 0)
    east = east_ref[...]
    for z in range(4):
        rigidity = coef_ref[0, z]
        cohesion = coef_ref[2, z]
        keep = [mask_ref[d, z].astype(f32) for d in range(3)]
        total = jnp.zeros((64, PEERS), f32)
        trial = []
        for c in range(3):
            k = c * 4 + z
            v = velocity_ref[c, z]
            edge = pltpu.roll(east, PEERS - 1 - k, 1)
            ahead_x = jnp.where(lane == PEERS - 1, edge, pltpu.roll(v, PEERS - 1, 1))
            ahead_y = jnp.where(row == 63, north_ref[pl.ds(k, 1), :], pltpu.roll(v, 63, 0))
            tx = keep[0] * (stress_ref[c, 0, z] + rigidity * (ahead_x - v))
            ty = keep[1] * (stress_ref[c, 1, z] + rigidity * (ahead_y - v))
            if z < 3:
                tz = keep[2] * (stress_ref[c, 2, z] + rigidity * (velocity_ref[c, z + 1] - v))
            else:
                pulled = [traction_ref[tile, pl.ds((3 + c) * 8, 8), :] for tile in range(GX)]
                tz = keep[2] * jnp.concatenate(pulled, axis=0)
            trial.append((tx, ty, tz))
            total = total + (tx * tx + ty * ty + tz * tz)
        factor = cohesion / jnp.maximum(jnp.sqrt(total), cohesion)
        for c in range(3):
            for d in range(3):
                o_ref[c, d, z] = trial[c][d] * factor
    if rims:
        west_ref, south_ref = rim_refs
        west_ref[...] = packed_column([o_ref[k // 4, 0, k % 4] for k in range(12)], PEERS - 1, lane)
        for k in range(12):
            south_ref[pl.ds(k, 1), :] = o_ref[k // 4, 1, k % 4, pl.ds(63, 1), :]


def shape(*dims):
    return jax.ShapeDtypeStruct(dims, f32)


WORK = [pltpu.VMEM((PEERS, PEERS), f32), pltpu.VMEM((PEERS, PEERS), f32)]


def call(kernel, outs, *args, scratch=(), name=None):
    return pl.pallas_call(kernel, out_shape=outs, scratch_shapes=list(scratch), name=name)(*args)


def exchange_all(value):
    tiles = value.shape[0] // PEERS
    blocks = value.reshape(PEERS, 1, tiles * PEERS)
    blocks = lax.all_to_all(blocks, both, split_axis=0, concat_axis=0, tiled=True)
    return blocks.reshape(tiles * PEERS, PEERS)


def exchange_row(value):
    return lax.all_to_all(value, "gx", split_axis=0, concat_axis=0, tiled=True)


def shifted(value, axis, steps):
    count = lax.axis_size(axis)
    return lax.ppermute(value, axis, [(source, (source + steps) % count) for source in range(count)])


def planes_of(velocity):
    block = (3, 1, 64, PEERS)
    return pl.pallas_call(
        planes_kernel,
        grid=(1,),
        in_specs=[
            pl.BlockSpec(block, lambda i: (0, 0, 0, 0)),
            pl.BlockSpec(block, lambda i: (0, 3, 0, 0)),
        ],
        out_specs=pl.BlockSpec((GX, 48, PEERS), lambda i: (0, 0, 0)),
        out_shape=shape(GX, 48, PEERS),
        name="planes",
    )(velocity, velocity)


def zones_of(zone_table, zones, stress):
    whole = lambda *dims: pl.BlockSpec(dims, lambda i: (0,) * len(dims))
    return pl.pallas_call(
        zones_kernel,
        grid=(1,),
        in_specs=[
            pl.BlockSpec(memory_space=pltpu.SMEM),
            whole(4, 64, PEERS),
            pl.BlockSpec((3, 1, 4, 64, PEERS), lambda i: (0, 0, 0, 0, 0)),
            pl.BlockSpec((3, 1, 4, 8, PEERS), lambda i: (0, 1, 0, 7, 0)),
        ],
        out_specs=[whole(3, 4, 64, PEERS), whole(64, PEERS), whole(16, PEERS)],
        out_shape=[shape(3, 4, 64, PEERS), shape(64, PEERS), shape(16, PEERS)],
        name="zones",
    )(zone_table, zones, stress, stress)


def tails_of(history, memory):
    out_spec = pl.BlockSpec((1, 1, 2, 8, 1024), lambda p, c: (p, c, 0, 0, 0))
    now, later = pl.pallas_call(
        history_kernel,
        grid=(2, 3),
        in_specs=[
            pl.BlockSpec((1, 1, 31, 2, 8, 1024), lambda p, c: (p, c, 0, 0, 0, 0)),
            pl.BlockSpec((1, 31, 8, 1024), lambda p, c: (p, 0, 0, 0)),
        ],
        out_specs=[out_spec, out_spec],
        out_shape=[shape(2, 3, 2, 8, 1024)] * 2,
        name="tails",
    )(history, memory)
    return now.reshape(12, 8, 1024), later.reshape(12, 8, 1024)


def body(velocity, stress, face_mask, zones, zone_table, impedance, memory, history):
    mx, my, twist = tables()
    impedance = impedance.reshape(6, 8, 1024)
    first = memory[:, 0]
    field = shape(3, 4, 64, PEERS)
    rim_x, rim_y = shape(64, PEERS), shape(16, PEERS)
    packed = shape(6 * PEERS, PEERS)

    rows = exchange_row(planes_of(velocity))
    coef, west, south = zones_of(zone_table, zones, stress)
    west, south = shifted(west, "gx", 1), shifted(south, "gy", 1)
    now, later = tails_of(history, memory)
    sent = exchange_all(call(forward_kernel, packed, rows, mx, twist, scratch=WORK, name="forward"))
    early, feed = call(
        functools.partial(early_kernel, True),
        [field, shape(GX, 64, PEERS)],
        velocity, stress, west, south, coef,
        name="early0",
    )
    feed = exchange_row(feed)
    lines, later = call(
        functools.partial(dip_kernel, True),
        [packed, shape(12, 8, 1024)],
        sent, impedance, now, first, later, my, twist,
        scratch=WORK, name="dip0",
    )
    lines = exchange_all(lines)
    traction, packed_next = call(
        turn_kernel,
        [shape(GX, 48, PEERS), packed],
        lines, feed, mx, twist,
        scratch=WORK + [pltpu.VMEM((GX, 48, PEERS), f32)], name="turn",
    )
    sent = exchange_all(packed_next)
    traction = exchange_row(traction)
    velocity, east, north = call(velocity_kernel, [field, rim_x, rim_y], early, traction, coef, name="velocity0")
    east, north = shifted(east, "gx", -1), shifted(north, "gy", -1)
    lines = call(
        functools.partial(dip_kernel, False), packed, sent, impedance, later, my, twist, scratch=WORK, name="dip1"
    )
    lines = exchange_all(lines)
    stress, west, south = call(
        functools.partial(stress_kernel, True),
        [shape(3, 3, 4, 64, PEERS), rim_x, rim_y],
        velocity, east, north, stress, face_mask, coef, traction,
        name="stress0",
    )
    west, south = shifted(west, "gx", 1), shifted(south, "gy", 1)
    early = call(
        functools.partial(early_kernel, False), field, velocity, stress, west, south, coef, name="early1"
    )
    traction = call(inverse_kernel, shape(GX, 48, PEERS), lines, mx, twist, scratch=WORK, name="inverse")
    traction = exchange_row(traction)
    velocity, east, north = call(velocity_kernel, [field, rim_x, rim_y], early, traction, coef, name="velocity1")
    east, north = shifted(east, "gx", -1), shifted(north, "gy", -1)
    stress = call(
        functools.partial(stress_kernel, False),
        shape(3, 3, 4, 64, PEERS),
        velocity, east, north, stress, face_mask, coef, traction,
        name="stress1",
    )
    return (velocity, stress)


def solution(mesh):
    in_specs = (
        P(None, None, "gy", "gx"),
        P(None, None, None, "gy", "gx"),
        P(None, None, "gy", "gx"),
        P(None, "gy", "gx"),
        P(),
        P(None, None, both, None),
        P(None, None, both, None),
        P(None, None, None, None, both, None),
    )
    out_specs = (P(None, None, "gy", "gx"), P(None, None, None, "gy", "gx"))
    return jax.shard_map(body, mesh=mesh, in_specs=in_specs, out_specs=out_specs, check_vma=False)
```

time: 538 us -> 174 us (0.32); the launches traced: 528 us -> 171 us
  local copies, waits for them, and re-layouts: 176 us -> 4.62 us
  matrix products: 161 us -> 0 us
  other arithmetic: 83.1 us -> 0 us
  blocking collectives: 0 us -> 71.7 us
  starting transfers between devices: 71.3 us -> 29 us
  Pallas kernels: 0 us -> 41 us
  waiting for transfers between devices: 33.5 us -> 24.3 us
    dot_general x58 -> x0, matrix products: 161 us -> none  [the longest x28 121 us: second_section(): return jnp.einsum('...kb,bq->...qk', values, table, precision=highest)]
    all_to_all x0 -> x4, blocking collectives: none -> 71.7 us  [the longest x3 56.3 us: exchange_all(): lax.all_to_all(blocks, both, split_axis=0, concat_axis=0, tiled=True)]
    unnamed x160 -> x24, local copies, waits for them, and re-layouts: 46.7 us -> 3.14 us
    pallas_call x0 -> x14, Pallas kernels: none -> 41 us  [the longest x11 29.3 us: call(): pl.pallas_call(kernel, out_shape=outs, scratch_shapes=list(scratch), name...]
    all_to_all x10 -> x4, starting transfers between devices: 57.5 us -> 18.2 us  [the longest x3 11.9 us: exchange_row(): return lax.all_to_all(value, 'gx', split_axis=0, concat_axis=0, tiled=True)]
    mul x20 -> x0, local copies, waits for them, and re-layouts: 36 us -> none  [the longest x10 18.6 us: transform_last(): out_real.reshape(lead + (length,)) * scale]
    reshape x8 -> x0, local copies, waits for them, and re-layouts: 25.5 us -> none  [the longest x2 12.5 us: one_exchange(): blocks = blocks.reshape(-1, *inside)]
    all_to_all x10 -> x4, waiting for transfers between devices: 28.1 us -> 6.3 us  [the longest x3 6.29 us: exchange_row(): return lax.all_to_all(value, 'gx', split_axis=0, concat_axis=0, tiled=True)]
  transfers between devices with their start and end apart: 18 -> 12, of which waited for: 7 -> 7; matrix products, arithmetic and copies ran while one was open for 47% -> 1% of each run, Pallas kernels for 0% -> 15%
where the time goes in v1:
time: 174 us; the launch traced here: 171 us
  blocking collectives  71.7 us (41%)
  Pallas kernels  41 us (24%)
  starting transfers between devices  29 us (17%)
  waiting for transfers between devices  24.3 us (14%)
  local copies, waits for them, and re-layouts  4.62 us (3%)
    all_to_all x3, blocking collectives, exchange_all(): lax.all_to_all(blocks, both, split_axis=0, concat_axis=0, tiled=True)  56.3 us
    pallas_call x11, Pallas kernels, call(): pl.pallas_call(kernel, out_shape=outs, scratch_shapes=list(scratch), name...  29.3 us
    ppermute x8, waiting for transfers between devices, shifted(): lax.ppermute(value, axis, [(source, (source + steps) % count) for source...  18 us
    all_to_all x1, blocking collectives, exchange_row(): return lax.all_to_all(value, 'gx', split_axis=0, concat_axis=0, tiled=True)  15.4 us
    all_to_all x3, starting transfers between devices, exchange_row(): return lax.all_to_all(value, 'gx', split_axis=0, concat_axis=0, tiled=True)  11.9 us
    ppermute x8, starting transfers between devices, shifted(): lax.ppermute(value, axis, [(source, (source + steps) % count) for source...  10.7 us
    pallas_call x1, Pallas kernels, tails_of(): pl.pallas_call(history_kernel, grid=(2, 3), in_specs=[pl.BlockSpec((1, 1,...  8 us
    all_to_all x1, starting transfers between devices, exchange_all(): lax.all_to_all(blocks, both, split_axis=0, concat_axis=0, tiled=True)  6.39 us
  transfers between devices with their start and end apart: 12, of which 7 were waited for; matrix products, arithmetic and copies ran while one was open for 1% of the time, Pallas kernels for 15%

profile of v1, /device:TPU:2, one launch (start us, length us, event | category | flops | bytes accessed | tf_op | source)
XLA Modules:
  0.0 171.3 jit_solution(13449895897030851922)
XLA Ops:
  0.6 1.6 planes.1
  2.3 15.4 %all_to_all.40.x_ref = f32[8,48,128]{2,1,0:T(8,128)} all-to-all(f32[8,48,128]{2,1,0:T(8,128)} %planes.1), channel_id=1, replica_groups=mesh['gx'=8,'gy'=16] {'gx'}, dimensions={0} | all-to-all | bytes 393216 | tf_op jit(solution)/shard_map/all_to_all | solution.py:354
  17.7 2.2 %forward.1 = f32[768,128]{1,0:T(8,128)} custom-call(f32[8,48,128]{2,1,0:T(8,128)} %all_to_all.40.x_ref, bf16[2,256,256]{2,1,0:T(8,128)(2,1)} %constant.18.mx_ref, f32[2,8,8,128]{3,2,1,0:T(8,128)} %constant.8.clone.twist_ref.refs_3_.refs_1_), custom_call_target="tpu_custom_call" | custom-call | tf_op jit(solution)/shard_map/forward/pallas_call | solution.py:343
  19.9 6.4 %all-to-all-start.1 = ((f32[128,1,768]{2,1,0:T(1,128)}), f32[128,1,768]{2,1,0:T(1,128)S(1)}, u32[]{:S(2)}, u32[]{:S(2)}) async-start(f32[128,1,768]{2,1,0:T(1,128)} %bitcast.16), calls=%async_computation.1 | async-start | bytes 786432 | tf_op jit(solution)/shard_map/all_to_all | solution.py:349
  26.3 2.1 %zones.1 = (f32[3,4,64,128]{3,2,1,0:T(8,128)}, f32[64,128]{1,0:T(8,128)}, f32[16,128]{1,0:T(8,128)}) custom-call(f32[3,8]{1,0:T(4,128)} %table_ref.1, s32[4,64,128]{2,1,0:T(8,128)} %zones_ref.1, f32[3,3,4,64,128]{4,3,2,1,0:T(8,128)} %stress_ref.3, f32[3,3,4,64,128]{4,3,2,1,0:T(8,128)} %stress_ref.3), custom_call_target="tpu_custom_call" | custom-call | tf_op jit(solution)/shard_map/zones/pallas_call | solution.py:379
  28.4 1.6 collective-permute-start
  30.0 0.0 collective-permute-start.1
  30.0 5.4 %collective-permute-done.1.south_ref = f32[16,128]{1,0:T(8,128)S(1)} collective-permute-done((f32[16,128]{1,0:T(8,128)}, f32[16,128]{1,0:T(8,128)S(1)}, u32[]{:S(2)}, u32[]{:S(2)}) %collective-permute-start.1) | collective-permute-done | bytes 8224 | tf_op jit(solution)/shard_map/ppermute | solution.py:359
  35.4 1.2 collective-permute-done.west_ref
  36.6 0.6 copy-done.6
  37.2 2.6 %early0.1 = (f32[3,4,64,128]{3,2,1,0:T(8,128)}, f32[8,64,128]{2,1,0:T(8,128)}) custom-call(f32[3,4,64,128]{3,2,1,0:T(8,128)} %high_ref.1, f32[3,3,4,64,128]{4,3,2,1,0:T(8,128)} %stress_ref.3, f32[64,128]{1,0:T(8,128)} %copy-done.6, f32[16,128]{1,0:T(8,128)} %copy-done.10, f32[3,4,64,128]{3,2,1,0:T(8,128)} %get-tuple-element.24.coef_ref), custom_call_target="tpu_custom_call" | custom-call | tf_op jit(solution)/shard_map/early0/pallas_call | solution.py:343
  39.8 0.0 all-to-all-done.1
  39.8 4.9 %all-to-all-start.3 = ((f32[8,64,128]{2,1,0:T(8,128)}), f32[8,64,128]{2,1,0:T(8,128)S(1)}, u32[]{:S(2)}, u32[]{:S(2)}) async-start(f32[8,64,128]{2,1,0:T(8,128)} %get-tuple-element.29), calls=%async_computation.3 | async-start | bytes 524288 | tf_op jit(solution)/shard_map/all_to_all | solution.py:354
  44.7 8.0 %tails.1 = (f32[2,3,2,8,1024]{4,3,2,1,0:T(8,128)}, f32[2,3,2,8,1024]{4,3,2,1,0:T(8,128)}) custom-call(f32[2,3,31,2,8,1024]{5,4,3,2,1,0:T(8,128)} %history_ref.1, f32[2,31,8,1024]{3,2,1,0:T(8,128)} %memory_ref.1), custom_call_target="tpu_custom_call" | custom-call | tf_op jit(solution)/shard_map/tails/pallas_call | solution.py:396
  52.7 1.5 slice_bitcast_fusion.refs_0_
  54.2 3.4 %dip0.1 = (f32[768,128]{1,0:T(8,128)}, f32[12,8,1024]{2,1,0:T(8,128)}) custom-call(f32[768,128]{1,0:T(8,128)} %bitcast.15, f32[6,8,1024]{2,1,0:T(8,128)} %bitcast.21, f32[12,8,1024]{2,1,0:T(8,128)} %bitcast.23, f32[2,8,1024]{2,1,0:T(8,128)} %slice_bitcast_fusion.refs_0_, f32[12,8,1024]{2,1,0:T(8,128)} %bitcast.24, ...), custom_call_target="tpu_custom_call" | custom-call | tf_op jit(solution)/shard_map/dip0/pallas_call | solution.py:343
  57.6 0.0 all-to-all-done.3.early_ref
  57.6 21.0 %all_to_all.41 = f32[128,1,768]{2,1,0:T(1,128)} all-to-all(f32[128,1,768]{2,1,0:T(1,128)} %bitcast.25), channel_id=1, replica_groups=mesh['gx'=8,'gy'=16] {'gx','gy'}, dimensions={0} | all-to-all | bytes 786432 | tf_op jit(solution)/shard_map/all_to_all | solution.py:349
  78.6 2.9 %turn.1 = (f32[8,48,128]{2,1,0:T(8,128)}, f32[768,128]{1,0:T(8,128)}) custom-call(f32[768,128]{1,0:T(8,128)} %bitcast.18, f32[8,64,128]{2,1,0:T(8,128)} %copy-done.3, bf16[2,256,256]{2,1,0:T(8,128)(2,1)} %constant.18.mx_ref, f32[2,8,8,128]{3,2,1,0:T(8,128)} %constant.8.clone.twist_ref.refs_3_.refs_1_), custom_call_target="tpu_custom_call" | custom-call | tf_op jit(solution)/shard_map/turn/pallas_call | solution.py:343
  81.4 17.6 %all_to_all.42 = f32[128,1,768]{2,1,0:T(1,128)} all-to-all(f32[128,1,768]{2,1,0:T(1,128)} %bitcast.26), channel_id=1, replica_groups=mesh['gx'=8,'gy'=16] {'gx','gy'}, dimensions={0} | all-to-all | bytes 786432 | tf_op jit(solution)/shard_map/all_to_all | solution.py:349
  99.1 3.2 %dip1.1 = f32[768,128]{1,0:T(8,128)} custom-call(f32[768,128]{1,0:T(8,128)} %bitcast.19, f32[6,8,1024]{2,1,0:T(8,128)} %bitcast.22, f32[12,8,1024]{2,1,0:T(8,128)} %get-tuple-element.38.tail_ref, bf16[2,256,256]{2,1,0:T(8,128)(2,1)} %constant.25.refs_2_.refs_0_, f32[2,8,8,128]{3,2,1,0:T(8,128)} %constant.8.clone.twist_ref.refs_3_.refs_1_), custom_call_target="tpu_custom_call" | custom-call | tf_op jit(solution)/shard_map/dip1/pallas_call | solution.py:343
  102.3 17.6 %all_to_all.43 = f32[128,1,768]{2,1,0:T(1,128)} all-to-all(f32[128,1,768]{2,1,0:T(1,128)} %bitcast.20), channel_id=1, replica_groups=mesh['gx'=8,'gy'=16] {'gx','gy'}, dimensions={0} | all-to-all | bytes 786432 | tf_op jit(solution)/shard_map/all_to_all | solution.py:349
  119.9 3.6 %all-to-all-start.4 = ((f32[8,48,128]{2,1,0:T(8,128)}), f32[8,48,128]{2,1,0:T(8,128)S(1)}, u32[]{:S(2)}, u32[]{:S(2)}) async-start(f32[8,48,128]{2,1,0:T(8,128)} %get-tuple-element.30), calls=%async_computation.4 | async-start | bytes 393216 | tf_op jit(solution)/shard_map/all_to_all | solution.py:354
  123.5 2.1 %inverse.1 = f32[8,48,128]{2,1,0:T(8,128)} custom-call(f32[768,128]{1,0:T(8,128)} %bitcast.17, bf16[2,256,256]{2,1,0:T(8,128)(2,1)} %constant.18.mx_ref, f32[2,8,8,128]{3,2,1,0:T(8,128)} %constant.8.clone.twist_ref.refs_3_.refs_1_), custom_call_target="tpu_custom_call" | custom-call | tf_op jit(solution)/shard_map/inverse/pallas_call | solution.py:343
  125.7 6.3 %all-to-all-done.4.traction_ref = f32[8,48,128]{2,1,0:T(8,128)S(1)} async-done(((f32[8,48,128]{2,1,0:T(8,128)}), f32[8,48,128]{2,1,0:T(8,128)S(1)}, u32[]{:S(2)}, u32[]{:S(2)}) %all-to-all-start.4) | async-done | bytes 196640 | tf_op jit(solution)/shard_map/all_to_all | solution.py:354
  132.0 3.4 %all-to-all-start.7 = ((f32[8,48,128]{2,1,0:T(8,128)}), f32[8,48,128]{2,1,0:T(8,128)S(1)}, u32[]{:S(2)}, u32[]{:S(2)}) async-start(f32[8,48,128]{2,1,0:T(8,128)} %inverse.1), calls=%async_computation.7 | async-start | bytes 393216 | tf_op jit(solution)/shard_map/all_to_all | solution.py:354
  135.4 2.0 %velocity0.1 = (f32[3,4,64,128]{3,2,1,0:T(8,128)}, f32[64,128]{1,0:T(8,128)}, f32[16,128]{1,0:T(8,128)}) custom-call(f32[3,4,64,128]{3,2,1,0:T(8,128)} %get-tuple-element.25.early_ref, f32[8,48,128]{2,1,0:T(8,128)} %copy-done.1, f32[3,4,64,128]{3,2,1,0:T(8,128)} %get-tuple-element.24.coef_ref), custom_call_target="tpu_custom_call" | custom-call | tf_op jit(solution)/shard_map/velocity0/pallas_call | solution.py:343
  137.4 5.6 %collective-permute-start.2 = (f32[64,128]{1,0:T(8,128)}, f32[64,128]{1,0:T(8,128)S(1)}, u32[]{:S(2)}, u32[]{:S(2)}) collective-permute-start(f32[64,128]{1,0:T(8,128)} %get-tuple-element.32), channel_id=1, source_target_pairs={{0,112},{16,0},{32,16},{48,32},{64,48},{80,64},{96,80},{112,96},{1... | collective-permute-start | bytes 98312 | tf_op jit(solution)/shard_map/ppermute | solution.py:359
  142.9 0.0 collective-permute-start.3
  142.9 1.9 %collective-permute-done.3.north_ref = f32[16,128]{1,0:T(8,128)S(1)} collective-permute-done((f32[16,128]{1,0:T(8,128)}, f32[16,128]{1,0:T(8,128)S(1)}, u32[]{:S(2)}, u32[]{:S(2)}) %collective-permute-start.3) | collective-permute-done | bytes 8224 | tf_op jit(solution)/shard_map/ppermute | solution.py:359
  144.9 0.0 collective-permute-done.2.east_ref
  144.9 0.6 copy-done.8
  145.5 0.0 copy-done.4
  145.5 3.2 %stress0.1 = (f32[3,3,4,64,128]{4,3,2,1,0:T(8,128)}, f32[64,128]{1,0:T(8,128)}, f32[16,128]{1,0:T(8,128)}) custom-call(f32[3,4,64,128]{3,2,1,0:T(8,128)} %get-tuple-element.31.velocity_ref, f32[64,128]{1,0:T(8,128)} %copy-done.4, f32[16,128]{1,0:T(8,128)} %copy-done.8, f32[3,3,4,64,128]{4,3,2,1,0:T(8,128)} %stress_ref.3, s32[3,4,64,128]{3,2,1,0:T(8,128)} %mask_ref.3, ...), custom_call_target="tpu_custom_call" | custom-call | tf_op jit(solution)/shard_map/stress0/pallas_call | solution.py:343
  148.7 0.0 collective-permute-start.4
  148.7 0.3 collective-permute-start.5
  148.9 5.1 %collective-permute-done.5.south_ref = f32[16,128]{1,0:T(8,128)S(1)} collective-permute-done((f32[16,128]{1,0:T(8,128)}, f32[16,128]{1,0:T(8,128)S(1)}, u32[]{:S(2)}, u32[]{:S(2)}) %collective-permute-start.5) | collective-permute-done | bytes 8224 | tf_op jit(solution)/shard_map/ppermute | solution.py:359
  154.1 2.5 %collective-permute-done.4.west_ref = f32[64,128]{1,0:T(8,128)S(1)} collective-permute-done((f32[64,128]{1,0:T(8,128)}, f32[64,128]{1,0:T(8,128)S(1)}, u32[]{:S(2)}, u32[]{:S(2)}) %collective-permute-start.4) | collective-permute-done | bytes 32800 | tf_op jit(solution)/shard_map/ppermute | solution.py:359
  156.6 0.6 copy-done.7
  157.2 2.5 %early1.1.early_ref = f32[3,4,64,128]{3,2,1,0:T(8,128)} custom-call(f32[3,4,64,128]{3,2,1,0:T(8,128)} %get-tuple-element.31.velocity_ref, f32[3,3,4,64,128]{4,3,2,1,0:T(8,128)} %get-tuple-element.34.stress_ref, f32[64,128]{1,0:T(8,128)} %copy-done.7, f32[16,128]{1,0:T(8,128)} %copy-done.11, f32[3,4,64,128]{3,2,1,0:T(8,128)} %get-tuple-element.24.coef_ref), custom_call_target="tpu_custom_call" | custom-call | tf_op jit(solution)/shard_map/early1/pallas_call | solution.py:343
  159.7 0.0 all-to-all-done.7.traction_ref
  159.7 0.7 copy-done
  160.4 2.0 %velocity1.1 = (f32[3,4,64,128]{3,2,1,0:T(8,128)}, f32[64,128]{1,0:T(8,128)}, f32[16,128]{1,0:T(8,128)}) custom-call(f32[3,4,64,128]{3,2,1,0:T(8,128)} %early1.1.early_ref, f32[8,48,128]{2,1,0:T(8,128)} %copy-done, f32[3,4,64,128]{3,2,1,0:T(8,128)} %get-tuple-element.24.coef_ref), custom_call_target="tpu_custom_call" | custom-call | tf_op jit(solution)/shard_map/velocity1/pallas_call | solution.py:343
  162.4 3.3 %collective-permute-start.6 = (f32[64,128]{1,0:T(8,128)}, f32[64,128]{1,0:T(8,128)S(1)}, u32[]{:S(2)}, u32[]{:S(2)}) collective-permute-start(f32[64,128]{1,0:T(8,128)} %get-tuple-element.40), channel_id=1, source_target_pairs={{0,112},{16,0},{32,16},{48,32},{64,48},{80,64},{96,80},{112,96},{1... | collective-permute-start | bytes 98312 | tf_op jit(solution)/shard_map/ppermute | solution.py:359
  165.7 1.9 %collective-permute-done.7.north_ref = f32[16,128]{1,0:T(8,128)S(1)} collective-permute-done((f32[16,128]{1,0:T(8,128)}, f32[16,128]{1,0:T(8,128)S(1)}, u32[]{:S(2)}, u32[]{:S(2)}) %collective-permute-start.7) | collective-permute-done | bytes 8224 | tf_op jit(solution)/shard_map/ppermute | solution.py:359
  167.6 0.6 copy-done.9
  168.2 0.0 copy-done.5
  168.2 3.1 %stress1.1 = f32[3,3,4,64,128]{4,3,2,1,0:T(8,128)} custom-call(f32[3,4,64,128]{3,2,1,0:T(8,128)} %get-tuple-element.20.velocity_ref, f32[64,128]{1,0:T(8,128)} %copy-done.5, f32[16,128]{1,0:T(8,128)} %copy-done.9, f32[3,3,4,64,128]{4,3,2,1,0:T(8,128)} %get-tuple-element.34.stress_ref, s32[3,4,64,128]{3,2,1,0:T(8,128)} %mask_ref.3, ...), custom_call_target="tpu_custom_call" | custom-call | tf_op jit(solution)/shard_map/stress1/pallas_call | solution.py:343
  (19 shorter events, 0.0 us)
Async XLA Ops:
  19.9 19.9 %all-to-all-start.1 = ((f32[128,1,768]{2,1,0:T(1,128)}), f32[128,1,768]{2,1,0:T(1,128)S(1)}, u32[]{:S(2)}, u32[]{:S(2)}) async-start(f32[128,1,768]{2,1,0:T(1,128)} %bitcast.16), calls=%async_computation.1 | async-start | bytes 786432 | tf_op jit(solution)/shard_map/all_to_all | solution.py:349
  28.4 8.2 %collective-permute-start = (f32[64,128]{1,0:T(8,128)}, f32[64,128]{1,0:T(8,128)S(1)}, u32[]{:S(2)}, u32[]{:S(2)}) collective-permute-start(f32[64,128]{1,0:T(8,128)} %get-tuple-element.22), channel_id=1, source_target_pairs={{0,16},{16,32},{32,48},{48,64},{64,80},{80,96},{96,112},{112,0},{1... | collective-permute-start | bytes 98312 | tf_op jit(solution)/shard_map/ppermute | solution.py:359
  30.0 5.4 %collective-permute-start.1 = (f32[16,128]{1,0:T(8,128)}, f32[16,128]{1,0:T(8,128)S(1)}, u32[]{:S(2)}, u32[]{:S(2)}) collective-permute-start(f32[16,128]{1,0:T(8,128)} %get-tuple-element.23), channel_id=1, source_target_pairs={{0,1},{1,2},{2,3},{3,4},{4,5},{5,6},{6,7},{7,8},{8,9},{9,10},{10,1... | collective-permute-start | bytes 24584 | tf_op jit(solution)/shard_map/ppermute | solution.py:359
  35.4 1.2 copy-start.10
  36.6 0.6 copy-start.6
  39.8 12.9 %copy-start.2 = (f32[128,1,768]{2,1,0:T(1,128)}, f32[128,1,768]{2,1,0:T(1,128)S(1)}, u32[]{:S(2)}) copy-start(f32[128,1,768]{2,1,0:T(1,128)S(1)} %all-to-all-done.1) | copy-start | bytes 1179652
  39.8 17.7 %all-to-all-start.3 = ((f32[8,64,128]{2,1,0:T(8,128)}), f32[8,64,128]{2,1,0:T(8,128)S(1)}, u32[]{:S(2)}, u32[]{:S(2)}) async-start(f32[8,64,128]{2,1,0:T(8,128)} %get-tuple-element.29), calls=%async_computation.3 | async-start | bytes 524288 | tf_op jit(solution)/shard_map/all_to_all | solution.py:354
  57.6 21.0 %copy-start.3 = (f32[8,64,128]{2,1,0:T(8,128)}, f32[8,64,128]{2,1,0:T(8,128)S(1)}, u32[]{:S(2)}) copy-start(f32[8,64,128]{2,1,0:T(8,128)S(1)} %all-to-all-done.3.early_ref) | copy-start | bytes 786436
  119.9 12.0 %all-to-all-start.4 = ((f32[8,48,128]{2,1,0:T(8,128)}), f32[8,48,128]{2,1,0:T(8,128)S(1)}, u32[]{:S(2)}, u32[]{:S(2)}) async-start(f32[8,48,128]{2,1,0:T(8,128)} %get-tuple-element.30), calls=%async_computation.4 | async-start | bytes 393216 | tf_op jit(solution)/shard_map/all_to_all | solution.py:354
  132.0 3.4 %copy-start.1 = (f32[8,48,128]{2,1,0:T(8,128)}, f32[8,48,128]{2,1,0:T(8,128)S(1)}, u32[]{:S(2)}) copy-start(f32[8,48,128]{2,1,0:T(8,128)S(1)} %all-to-all-done.4.traction_ref) | copy-start | bytes 589828
  132.0 27.7 %all-to-all-start.7 = ((f32[8,48,128]{2,1,0:T(8,128)}), f32[8,48,128]{2,1,0:T(8,128)S(1)}, u32[]{:S(2)}, u32[]{:S(2)}) async-start(f32[8,48,128]{2,1,0:T(8,128)} %inverse.1), calls=%async_computation.7 | async-start | bytes 393216 | tf_op jit(solution)/shard_map/all_to_all | solution.py:354
  137.4 7.5 %collective-permute-start.2 = (f32[64,128]{1,0:T(8,128)}, f32[64,128]{1,0:T(8,128)S(1)}, u32[]{:S(2)}, u32[]{:S(2)}) collective-permute-start(f32[64,128]{1,0:T(8,128)} %get-tuple-element.32), channel_id=1, source_target_pairs={{0,112},{16,0},{32,16},{48,32},{64,48},{80,64},{96,80},{112,96},{1... | collective-permute-start | bytes 98312 | tf_op jit(solution)/shard_map/ppermute | solution.py:359
  142.9 1.9 %collective-permute-start.3 = (f32[16,128]{1,0:T(8,128)}, f32[16,128]{1,0:T(8,128)S(1)}, u32[]{:S(2)}, u32[]{:S(2)}) collective-permute-start(f32[16,128]{1,0:T(8,128)} %get-tuple-element.33), channel_id=1, source_target_pairs={{0,15},{1,0},{2,1},{3,2},{4,3},{5,4},{6,5},{7,6},{8,7},{9,8},{10,9... | collective-permute-start | bytes 24584 | tf_op jit(solution)/shard_map/ppermute | solution.py:359
  144.9 0.6 copy-start.8
  144.9 0.6 copy-start.4
  148.7 7.9 %collective-permute-start.4 = (f32[64,128]{1,0:T(8,128)}, f32[64,128]{1,0:T(8,128)S(1)}, u32[]{:S(2)}, u32[]{:S(2)}) collective-permute-start(f32[64,128]{1,0:T(8,128)} %get-tuple-element.35), channel_id=1, source_target_pairs={{0,16},{16,32},{32,48},{48,64},{64,80},{80,96},{96,112},{112,0},{1... | collective-permute-start | bytes 98312 | tf_op jit(solution)/shard_map/ppermute | solution.py:359
  148.7 5.4 %collective-permute-start.5 = (f32[16,128]{1,0:T(8,128)}, f32[16,128]{1,0:T(8,128)S(1)}, u32[]{:S(2)}, u32[]{:S(2)}) collective-permute-start(f32[16,128]{1,0:T(8,128)} %get-tuple-element.36), channel_id=1, source_target_pairs={{0,1},{1,2},{2,3},{3,4},{4,5},{5,6},{6,7},{7,8},{8,9},{9,10},{10,1... | collective-permute-start | bytes 24584 | tf_op jit(solution)/shard_map/ppermute | solution.py:359
  154.1 2.5 %copy-start.11 = (f32[16,128]{1,0:T(8,128)}, f32[16,128]{1,0:T(8,128)S(1)}, u32[]{:S(2)}) copy-start(f32[16,128]{1,0:T(8,128)S(1)} %collective-permute-done.5.south_ref) | copy-start | bytes 24580
  156.6 0.6 copy-start.7
  159.7 0.7 copy-start
  162.4 5.2 %collective-permute-start.6 = (f32[64,128]{1,0:T(8,128)}, f32[64,128]{1,0:T(8,128)S(1)}, u32[]{:S(2)}, u32[]{:S(2)}) collective-permute-start(f32[64,128]{1,0:T(8,128)} %get-tuple-element.40), channel_id=1, source_target_pairs={{0,112},{16,0},{32,16},{48,32},{64,48},{80,64},{96,80},{112,96},{1... | collective-permute-start | bytes 98312 | tf_op jit(solution)/shard_map/ppermute | solution.py:359
  165.7 1.9 %collective-permute-start.7 = (f32[16,128]{1,0:T(8,128)}, f32[16,128]{1,0:T(8,128)S(1)}, u32[]{:S(2)}, u32[]{:S(2)}) collective-permute-start(f32[16,128]{1,0:T(8,128)} %get-tuple-element.41), channel_id=1, source_target_pairs={{0,15},{1,0},{2,1},{3,2},{4,3},{5,4},{6,5},{7,6},{8,7},{9,8},{10,9... | collective-permute-start | bytes 24584 | tf_op jit(solution)/shard_map/ppermute | solution.py:359
  167.6 0.6 copy-start.9
  167.6 0.6 copy-start.5

commit v2 on v1

v2 whole, which is shorter than its diff:
```python
import functools
import math

import jax
import jax.numpy as jnp
import numpy as np
from jax import lax
from jax.experimental import pallas as pl
from jax.experimental.pallas import tpu as pltpu
from jax.sharding import PartitionSpec as P


time_step = 0.2
GX = 8
GY = 16
PEERS = 128
f32 = jnp.float32
bf16 = jnp.bfloat16
TILES = 7
both = ("gx", "gy")
half_root = math.sqrt(0.5)


def halves(table):
    high = jnp.asarray(table, f32).astype(bf16)
    low = (jnp.asarray(table, f32) - high.astype(f32)).astype(bf16)
    return jnp.stack([high, low])


def tables():
    index = np.arange(PEERS)
    angle = 2.0 * np.pi * (np.outer(index, index) % PEERS) / PEERS
    c, s = np.cos(angle) / 32.0, np.sin(angle) / 32.0
    along_x = np.block([[c, s], [-s, c]])
    place = 8 * (index % GY) + index // GY
    angle = 2.0 * np.pi * (np.outer(place, index) % PEERS) / PEERS
    c, s = np.cos(angle) / 32.0, np.sin(angle) / 32.0
    along_y = np.block([[c, -s], [s, c]])
    turn = 2.0 * np.pi * np.outer(np.arange(8), index) / 1024.0
    twist = np.stack([np.cos(turn), np.sin(turn)])
    twist = np.broadcast_to(twist[:, :, None, :], (2, 8, 8, PEERS))
    turn = 2.0 * np.pi * index / PEERS
    ahead = np.broadcast_to(np.stack([np.cos(turn), np.sin(turn)])[:, None, :], (2, 8, PEERS))
    return halves(along_x), halves(along_y), jnp.asarray(twist, f32), jnp.asarray(ahead, f32)


def plus(a, b):
    imag = a[1] if b[1] is None else b[1] if a[1] is None else a[1] + b[1]
    return (a[0] + b[0], imag)


def minus(a, b):
    imag = a[1] if b[1] is None else -b[1] if a[1] is None else a[1] - b[1]
    return (a[0] - b[0], imag)


def turned(a, sign):
    if a[1] is None:
        return (jnp.zeros_like(a[0]), a[0] if sign > 0 else -a[0])
    return (-a[1], a[0]) if sign > 0 else (a[1], -a[0])


def four(x, sign):
    a, b = plus(x[0], x[2]), minus(x[0], x[2])
    c, d = plus(x[1], x[3]), turned(minus(x[1], x[3]), sign)
    return [plus(a, c), plus(b, d), minus(a, c), minus(b, d)]


def eight(x, sign):
    even, odd = four(x[0::2], sign), four(x[1::2], sign)
    o1, o3 = odd[1], odd[3]
    odd1 = ((o1[0] - sign * o1[1]) * half_root, (o1[1] + sign * o1[0]) * half_root)
    odd3 = ((-o3[0] - sign * o3[1]) * half_root, (sign * o3[0] - o3[1]) * half_root)
    odd = [odd[0], odd1, turned(odd[2], sign), odd3]
    return [plus(e, o) for e, o in zip(even, odd)] + [minus(e, o) for e, o in zip(even, odd)]


def split(x):
    high = x.astype(bf16)
    return high, (x - high.astype(f32)).astype(bf16)


def product(a, b, dims):
    dot = functools.partial(lax.dot_general, dimension_numbers=(dims, ((), ())), preferred_element_type=f32)
    return dot(a[0], b[0]) + (dot(a[1], b[0]) + dot(a[0], b[1]))


def from_peers(x_ref, pair, matrix, re_ref, im_ref, tiles):
    x = jnp.concatenate([x_ref[pl.ds(2 * pair + part, PEERS, stride=tiles), :] for part in range(2)], axis=0)
    y = product(split(x), matrix, ((0,), (0,)))
    re_ref[...] = y[:, :PEERS]
    im_ref[...] = y[:, PEERS:]


def to_peers(o_ref, pair, matrix, re_ref, im_ref, tiles):
    t = split(jnp.concatenate([re_ref[...], im_ref[...]], axis=1))
    out = product(matrix, t, ((1,), (1,)))
    for part in range(2):
        o_ref[pl.ds(2 * pair + part, PEERS, stride=tiles), :] = out[part * PEERS : (part + 1) * PEERS]


def twisted(value, twist_ref, index, sign):
    if index == 0:
        return value
    c, s = twist_ref[0, index], twist_ref[1, index]
    if sign < 0:
        return (value[0] * c + value[1] * s, value[1] * c - value[0] * s)
    return (value[0] * c - value[1] * s, value[1] * c + value[0] * s)


def strike_forward(take, twist_ref, matrix, o_ref, re_ref, im_ref):
    for pair in range(3):
        for member in range(2):
            plane = 2 * pair + member
            waves = eight([(take(plane, tile), None) for tile in range(GX)], -1.0)
            for k in range(8):
                re, im = waves[k]
                if im is None:
                    im = jnp.zeros_like(re)
                re, im = twisted((re, im), twist_ref, k, -1)
                rows = pl.ds(member * 64 + k * 8, 8)
                re_ref[rows, :] = re
                im_ref[rows, :] = im
        to_peers(o_ref, pair, matrix, re_ref, im_ref, 6)


def strike_inverse(x_ref, twist_ref, matrix, d_ref, re_ref, im_ref, put):
    lane = lane_index((8, PEERS))
    edges = [jnp.zeros((8, PEERS), f32)] * GX
    for pair in range(3):
        from_peers(x_ref, pair, matrix, re_ref, im_ref, TILES)
        for member in range(2):
            plane = 2 * pair + member
            values = []
            for k in range(8):
                rows = pl.ds(member * 64 + k, 8, stride=8)
                values.append(twisted((re_ref[rows, :], im_ref[rows, :]), twist_ref, k, 1))
            field = eight(values, 1.0)
            for tile in range(GX):
                value = field[tile][0]
                d_ref[tile, pl.ds(plane * 8, 8), :] = value
                moved = pltpu.roll(value, plane, 1) if plane else value
                before = (tile + GX - 1) % GX
                edges[before] = jnp.where(lane == plane, moved, edges[before])
                put(plane, tile, value)
    for tile in range(GX):
        d_ref[tile, pl.ds(56, 8), :] = edges[tile]
    x = split(x_ref[pl.ds(6, PEERS, stride=TILES), :])
    y = product(x, (matrix[0][:PEERS], matrix[1][:PEERS]), ((0,), (0,)))
    re_ref[...] = y[:, :PEERS]
    im_ref[...] = y[:, PEERS:]
    values = []
    for k in range(8):
        low, high = pl.ds(k, 8, stride=8), pl.ds(64 + k, 8, stride=8)
        value = (re_ref[low, :] - im_ref[high, :], im_ref[low, :] + re_ref[high, :])
        values.append(twisted(value, twist_ref, k, 1))
    field = eight(values, 1.0)
    for tile in range(GX):
        d_ref[tile, pl.ds(48, 8), :] = field[tile][0]


def forward_kernel(x_ref, mx_ref, twist_ref, o_ref, re_ref, im_ref):
    matrix = (mx_ref[0], mx_ref[1])
    take = lambda plane, tile: x_ref[tile, pl.ds(plane * 24, 8), :]
    strike_forward(take, twist_ref, matrix, o_ref, re_ref, im_ref)


def dip_kernel(carry, x_ref, my_ref, twist_ref, ahead_ref, impedance_ref, *refs):
    if carry:
        now, (memory_ref, *later) = refs[:2], refs[2:5]
        o_ref, *next_refs = refs[5:8]
        re_ref, im_ref, re2_ref, im2_ref, z_ref, tail_ref, sems, first_ref, later_ref, more_sems = refs[8:]
    else:
        now = refs[:2]
        o_ref, re_ref, im_ref, re2_ref, im2_ref, z_ref, tail_ref, sems = refs[2:]

    def copies(pair):
        jobs = []
        for plane in (2 * pair, 2 * pair + 1):
            side, part = plane // 3, pl.ds(2 * (plane % 3), 2)
            jobs.append((impedance_ref.at[plane], z_ref.at[plane], sems.at[plane, 0]))
            jobs.append((now[side].at[part], tail_ref.at[plane], sems.at[plane, 1]))
            if carry:
                jobs.append((later[side].at[part], later_ref.at[plane], more_sems.at[plane, 0]))
        if carry and pair == 0:
            jobs.append((memory_ref.at[:, 0], first_ref, more_sems.at[6, 0]))
        return [pltpu.make_async_copy(*job) for job in jobs]

    arriving = [copies(pair) for pair in range(3)]
    for group in arriving:
        for copy in group:
            copy.start()
    leaving = []
    matrix = (my_ref[0], my_ref[1])
    re2_ref[...] = jnp.zeros((PEERS, PEERS), f32)
    im2_ref[...] = jnp.zeros((PEERS, PEERS), f32)
    c8, s8 = ahead_ref[0], ahead_ref[1]
    for pair in range(3):
        from_peers(x_ref, pair, matrix, re_ref, im_ref, 6)
        for copy in arriving[pair]:
            copy.wait()
        for member in range(2):
            plane = 2 * pair + member
            side, part = plane // 3, 2 * (plane % 3)
            values = []
            for j in range(8):
                rows = pl.ds(member * 64 + j, 8, stride=8)
                values.append(twisted((re_ref[rows, :], im_ref[rows, :]), twist_ref, j, -1))
            spectrum = eight(values, -1.0)
            response = []
            for tile in range(8):
                lanes = pl.ds(tile * PEERS, PEERS)
                z = z_ref[plane, :, lanes]
                re, im = spectrum[tile]
                response.append((tail_ref[plane, 0, :, lanes] - z * re, tail_ref[plane, 1, :, lanes] - z * im))
                if carry:
                    first = first_ref[side, :, lanes]
                    later_ref[plane, 0, :, lanes] = later_ref[plane, 0, :, lanes] + first * re
                    later_ref[plane, 1, :, lanes] = later_ref[plane, 1, :, lanes] + first * im
            if carry:
                target = next_refs[side].at[pl.ds(part, 2)]
                leaving.append(pltpu.make_async_copy(later_ref.at[plane], target, more_sems.at[plane, 1]))
                leaving[-1].start()
            lines = eight(response, 1.0)
            for j in range(8):
                re, im = twisted(lines[j], twist_ref, j, 1)
                rows = pl.ds(member * 64 + j * 8, 8)
                re_ref[rows, :] = re
                im_ref[rows, :] = im
                if j == 0:
                    re, im = re * c8 - im * s8, im * c8 + re * s8
                    for half, (a, b) in enumerate(((re, im), (im, -re))):
                        rows = pl.ds(half * 64 + plane * 8, 8)
                        re2_ref[rows, :] = a
                        im2_ref[rows, :] = b
        to_peers(o_ref, pair, matrix, re_ref, im_ref, TILES)
    t = split(jnp.concatenate([re2_ref[...], im2_ref[...]], axis=1))
    o_ref[pl.ds(6, PEERS, stride=TILES), :] = product((matrix[0][:PEERS], matrix[1][:PEERS]), t, ((1,), (1,)))
    for copy in leaving:
        copy.wait()


def turn_kernel(x_ref, early_ref, mx_ref, twist_ref, o_ref, d_ref, re_ref, im_ref, plane_ref):
    matrix = (mx_ref[0], mx_ref[1])

    def put(plane, tile, value):
        gain = early_ref[tile, pl.ds(48 + (plane // 3) * 8, 8), :]
        plane_ref[tile, pl.ds(plane * 8, 8), :] = early_ref[tile, pl.ds(plane * 8, 8), :] + gain * value

    strike_inverse(x_ref, twist_ref, matrix, d_ref, re_ref, im_ref, put)
    take = lambda plane, tile: plane_ref[tile, pl.ds(plane * 8, 8), :]
    strike_forward(take, twist_ref, matrix, o_ref, re_ref, im_ref)


def inverse_kernel(x_ref, mx_ref, twist_ref, d_ref, re_ref, im_ref):
    matrix = (mx_ref[0], mx_ref[1])
    strike_inverse(x_ref, twist_ref, matrix, d_ref, re_ref, im_ref, lambda plane, tile, value: None)


def history_kernel(history_ref, memory_ref, now_ref, next_ref):
    lags = history_ref.shape[2]
    for tile in range(8):
        lanes = pl.ds(tile * PEERS, PEERS)
        for part in range(2):
            now = jnp.zeros((8, PEERS), f32)
            later = jnp.zeros((8, PEERS), f32)
            for lag in range(lags):
                value = history_ref[0, 0, lag, part, :, lanes]
                now = now + memory_ref[0, lag, :, lanes] * value
                if lag + 1 < lags:
                    later = later + memory_ref[0, lag + 1, :, lanes] * value
            now_ref[part, :, lanes] = now
            next_ref[part, :, lanes] = later


def pack_kernel(table_ref, velocity_ref, stress_ref, zones_ref, o_ref, v_ref, x_ref, y_ref, z_ref, zone_ref, sems):
    copies = []
    for side in range(2):
        jobs = (
            (velocity_ref.at[:, 3 * side], v_ref.at[side]),
            (stress_ref.at[:, 0, 3 * side], x_ref.at[side]),
            (stress_ref.at[:, 1, 3 * side], y_ref.at[side]),
            (stress_ref.at[:, 2, 2 * side], z_ref.at[side]),
            (zones_ref.at[3 * side], zone_ref.at[side]),
        )
        for number, (source, target) in enumerate(jobs):
            copies.append(pltpu.make_async_copy(source, target, sems.at[side, number]))
    for copy in copies:
        copy.start()
    for copy in copies:
        copy.wait()
    row = lax.broadcasted_iota(jnp.int32, (64, PEERS), 0)
    for side in range(2):
        zone = zone_ref[side]
        gain = jnp.zeros(zone.shape, f32)
        for index in range(table_ref.shape[1]):
            gain = jnp.where(zone == index, table_ref[1, index], gain)
        gain = gain * time_step
        for c in range(3):
            plane = 3 * side + c
            v, x, y, z = v_ref[side, c], x_ref[side, c], y_ref[side, c], z_ref[side, c]
            behind = jnp.where(row == 0, 0.0, pltpu.roll(y, 1, 0))
            force = x + (y - behind) + (z if side == 0 else -z)
            early = v + gain * force
            for tile in range(GX):
                lines = slice(tile * 8, tile * 8 + 8)
                o_ref[tile, pl.ds(plane * 24, 8), :] = v[lines]
                o_ref[tile, pl.ds(plane * 24 + 8, 8), :] = early[lines]
                o_ref[tile, pl.ds(plane * 24 + 16, 8), :] = x[lines]
                o_ref[tile, pl.ds(160 + plane, 1), :] = y_ref[side, c, pl.ds(63, 1), :]
        for tile in range(GX):
            signed = gain[tile * 8 : tile * 8 + 8]
            o_ref[tile, pl.ds(144 + 8 * side, 8), :] = -signed if side == 0 else signed
            o_ref[tile, pl.ds(166 + side, 1), :] = jnp.zeros((1, PEERS), f32)


def lane_index(shape):
    return lax.broadcasted_iota(jnp.int32, shape, len(shape) - 1)


def packed_column(values, column, lane):
    out = jnp.zeros(values[0].shape, f32)
    for k, value in enumerate(values):
        shift = (k - column) % PEERS
        moved = pltpu.roll(value, shift, 1) if shift else value
        out = jnp.where(lane == k, moved, out)
    return out


def zones_kernel(table_ref, zones_ref, x_ref, y_ref, coef_ref, west_ref, south_ref):
    for z in range(4):
        zone = zones_ref[z]
        rows = [jnp.zeros(zone.shape, f32)] * 3
        for index in range(table_ref.shape[1]):
            matched = zone == index
            rows = [jnp.where(matched, table_ref[row, index], rows[row]) for row in range(3)]
        coef_ref[0, z] = rows[0] * time_step
        coef_ref[1, z] = rows[1] * time_step
        coef_ref[2, z] = rows[2]
    lane = lane_index((64, PEERS))
    west_ref[...] = packed_column([x_ref[k // 4, 0, k % 4] for k in range(12)], PEERS - 1, lane)
    for k in range(12):
        south_ref[pl.ds(k, 1), :] = y_ref[k // 4, 0, k % 4, pl.ds(7, 1), :]


def pushed(c, z, lane, row, velocity, stress_ref, west, south_ref, gain):
    k = c * 4 + z
    x, y = stress_ref[c, 0, z], stress_ref[c, 1, z]
    edge = pltpu.roll(west, PEERS - k, 1) if k else west
    behind_x = jnp.where(lane == 0, edge, pltpu.roll(x, 1, 1))
    behind_y = jnp.where(row == 0, south_ref[pl.ds(k, 1), :], pltpu.roll(y, 1, 0))
    force = x - behind_x + y - behind_y
    if z < 3:
        force = force + stress_ref[c, 2, z]
    if z > 0:
        force = force - stress_ref[c, 2, z - 1]
    return velocity + gain * force


def early_kernel(velocity_ref, stress_ref, west_ref, south_ref, coef_ref, mark_ref, early_ref, east_ref, north_ref):
    lane = lane_index((64, PEERS))
    row = lax.broadcasted_iota(jnp.int32, (64, PEERS), 0)
    west = west_ref[...]
    for c in range(3):
        for z in range(4):
            early_ref[c, z] = pushed(
                c, z, lane, row, velocity_ref[c, z], stress_ref, west, south_ref, coef_ref[1, z]
            )
    fields = [early_ref.at[k // 4, k % 4] for k in range(12)] + [coef_ref.at[1, 0], coef_ref.at[1, 3]]
    east_ref[...] = packed_column([field[...] for field in fields], 0, lane)
    for k, field in enumerate(fields):
        north_ref[pl.ds(k, 1), :] = field[pl.ds(0, 1), :]
    north_ref[pl.ds(14, 2), :] = jnp.zeros((2, PEERS), f32)


def feed_kernel(rows_ref, south_ref, feed_ref):
    lane = lane_index((8, PEERS))
    row = lax.broadcasted_iota(jnp.int32, (8, PEERS), 0)
    for tile in range(GX):
        for side in range(2):
            signed = rows_ref[tile, pl.ds(144 + 8 * side, 8), :]
            feed_ref[tile, pl.ds(48 + 8 * side, 8), :] = signed
            gain = -signed if side == 0 else signed
            for c in range(3):
                plane = 3 * side + c
                lines = pl.ds(plane * 24 + 16, 8)
                x, before = rows_ref[tile, lines, :], rows_ref[(tile + GX - 1) % GX, lines, :]
                behind = jnp.where(lane == 0, pltpu.roll(before, 1, 1), pltpu.roll(x, 1, 1))
                south = jnp.where(row == 0, south_ref[tile, pl.ds(plane, 1), :], 0.0)
                early = rows_ref[tile, pl.ds(plane * 24 + 8, 8), :]
                feed_ref[tile, pl.ds(plane * 8, 8), :] = early - gain * (behind + south)


def cells_kernel(rims, early_ref, east_ref, north_ref, d_ref, coef_ref, stress_ref, mask_ref, v_ref, o_ref, *refs):
    lane = lane_index((64, PEERS))
    row = lax.broadcasted_iota(jnp.int32, (64, PEERS), 0)
    for c in range(3):
        for z in range(4):
            v_ref[c, z] = early_ref[c, z]
    for tile in range(GX):
        rows = pl.ds(tile * 8, 8)
        for plane in range(6):
            c, z = plane % 3, 3 * (plane // 3)
            push = coef_ref[1, z, rows, :] * d_ref[tile, pl.ds(plane * 8, 8), :]
            base = early_ref[c, z, rows, :]
            v_ref[c, z, rows, :] = base - push if z == 0 else base + push
    east = east_ref[...]
    edge = jnp.concatenate([d_ref[tile, pl.ds(56, 8), :] for tile in range(GX)], axis=0)
    last = lambda value, k: pltpu.roll(value, PEERS - 1 - k, 1)
    for z in range(4):
        rigidity = coef_ref[0, z]
        cohesion = coef_ref[2, z]
        keep = [mask_ref[d, z].astype(f32) for d in range(3)]
        total = jnp.zeros((64, PEERS), f32)
        trial = []
        for c in range(3):
            k = c * 4 + z
            v = v_ref[c, z]
            past_x, past_y = last(east, k), north_ref[pl.ds(k, 1), :]
            if z in (0, 3):
                plane, gain = c + z, 12 if z == 0 else 13
                push_x = last(east, gain) * last(edge, plane)
                push_y = north_ref[pl.ds(gain, 1), :] * d_ref[GX - 1, pl.ds(48 + plane, 1), :]
                past_x = past_x - push_x if z == 0 else past_x + push_x
                past_y = past_y - push_y if z == 0 else past_y + push_y
            ahead_x = jnp.where(lane == PEERS - 1, past_x, pltpu.roll(v, PEERS - 1, 1))
            ahead_y = jnp.where(row == 63, past_y, pltpu.roll(v, 63, 0))
            tx = keep[0] * (stress_ref[c, 0, z] + rigidity * (ahead_x - v))
            ty = keep[1] * (stress_ref[c, 1, z] + rigidity * (ahead_y - v))
            if z < 3:
                tz = keep[2] * (stress_ref[c, 2, z] + rigidity * (v_ref[c, z + 1] - v))
            else:
                pulled = [d_ref[tile, pl.ds((3 + c) * 8, 8), :] for tile in range(GX)]
                tz = keep[2] * jnp.concatenate(pulled, axis=0)
            trial.append((tx, ty, tz))
            total = total + (tx * tx + ty * ty + tz * tz)
        factor = cohesion / jnp.maximum(jnp.sqrt(total), cohesion)
        for c in range(3):
            for d in range(3):
                o_ref[c, d, z] = trial[c][d] * factor
    if rims:
        west_ref, south_ref = refs
        west_ref[...] = packed_column([o_ref[k // 4, 0, k % 4] for k in range(12)], PEERS - 1, lane)
        for k in range(12):
            south_ref[pl.ds(k, 1), :] = o_ref[k // 4, 1, k % 4, pl.ds(63, 1), :]
        south_ref[pl.ds(12, 4), :] = jnp.zeros((4, PEERS), f32)


def shape(*dims):
    return jax.ShapeDtypeStruct(dims, f32)


WORK = [pltpu.VMEM((PEERS, PEERS), f32), pltpu.VMEM((PEERS, PEERS), f32)]


def near(*dims):
    return pltpu.VMEM(dims, f32)


def room(size):
    return pltpu.CompilerParams(vmem_limit_bytes=size << 20)


def far(*dims):
    return pltpu.HBM(dims, f32)


def held(arrays, space):
    return [pltpu.with_memory_space_constraint(a, space) for a in arrays]


def call(kernel, outs, *args, scratch=(), close=True):
    args = held(args, pltpu.VMEM if close else pltpu.HBM)
    return pl.pallas_call(kernel, out_shape=outs, scratch_shapes=list(scratch), compiler_params=room(8))(*args)


def exchange_all(value):
    tiles = value.shape[0] // PEERS
    blocks = value.reshape(PEERS, 1, tiles * PEERS)
    blocks = lax.all_to_all(blocks, both, split_axis=0, concat_axis=0, tiled=True)
    return blocks.reshape(tiles * PEERS, PEERS)


def exchange_row(value):
    return lax.all_to_all(value, "gx", split_axis=0, concat_axis=0, tiled=True)


def shifted(value, axis, steps):
    count = lax.axis_size(axis)
    return lax.ppermute(value, axis, [(source, (source + steps) % count) for source in range(count)])


def pack(zone_table, velocity, stress, zones):
    whole = pl.BlockSpec(memory_space=pltpu.HBM)
    field = pltpu.VMEM((2, 3, 64, PEERS), f32)
    return pl.pallas_call(
        pack_kernel,
        in_specs=[pl.BlockSpec(memory_space=pltpu.SMEM), whole, whole, whole],
        out_shape=near(GX, 168, PEERS),
        scratch_shapes=[field] * 4 + [pltpu.VMEM((2, 64, PEERS), jnp.int32), pltpu.SemaphoreType.DMA((2, 5))],
        compiler_params=room(16),
        name="pack",
    )(zone_table, *held((velocity, stress, zones), pltpu.HBM))


def zones_of(zone_table, zones, stress):
    whole = lambda *dims: pl.BlockSpec(dims, lambda i: (0,) * len(dims))
    return pl.pallas_call(
        zones_kernel,
        grid=(1,),
        in_specs=[
            pl.BlockSpec(memory_space=pltpu.SMEM),
            whole(4, 64, PEERS),
            pl.BlockSpec((3, 1, 4, 64, PEERS), lambda i: (0, 0, 0, 0, 0)),
            pl.BlockSpec((3, 1, 4, 8, PEERS), lambda i: (0, 1, 0, 7, 0)),
        ],
        out_specs=[whole(3, 4, 64, PEERS), whole(64, PEERS), whole(16, PEERS)],
        out_shape=[far(3, 4, 64, PEERS), far(64, PEERS), far(16, PEERS)],
        compiler_params=room(16),
        name="zones",
    )(zone_table, *held((zones, stress, stress), pltpu.HBM))


def tails_of(history, memory, plane):
    out_spec = pl.BlockSpec((2, 8, 1024), lambda c: (c, 0, 0))
    return pl.pallas_call(
        history_kernel,
        grid=(3,),
        in_specs=[
            pl.BlockSpec((1, 1, 31, 2, 8, 1024), lambda c: (plane, c, 0, 0, 0, 0)),
            pl.BlockSpec((1, 31, 8, 1024), lambda c: (plane, 0, 0, 0)),
        ],
        out_specs=[out_spec, out_spec],
        out_shape=[far(6, 8, 1024)] * 2,
        compiler_params=room(16),
    )(*held((history, memory), pltpu.HBM))


def mark_kernel(x_ref, o_ref):
    o_ref[...] = x_ref[0, 0, pl.ds(0, 8), :]


def steps(velocity, stress, face_mask, zones, zone_table, impedance, memory, history):
    mx, my, twist, ahead = tables()
    impedance = impedance.reshape(6, 8, 1024)
    sending, returning = near(6 * PEERS, PEERS), near(TILES * PEERS, PEERS)
    dma = pltpu.SemaphoreType.DMA
    line = pltpu.VMEM((6, 2, 8, 1024), f32)

    def make_dip(carry, sent, *operands):
        spec = lambda space, count: [pl.BlockSpec(memory_space=space)] * count
        scratch = [square] * 4 + [pltpu.VMEM((6, 8, 1024), f32), line, dma((6, 2))]
        outs, out_specs = returning, spec(pltpu.VMEM, 1)[0]
        if carry:
            scratch += [pltpu.VMEM((2, 8, 1024), f32), line, dma((7, 2))]
            outs = [returning, far(6, 8, 1024), far(6, 8, 1024)]
            out_specs = spec(pltpu.VMEM, 1) + spec(pltpu.HBM, 2)
        return pl.pallas_call(
            functools.partial(dip_kernel, carry),
            in_specs=spec(pltpu.VMEM, 4) + spec(pltpu.HBM, len(operands)),
            out_specs=out_specs,
            out_shape=outs,
            scratch_shapes=scratch,
            compiler_params=room(8),
        )(*held((sent, my, twist, ahead), pltpu.VMEM), *held(operands, pltpu.HBM))

    square = pltpu.VMEM((PEERS, PEERS), f32)

    def make_early(velocity, stress, west, south, mark):
        outs = [far(3, 4, 64, PEERS), far(64, PEERS), far(16, PEERS)]
        return call(early_kernel, outs, velocity, stress, west, south, coef, mark, close=False)

    def make_cells(rims, *operands):
        outs = [shape(3, 4, 64, PEERS), shape(3, 3, 4, 64, PEERS)]
        if rims:
            outs = [far(3, 4, 64, PEERS), far(3, 3, 4, 64, PEERS), far(64, PEERS), far(16, PEERS)]
        return call(functools.partial(cells_kernel, rims), outs, *operands, close=not rims)

    rows = exchange_row(pack(zone_table, velocity, stress, zones))
    coef, west, south = zones_of(zone_table, zones, stress)
    west, south = shifted(west, "gx", 1), shifted(south, "gy", 1)
    now, later = zip(tails_of(history, memory, 0), tails_of(history, memory, 1))
    sent = exchange_all(call(forward_kernel, sending, rows, mx, twist, scratch=WORK))
    onward = [((GX - 1) * GY + h, (h + 1) % GY) for h in range(GY)]
    above = lax.ppermute(rows[:, 160:168], both, onward)
    early, east, north = make_early(velocity, stress, west, south, south)
    east, north = shifted(east, "gx", -1), shifted(north, "gy", -1)
    lines, *later = make_dip(True, sent, impedance, *now, memory, *later)
    lines = exchange_all(lines)
    feed = call(feed_kernel, near(GX, 64, PEERS), rows, above)
    sending1, traction = call(
        turn_kernel,
        [sending, near(GX, 64, PEERS)],
        lines, feed, mx, twist,
        scratch=[square] * 2 + [pltpu.VMEM((GX, 48, PEERS), f32)],
    )
    sent = exchange_all(sending1)
    traction = exchange_row(traction)
    lines = make_dip(False, sent, impedance, *later)
    lines = exchange_all(lines)
    velocity, stress, west, south = make_cells(True, early, east, north, traction, coef, stress, face_mask)
    west, south = shifted(west, "gx", 1), shifted(south, "gy", 1)
    mark = call(mark_kernel, shape(8, PEERS), coef, close=False)
    early, east, north = make_early(velocity, stress, west, south, mark)
    east, north = shifted(east, "gx", -1), shifted(north, "gy", -1)
    traction = call(inverse_kernel, near(GX, 64, PEERS), lines, mx, twist, scratch=[square] * 2)
    traction = exchange_row(traction)
    velocity, stress = make_cells(False, early, east, north, traction, coef, stress, face_mask)
    return (velocity, stress)


def solution(mesh):
    in_specs = (
        P(None, None, "gy", "gx"),
        P(None, None, None, "gy", "gx"),
        P(None, None, "gy", "gx"),
        P(None, "gy", "gx"),
        P(),
        P(None, None, both, None),
        P(None, None, both, None),
        P(None, None, None, None, both, None),
    )
    out_specs = (P(None, None, "gy", "gx"), P(None, None, None, "gy", "gx"))
    return jax.shard_map(steps, mesh=mesh, in_specs=in_specs, out_specs=out_specs, check_vma=False)
```

time: 174 us -> 165 us (0.948)
  the two profiles are of different devices: /device:TPU:2 before, /device:TPU:96 now
where the time goes in v2:
time: 165 us; the launch traced here: 164 us
  blocking collectives  51.2 us (31%)
  waiting for transfers between devices  38.8 us (24%)
  Pallas kernels  35 us (21%)
  starting transfers between devices  34.2 us (21%)
  local copies, waits for them, and re-layouts  4.16 us (3%)
    all_to_all x2, blocking collectives, exchange_all(): lax.all_to_all(blocks, both, split_axis=0, concat_axis=0, tiled=True)  33.2 us
    ppermute x8, waiting for transfers between devices, shifted(): lax.ppermute(value, axis, [(source, (source + steps) % count) for source...  22.6 us
    all_to_all x1, blocking collectives, exchange_row(): return lax.all_to_all(value, 'gx', split_axis=0, concat_axis=0, tiled=True)  18 us
    all_to_all x2, starting transfers between devices, exchange_all(): lax.all_to_all(blocks, both, split_axis=0, concat_axis=0, tiled=True)  17.2 us
    pallas_call x9, Pallas kernels, call(): pl.pallas_call(kernel, out_shape=outs, scratch_shapes=list(scratch), comp...  14.9 us
    all_to_all x2, starting transfers between devices, exchange_row(): return lax.all_to_all(value, 'gx', split_axis=0, concat_axis=0, tiled=True)  11.4 us
    all_to_all x2, waiting for transfers between devices, exchange_all(): lax.all_to_all(blocks, both, split_axis=0, concat_axis=0, tiled=True)  10.5 us
    pallas_call x2, Pallas kernels, tails_of(): pl.pallas_call(history_kernel, grid=(3,), in_specs=[pl.BlockSpec((1, 1, 3...  9.83 us
  transfers between devices with their start and end apart: 13, of which 9 were waited for; matrix products, arithmetic and copies ran while one was open for 0% of the time, Pallas kernels for 14%

profile of v2, /device:TPU:96, one launch (start us, length us, event | category | flops | bytes accessed | tf_op | source)
XLA Modules:
  0.0 164.2 jit_solution(607683553894472869)
XLA Ops:
  0.6 0.0 copy-start.9
  0.6 0.7 copy-done.9
  1.3 2.0 %pack.1 = f32[8,168,128]{2,1,0:T(8,128)S(1)} custom-call(f32[3,8]{1,0:T(4,128)S(1)} %copy-done.9, f32[3,4,64,128]{3,2,1,0:T(8,128)} %velocity_ref.3, f32[3,3,4,64,128]{4,3,2,1,0:T(8,128)} %stress_ref.5, s32[4,64,128]{2,1,0:T(8,128)} %zones_ref.3), custom_call_target="tpu_custom_call" | custom-call | tf_op jit(solution)/shard_map/pack/pallas_call | solution.py:496
  3.3 0.0 copy-start.2
  3.3 0.0 copy-start.3
  3.3 18.0 %all_to_all.35.x_ref.rows_ref = f32[8,168,128]{2,1,0:T(8,128)S(1)} all-to-all(f32[8,168,128]{2,1,0:T(8,128)S(1)} %pack.1), channel_id=1, replica_groups=mesh['gx'=8,'gy'=16] {'gx'}, dimensions={0} | all-to-all | bytes 1376256 | tf_op jit(solution)/shard_map/all_to_all | solution.py:485
  21.4 1.2 shard_map.150
  22.6 7.8 %all-to-all-start.1 = ((f32[128,1,768]{2,1,0:T(1,128)}), f32[128,1,768]{2,1,0:T(1,128)S(1)}, u32[]{:S(2)}, u32[]{:S(2)}) async-start(f32[128,1,768]{2,1,0:T(1,128)} %bitcast), calls=%async_computation.1 | async-start | bytes 786432 | tf_op jit(solution)/shard_map/all_to_all | solution.py:480
  30.4 4.9 %shard_map.152 = (f32[6,8,1024]{2,1,0:T(8,128)}, f32[6,8,1024]{2,1,0:T(8,128)}) custom-call(f32[2,3,31,2,8,1024]{5,4,3,2,1,0:T(8,128)} %history_ref.3, f32[2,31,8,1024]{3,2,1,0:T(8,128)} %refs_2_.1), custom_call_target="tpu_custom_call" | custom-call | tf_op jit(solution)/shard_map/pallas_call | solution.py:526
  35.3 4.9 %shard_map.151 = (f32[6,8,1024]{2,1,0:T(8,128)}, f32[6,8,1024]{2,1,0:T(8,128)}) custom-call(f32[2,3,31,2,8,1024]{5,4,3,2,1,0:T(8,128)} %history_ref.3, f32[2,31,8,1024]{3,2,1,0:T(8,128)} %refs_2_.1), custom_call_target="tpu_custom_call" | custom-call | tf_op jit(solution)/shard_map/pallas_call | solution.py:526
  40.3 0.4 all-to-all-done.1
  40.7 4.0 %shard_map.153 = (f32[896,128]{1,0:T(8,128)}, f32[6,8,1024]{2,1,0:T(8,128)}, f32[6,8,1024]{2,1,0:T(8,128)}) custom-call(f32[768,128]{1,0:T(8,128)S(1)} %bitcast.12, bf16[2,256,256]{2,1,0:T(8,128)(2,1)S(1)} %copy-done.5, f32[2,8,8,128]{3,2,1,0:T(8,128)S(1)} %copy-done.3, f32[2,8,128]{2,1,0:T(8,128)S(1)} %copy-done.7, f32[6,8,1024]{2,1,0:T(8,128)} %bitcast.15, ...), custom_call_target="tpu_custom_call" | custom-call | tf_op jit(solution)/shard_map/pallas_call | solution.py:558
  44.7 9.4 %all-to-all-start.2 = ((f32[128,1,896]{2,1,0:T(1,128)}), f32[128,1,896]{2,1,0:T(1,128)S(1)}, u32[]{:S(2)}, u32[]{:S(2)}) async-start(f32[128,1,896]{2,1,0:T(1,128)} %bitcast.3), calls=%async_computation.2 | async-start | bytes 917504 | tf_op jit(solution)/shard_map/all_to_all | solution.py:480
  54.0 0.7 collective-permute-start.4
  54.7 0.2 shard_map.154.early_ref
  54.9 10.1 %all-to-all-done.2 = f32[128,1,896]{2,1,0:T(1,128)S(1)} async-done(((f32[128,1,896]{2,1,0:T(1,128)}), f32[128,1,896]{2,1,0:T(1,128)S(1)}, u32[]{:S(2)}, u32[]{:S(2)}) %all-to-all-start.2) | async-done | bytes 458784 | tf_op jit(solution)/shard_map/all_to_all | solution.py:480
  64.9 1.2 shard_map.155
  66.2 16.3 %all_to_all.36 = f32[128,1,768]{2,1,0:T(1,128)S(1)} all-to-all(f32[128,1,768]{2,1,0:T(1,128)S(1)} %bitcast.14), channel_id=1, replica_groups=mesh['gx'=8,'gy'=16] {'gx','gy'}, dimensions={0} | all-to-all | bytes 786432 | tf_op jit(solution)/shard_map/all_to_all | solution.py:480
  82.5 2.3 %shard_map.159 = f32[896,128]{1,0:T(8,128)S(1)} custom-call(f32[768,128]{1,0:T(8,128)S(1)} %bitcast.13, bf16[2,256,256]{2,1,0:T(8,128)(2,1)S(1)} %copy-done.5, f32[2,8,8,128]{3,2,1,0:T(8,128)S(1)} %copy-done.3, f32[2,8,128]{2,1,0:T(8,128)S(1)} %copy-done.7, f32[6,8,1024]{2,1,0:T(8,128)} %bitcast.16, f32[6,8,1024]{2,1,0:T(8,128)} %get-tuple-element.44.refs_0_, ...), custom_call_target="tpu_custom_call" | custom-call | tf_op jit(solution)/shard_map/pallas_call | solution.py:558
  84.8 16.9 %all_to_all.37 = f32[128,1,896]{2,1,0:T(1,128)S(1)} all-to-all(f32[128,1,896]{2,1,0:T(1,128)S(1)} %bitcast.11), channel_id=1, replica_groups=mesh['gx'=8,'gy'=16] {'gx','gy'}, dimensions={0} | all-to-all | bytes 917504 | tf_op jit(solution)/shard_map/all_to_all | solution.py:480
  101.8 5.7 %all-to-all-start.3 = ((f32[8,64,128]{2,1,0:T(8,128)}), f32[8,64,128]{2,1,0:T(8,128)S(1)}, u32[]{:S(2)}, u32[]{:S(2)}) async-start(f32[8,64,128]{2,1,0:T(8,128)} %get-tuple-element.35), calls=%async_computation.3 | async-start | bytes 524288 | tf_op jit(solution)/shard_map/all_to_all | solution.py:485
  107.4 1.2 shard_map.160
  108.7 5.7 %all-to-all-done.3.d_ref = f32[8,64,128]{2,1,0:T(8,128)S(1)} async-done(((f32[8,64,128]{2,1,0:T(8,128)}), f32[8,64,128]{2,1,0:T(8,128)S(1)}, u32[]{:S(2)}, u32[]{:S(2)}) %all-to-all-start.3) | async-done | bytes 262176 | tf_op jit(solution)/shard_map/all_to_all | solution.py:485
  114.3 5.7 %all-to-all-start.6 = ((f32[8,64,128]{2,1,0:T(8,128)}), f32[8,64,128]{2,1,0:T(8,128)S(1)}, u32[]{:S(2)}, u32[]{:S(2)}) async-start(f32[8,64,128]{2,1,0:T(8,128)} %shard_map.160), calls=%async_computation.6 | async-start | bytes 524288 | tf_op jit(solution)/shard_map/all_to_all | solution.py:485
  120.0 2.1 %zones.1 = (f32[3,4,64,128]{3,2,1,0:T(8,128)}, f32[64,128]{1,0:T(8,128)}, f32[16,128]{1,0:T(8,128)}) custom-call(f32[3,8]{1,0:T(4,128)S(1)} %copy-done.10, s32[4,64,128]{2,1,0:T(8,128)} %zones_ref.3, f32[3,3,4,64,128]{4,3,2,1,0:T(8,128)} %stress_ref.5, f32[3,3,4,64,128]{4,3,2,1,0:T(8,128)} %stress_ref.5), custom_call_target="tpu_custom_call" | custom-call | tf_op jit(solution)/shard_map/zones/pallas_call | solution.py:508
  122.1 3.0 %collective-permute-start = (f32[64,128]{1,0:T(8,128)}, f32[64,128]{1,0:T(8,128)S(1)}, u32[]{:S(2)}, u32[]{:S(2)}) collective-permute-start(f32[64,128]{1,0:T(8,128)} %get-tuple-element.24), channel_id=1, source_target_pairs={{0,16},{16,32},{32,48},{48,64},{64,80},{80,96},{96,112},{112,0},{1... | collective-permute-start | bytes 98312 | tf_op jit(solution)/shard_map/ppermute | solution.py:490
  125.1 5.4 %collective-permute-done.1.south_ref.mark_ref = f32[16,128]{1,0:T(8,128)S(1)} collective-permute-done((f32[16,128]{1,0:T(8,128)}, f32[16,128]{1,0:T(8,128)S(1)}, u32[]{:S(2)}, u32[]{:S(2)}) %collective-permute-start.1) | collective-permute-done | bytes 8224 | tf_op jit(solution)/shard_map/ppermute | solution.py:490
  130.5 0.6 copy-done.14
  131.1 0.0 copy-done.13
  131.1 2.6 %shard_map.149 = (f32[3,4,64,128]{3,2,1,0:T(8,128)}, f32[64,128]{1,0:T(8,128)}, f32[16,128]{1,0:T(8,128)}) custom-call(f32[3,4,64,128]{3,2,1,0:T(8,128)} %velocity_ref.3, f32[3,3,4,64,128]{4,3,2,1,0:T(8,128)} %stress_ref.5, f32[64,128]{1,0:T(8,128)} %copy-done.13, f32[16,128]{1,0:T(8,128)} %copy-done.14, f32[3,4,64,128]{3,2,1,0:T(8,128)} %get-tuple-element.26.coef_ref.x_ref, ...), custom_call_target="tpu_custom_call" | custom-call | tf_op jit(solution)/shard_map/pallas_call | solution.py:474
  133.7 1.6 collective-permute-done.3.north_ref
  135.2 6.2 %collective-permute-done.2.east_ref = f32[64,128]{1,0:T(8,128)S(1)} collective-permute-done((f32[64,128]{1,0:T(8,128)}, f32[64,128]{1,0:T(8,128)S(1)}, u32[]{:S(2)}, u32[]{:S(2)}) %collective-permute-start.2) | collective-permute-done | bytes 32800 | tf_op jit(solution)/shard_map/ppermute | solution.py:490
  141.4 0.6 copy-done.15
  142.0 3.2 %shard_map.156 = (f32[3,4,64,128]{3,2,1,0:T(8,128)}, f32[3,3,4,64,128]{4,3,2,1,0:T(8,128)}, f32[64,128]{1,0:T(8,128)}, f32[16,128]{1,0:T(8,128)}) custom-call(f32[3,4,64,128]{3,2,1,0:T(8,128)} %get-tuple-element.27.early_ref, f32[64,128]{1,0:T(8,128)} %copy-done.15, f32[16,128]{1,0:T(8,128)} %copy-done.16, f32[8,64,128]{2,1,0:T(8,128)} %copy-done.11, ...), custom_call_target="tpu_custom_call" | custom-call | tf_op jit(solution)/shard_map/pallas_call | solution.py:474
  145.2 0.0 copy-start.1
  145.2 0.0 copy-start.4
  145.3 0.1 collective-permute-start.6
  145.3 1.1 shard_map.157.mark_ref
  146.5 0.6 copy-done.8
  147.0 3.7 %collective-permute-done.6.south_ref = f32[16,128]{1,0:T(8,128)S(1)} collective-permute-done((f32[16,128]{1,0:T(8,128)}, f32[16,128]{1,0:T(8,128)S(1)}, u32[]{:S(2)}, u32[]{:S(2)}) %collective-permute-start.6) | collective-permute-done | bytes 8224 | tf_op jit(solution)/shard_map/ppermute | solution.py:490
  150.7 0.6 copy-done.17
  151.3 0.0 copy-done.12
  151.3 2.6 %shard_map.158 = (f32[3,4,64,128]{3,2,1,0:T(8,128)}, f32[64,128]{1,0:T(8,128)}, f32[16,128]{1,0:T(8,128)}) custom-call(f32[3,4,64,128]{3,2,1,0:T(8,128)} %get-tuple-element.36.velocity_ref, f32[3,3,4,64,128]{4,3,2,1,0:T(8,128)} %get-tuple-element.37.stress_ref, f32[64,128]{1,0:T(8,128)} %copy-done.12, f32[16,128]{1,0:T(8,128)} %copy-done.17, ...), custom_call_target="tpu_custom_call" | custom-call | tf_op jit(solution)/shard_map/pallas_call | solution.py:474
  153.9 1.9 %collective-permute-start.7 = (f32[64,128]{1,0:T(8,128)}, f32[64,128]{1,0:T(8,128)S(1)}, u32[]{:S(2)}, u32[]{:S(2)}) collective-permute-start(f32[64,128]{1,0:T(8,128)} %get-tuple-element.41), channel_id=1, source_target_pairs={{0,112},{16,0},{32,16},{48,32},{64,48},{80,64},{96,80},{112,96},{1... | collective-permute-start | bytes 98312 | tf_op jit(solution)/shard_map/ppermute | solution.py:490
  155.9 1.6 collective-permute-done.8.north_ref
  157.4 4.2 %collective-permute-done.7.east_ref = f32[64,128]{1,0:T(8,128)S(1)} collective-permute-done((f32[64,128]{1,0:T(8,128)}, f32[64,128]{1,0:T(8,128)S(1)}, u32[]{:S(2)}, u32[]{:S(2)}) %collective-permute-start.7) | collective-permute-done | bytes 32800 | tf_op jit(solution)/shard_map/ppermute | solution.py:490
  161.7 1.0 copy-done.6
  162.7 1.5 shard_map.161
  (33 shorter events, 0.1 us)
Async XLA Ops:
  0.6 0.7 copy-start.9
  3.3 18.1 %copy-start.2 = (bf16[2,256,256]{2,1,0:T(8,128)(2,1)S(1)}, bf16[2,256,256]{2,1,0:T(8,128)(2,1)}, u32[]{:S(2)}) copy-start(bf16[2,256,256]{2,1,0:T(8,128)(2,1)} %constant.21.mx_ref) | copy-start | bytes 786436
  3.3 18.0 %copy-start.3 = (f32[2,8,8,128]{3,2,1,0:T(8,128)S(1)}, f32[2,8,8,128]{3,2,1,0:T(8,128)}, u32[]{:S(2)}) copy-start(f32[2,8,8,128]{3,2,1,0:T(8,128)} %constant.10.clone.twist_ref) | copy-start | bytes 196612
  22.6 18.1 %all-to-all-start.1 = ((f32[128,1,768]{2,1,0:T(1,128)}), f32[128,1,768]{2,1,0:T(1,128)S(1)}, u32[]{:S(2)}, u32[]{:S(2)}) async-start(f32[128,1,768]{2,1,0:T(1,128)} %bitcast), calls=%async_computation.1 | async-start | bytes 786432 | tf_op jit(solution)/shard_map/all_to_all | solution.py:480
  35.3 5.4 %copy-start.5 = (bf16[2,256,256]{2,1,0:T(8,128)(2,1)S(1)}, bf16[2,256,256]{2,1,0:T(8,128)(2,1)}, u32[]{:S(2)}) copy-start(bf16[2,256,256]{2,1,0:T(8,128)(2,1)} %constant.28.my_ref) | copy-start | bytes 786436
  35.3 5.4 %copy-start.7 = (f32[2,8,128]{2,1,0:T(8,128)S(1)}, f32[2,8,128]{2,1,0:T(8,128)}, u32[]{:S(2)}) copy-start(f32[2,8,128]{2,1,0:T(8,128)} %constant.11.clone.ahead_ref) | copy-start | bytes 24580
  44.7 20.3 %all-to-all-start.2 = ((f32[128,1,896]{2,1,0:T(1,128)}), f32[128,1,896]{2,1,0:T(1,128)S(1)}, u32[]{:S(2)}, u32[]{:S(2)}) async-start(f32[128,1,896]{2,1,0:T(1,128)} %bitcast.3), calls=%async_computation.2 | async-start | bytes 917504 | tf_op jit(solution)/shard_map/all_to_all | solution.py:480
  54.0 0.7 collective-permute-start.4
  101.8 18.3 %copy-start.10 = (f32[3,8]{1,0:T(4,128)S(1)}, f32[3,8]{1,0:T(4,128)}, u32[]{:S(2)}) copy-start(f32[3,8]{1,0:T(4,128)} %table_ref.3) | copy-start | bytes 292
  101.8 12.6 %all-to-all-start.3 = ((f32[8,64,128]{2,1,0:T(8,128)}), f32[8,64,128]{2,1,0:T(8,128)S(1)}, u32[]{:S(2)}, u32[]{:S(2)}) async-start(f32[8,64,128]{2,1,0:T(8,128)} %get-tuple-element.35), calls=%async_computation.3 | async-start | bytes 524288 | tf_op jit(solution)/shard_map/all_to_all | solution.py:485
  114.3 7.8 %copy-start.11 = (f32[8,64,128]{2,1,0:T(8,128)}, f32[8,64,128]{2,1,0:T(8,128)S(1)}, u32[]{:S(2)}) copy-start(f32[8,64,128]{2,1,0:T(8,128)S(1)} %all-to-all-done.3.d_ref) | copy-start | bytes 786436
  114.3 47.4 %all-to-all-start.6 = ((f32[8,64,128]{2,1,0:T(8,128)}), f32[8,64,128]{2,1,0:T(8,128)S(1)}, u32[]{:S(2)}, u32[]{:S(2)}) async-start(f32[8,64,128]{2,1,0:T(8,128)} %shard_map.160), calls=%async_computation.6 | async-start | bytes 524288 | tf_op jit(solution)/shard_map/all_to_all | solution.py:485
  122.1 8.4 %collective-permute-start = (f32[64,128]{1,0:T(8,128)}, f32[64,128]{1,0:T(8,128)S(1)}, u32[]{:S(2)}, u32[]{:S(2)}) collective-permute-start(f32[64,128]{1,0:T(8,128)} %get-tuple-element.24), channel_id=1, source_target_pairs={{0,16},{16,32},{32,48},{48,64},{64,80},{80,96},{96,112},{112,0},{1... | collective-permute-start | bytes 98312 | tf_op jit(solution)/shard_map/ppermute | solution.py:490
  125.1 5.4 %collective-permute-start.1 = (f32[16,128]{1,0:T(8,128)}, f32[16,128]{1,0:T(8,128)S(1)}, u32[]{:S(2)}, u32[]{:S(2)}) collective-permute-start(f32[16,128]{1,0:T(8,128)} %get-tuple-element.25), channel_id=1, source_target_pairs={{0,1},{1,2},{2,3},{3,4},{4,5},{5,6},{6,7},{7,8},{8,9},{9,10},{10,1... | collective-permute-start | bytes 24584 | tf_op jit(solution)/shard_map/ppermute | solution.py:490
  130.5 0.6 copy-start.14
  130.5 0.6 copy-start.13
  133.7 7.7 %collective-permute-start.2 = (f32[64,128]{1,0:T(8,128)}, f32[64,128]{1,0:T(8,128)S(1)}, u32[]{:S(2)}, u32[]{:S(2)}) collective-permute-start(f32[64,128]{1,0:T(8,128)} %get-tuple-element.28), channel_id=1, source_target_pairs={{0,112},{16,0},{32,16},{48,32},{64,48},{80,64},{96,80},{112,96},{1... | collective-permute-start | bytes 98312 | tf_op jit(solution)/shard_map/ppermute | solution.py:490
  133.7 1.6 collective-permute-start.3
  135.2 6.2 %copy-start.16 = (f32[16,128]{1,0:T(8,128)}, f32[16,128]{1,0:T(8,128)S(1)}, u32[]{:S(2)}) copy-start(f32[16,128]{1,0:T(8,128)S(1)} %collective-permute-done.3.north_ref) | copy-start | bytes 24580
  141.4 0.6 copy-start.15
  145.2 5.5 %collective-permute-start.5 = (f32[64,128]{1,0:T(8,128)}, f32[64,128]{1,0:T(8,128)S(1)}, u32[]{:S(2)}, u32[]{:S(2)}) collective-permute-start(f32[64,128]{1,0:T(8,128)} %get-tuple-element.38), channel_id=1, source_target_pairs={{0,16},{16,32},{32,48},{48,64},{64,80},{80,96},{96,112},{112,0},{1... | collective-permute-start | bytes 98312 | tf_op jit(solution)/shard_map/ppermute | solution.py:490
  145.2 16.5 %copy-start = (f32[3,4,64,128]{3,2,1,0:T(8,128)S(1)}, f32[3,4,64,128]{3,2,1,0:T(8,128)}, u32[]{:S(2)}) copy-start(f32[3,4,64,128]{3,2,1,0:T(8,128)} %get-tuple-element.26.coef_ref.x_ref) | copy-start | bytes 1179652
  145.2 16.4 %copy-start.1 = (f32[3,3,4,64,128]{4,3,2,1,0:T(8,128)S(1)}, f32[3,3,4,64,128]{4,3,2,1,0:T(8,128)}, u32[]{:S(2)}) copy-start(f32[3,3,4,64,128]{4,3,2,1,0:T(8,128)} %get-tuple-element.37.stress_ref) | copy-start | bytes 3538948
  145.2 16.4 %copy-start.4 = (s32[3,4,64,128]{3,2,1,0:T(8,128)S(1)}, s32[3,4,64,128]{3,2,1,0:T(8,128)}, u32[]{:S(2)}) copy-start(s32[3,4,64,128]{3,2,1,0:T(8,128)} %mask_ref.3) | copy-start | bytes 1179652
  145.3 5.5 %collective-permute-start.6 = (f32[16,128]{1,0:T(8,128)}, f32[16,128]{1,0:T(8,128)S(1)}, u32[]{:S(2)}, u32[]{:S(2)}) collective-permute-start(f32[16,128]{1,0:T(8,128)} %get-tuple-element.39), channel_id=1, source_target_pairs={{0,1},{1,2},{2,3},{3,4},{4,5},{5,6},{6,7},{7,8},{8,9},{9,10},{10,1... | collective-permute-start | bytes 24584 | tf_op jit(solution)/shard_map/ppermute | solution.py:490
  146.5 0.6 copy-start.8
  150.7 0.6 copy-start.17
  150.7 0.6 copy-start.12
  153.9 7.7 %collective-permute-start.7 = (f32[64,128]{1,0:T(8,128)}, f32[64,128]{1,0:T(8,128)S(1)}, u32[]{:S(2)}, u32[]{:S(2)}) collective-permute-start(f32[64,128]{1,0:T(8,128)} %get-tuple-element.41), channel_id=1, source_target_pairs={{0,112},{16,0},{32,16},{48,32},{64,48},{80,64},{96,80},{112,96},{1... | collective-permute-start | bytes 98312 | tf_op jit(solution)/shard_map/ppermute | solution.py:490
  155.9 1.6 collective-permute-start.8
  161.7 1.0 copy-start.6

commit v3 on v2

--- a/solution.py
+++ b/solution.py
@@ -161,18 +161,13 @@
 
 def forward_kernel(x_ref, mx_ref, twist_ref, o_ref, re_ref, im_ref):
     matrix = (mx_ref[0], mx_ref[1])
-    take = lambda plane, tile: x_ref[tile, pl.ds(plane * 24, 8), :]
+    take = lambda plane, tile: x_ref[tile, pl.ds(plane * 16, 8), :]
     strike_forward(take, twist_ref, matrix, o_ref, re_ref, im_ref)
 
 
 def dip_kernel(carry, x_ref, my_ref, twist_ref, ahead_ref, impedance_ref, *refs):
-    if carry:
-        now, (memory_ref, *later) = refs[:2], refs[2:5]
-        o_ref, *next_refs = refs[5:8]
-        re_ref, im_ref, re2_ref, im2_ref, z_ref, tail_ref, sems, first_ref, later_ref, more_sems = refs[8:]
-    else:
-        now = refs[:2]
-        o_ref, re_ref, im_ref, re2_ref, im2_ref, z_ref, tail_ref, sems = refs[2:]
+    now, o_ref, spectrum_ref = refs[:2], refs[2], refs[3]
+    re_ref, im_ref, re2_ref, im2_ref, z_ref, tail_ref, sems = refs[3 + carry :]
 
     def copies(pair):
         jobs = []
@@ -180,17 +175,12 @@
             side, part = plane // 3, pl.ds(2 * (plane % 3), 2)
             jobs.append((impedance_ref.at[plane], z_ref.at[plane], sems.at[plane, 0]))
             jobs.append((now[side].at[part], tail_ref.at[plane], sems.at[plane, 1]))
-            if carry:
-                jobs.append((later[side].at[part], later_ref.at[plane], more_sems.at[plane, 0]))
-        if carry and pair == 0:
-            jobs.append((memory_ref.at[:, 0], first_ref, more_sems.at[6, 0]))
         return [pltpu.make_async_copy(*job) for job in jobs]
 
     arriving = [copies(pair) for pair in range(3)]
     for group in arriving:
         for copy in group:
             copy.start()
-    leaving = []
     matrix = (my_ref[0], my_ref[1])
     re2_ref[...] = jnp.zeros((PEERS, PEERS), f32)
     im2_ref[...] = jnp.zeros((PEERS, PEERS), f32)
@@ -201,7 +191,6 @@
             copy.wait()
         for member in range(2):
             plane = 2 * pair + member
-            side, part = plane // 3, 2 * (plane % 3)
             values = []
             for j in range(8):
                 rows = pl.ds(member * 64 + j, 8, stride=8)
@@ -214,13 +203,8 @@
                 re, im = spectrum[tile]
                 response.append((tail_ref[plane, 0, :, lanes] - z * re, tail_ref[plane, 1, :, lanes] - z * im))
                 if carry:
-                    first = first_ref[side, :, lanes]
-                    later_ref[plane, 0, :, lanes] = later_ref[plane, 0, :, lanes] + first * re
-                    later_ref[plane, 1, :, lanes] = later_ref[plane, 1, :, lanes] + first * im
-            if carry:
-                target = next_refs[side].at[pl.ds(part, 2)]
-                leaving.append(pltpu.make_async_copy(later_ref.at[plane], target, more_sems.at[plane, 1]))
-                leaving[-1].start()
+                    spectrum_ref[2 * plane, :, lanes] = re
+                    spectrum_ref[2 * plane + 1, :, lanes] = im
             lines = eight(response, 1.0)
             for j in range(8):
                 re, im = twisted(lines[j], twist_ref, j, 1)
@@ -236,8 +220,15 @@
         to_peers(o_ref, pair, matrix, re_ref, im_ref, TILES)
     t = split(jnp.concatenate([re2_ref[...], im2_ref[...]], axis=1))
     o_ref[pl.ds(6, PEERS, stride=TILES), :] = product((matrix[0][:PEERS], matrix[1][:PEERS]), t, ((1,), (1,)))
-    for copy in leaving:
-        copy.wait()
+
+
+def carry_kernel(spectrum_ref, memory_ref, *refs):
+    for plane in range(6):
+        side = plane // 3
+        for part in range(2):
+            row = 2 * (plane % 3) + part
+            value = memory_ref[side, 0] * spectrum_ref[2 * plane + part]
+            refs[2 + side][row] = refs[side][row] + value
 
 
 def turn_kernel(x_ref, early_ref, mx_ref, twist_ref, o_ref, d_ref, re_ref, im_ref, plane_ref):
@@ -290,6 +281,8 @@
     for copy in copies:
         copy.wait()
     row = lax.broadcasted_iota(jnp.int32, (64, PEERS), 0)
+    lane = lane_index((64, PEERS))
+    edge = packed_column([x_ref[plane // 3, plane % 3] for plane in range(6)], PEERS - 1, lane)
     for side in range(2):
         zone = zone_ref[side]
         gain = jnp.zeros(zone.shape, f32)
@@ -299,19 +292,21 @@
         for c in range(3):
             plane = 3 * side + c
             v, x, y, z = v_ref[side, c], x_ref[side, c], y_ref[side, c], z_ref[side, c]
-            behind = jnp.where(row == 0, 0.0, pltpu.roll(y, 1, 0))
-            force = x + (y - behind) + (z if side == 0 else -z)
+            behind_x = jnp.where(lane == 0, 0.0, pltpu.roll(x, 1, 1))
+            behind_y = jnp.where(row == 0, 0.0, pltpu.roll(y, 1, 0))
+            force = (x - behind_x) + (y - behind_y) + (z if side == 0 else -z)
             early = v + gain * force
             for tile in range(GX):
                 lines = slice(tile * 8, tile * 8 + 8)
-                o_ref[tile, pl.ds(plane * 24, 8), :] = v[lines]
-                o_ref[tile, pl.ds(plane * 24 + 8, 8), :] = early[lines]
-                o_ref[tile, pl.ds(plane * 24 + 16, 8), :] = x[lines]
-                o_ref[tile, pl.ds(160 + plane, 1), :] = y_ref[side, c, pl.ds(63, 1), :]
+                o_ref[tile, pl.ds(plane * 16, 8), :] = v[lines]
+                o_ref[tile, pl.ds(plane * 16 + 8, 8), :] = early[lines]
+                o_ref[tile, pl.ds(120 + plane, 1), :] = y_ref[side, c, pl.ds(63, 1), :]
         for tile in range(GX):
-            signed = gain[tile * 8 : tile * 8 + 8]
-            o_ref[tile, pl.ds(144 + 8 * side, 8), :] = -signed if side == 0 else signed
-            o_ref[tile, pl.ds(166 + side, 1), :] = jnp.zeros((1, PEERS), f32)
+            lines = slice(tile * 8, tile * 8 + 8)
+            o_ref[tile, pl.ds(96 + 8 * side, 8), :] = -gain[lines] if side == 0 else gain[lines]
+            o_ref[tile, pl.ds(126 + side, 1), :] = jnp.zeros((1, PEERS), f32)
+            if side == 0:
+                o_ref[tile, pl.ds(112, 8), :] = edge[lines]
 
 
 def lane_index(shape):
@@ -357,7 +352,7 @@
     return velocity + gain * force
 
 
-def early_kernel(velocity_ref, stress_ref, west_ref, south_ref, coef_ref, mark_ref, early_ref, east_ref, north_ref):
+def early_kernel(velocity_ref, stress_ref, west_ref, south_ref, coef_ref, early_ref, east_ref, north_ref):
     lane = lane_index((64, PEERS))
     row = lax.broadcasted_iota(jnp.int32, (64, PEERS), 0)
     west = west_ref[...]
@@ -377,17 +372,17 @@
     lane = lane_index((8, PEERS))
     row = lax.broadcasted_iota(jnp.int32, (8, PEERS), 0)
     for tile in range(GX):
+        edge = rows_ref[(tile + GX - 1) % GX, pl.ds(112, 8), :]
         for side in range(2):
-            signed = rows_ref[tile, pl.ds(144 + 8 * side, 8), :]
+            signed = rows_ref[tile, pl.ds(96 + 8 * side, 8), :]
             feed_ref[tile, pl.ds(48 + 8 * side, 8), :] = signed
             gain = -signed if side == 0 else signed
             for c in range(3):
                 plane = 3 * side + c
-                lines = pl.ds(plane * 24 + 16, 8)
-                x, before = rows_ref[tile, lines, :], rows_ref[(tile + GX - 1) % GX, lines, :]
-                behind = jnp.where(lane == 0, pltpu.roll(before, 1, 1), pltpu.roll(x, 1, 1))
+                west = pltpu.roll(edge, PEERS - plane, 1) if plane else edge
+                behind = jnp.where(lane == 0, west, 0.0)
                 south = jnp.where(row == 0, south_ref[tile, pl.ds(plane, 1), :], 0.0)
-                early = rows_ref[tile, pl.ds(plane * 24 + 8, 8), :]
+                early = rows_ref[tile, pl.ds(plane * 16 + 8, 8), :]
                 feed_ref[tile, pl.ds(plane * 8, 8), :] = early - gain * (behind + south)
 
 
@@ -470,7 +465,8 @@
 
 
 def call(kernel, outs, *args, scratch=(), close=True):
-    args = held(args, pltpu.VMEM if close else pltpu.HBM)
+    if close:
+        args = held(args, pltpu.VMEM)
     return pl.pallas_call(kernel, out_shape=outs, scratch_shapes=list(scratch), compiler_params=room(8))(*args)
 
 
@@ -496,11 +492,11 @@
     return pl.pallas_call(
         pack_kernel,
         in_specs=[pl.BlockSpec(memory_space=pltpu.SMEM), whole, whole, whole],
-        out_shape=near(GX, 168, PEERS),
+        out_shape=near(GX, PEERS, PEERS),
         scratch_shapes=[field] * 4 + [pltpu.VMEM((2, 64, PEERS), jnp.int32), pltpu.SemaphoreType.DMA((2, 5))],
         compiler_params=room(16),
         name="pack",
-    )(zone_table, *held((velocity, stress, zones), pltpu.HBM))
+    )(*held((zone_table, velocity, stress, zones), pltpu.HBM))
 
 
 def zones_of(zone_table, zones, stress):
@@ -518,7 +514,7 @@
         out_shape=[far(3, 4, 64, PEERS), far(64, PEERS), far(16, PEERS)],
         compiler_params=room(16),
         name="zones",
-    )(zone_table, *held((zones, stress, stress), pltpu.HBM))
+    )(*held((zone_table, zones, stress, stress), pltpu.HBM))
 
 
 def tails_of(history, memory, plane):
@@ -536,44 +532,50 @@
     )(*held((history, memory), pltpu.HBM))
 
 
-def mark_kernel(x_ref, o_ref):
-    o_ref[...] = x_ref[0, 0, pl.ds(0, 8), :]
-
-
 def steps(velocity, stress, face_mask, zones, zone_table, impedance, memory, history):
     mx, my, twist, ahead = tables()
     impedance = impedance.reshape(6, 8, 1024)
     sending, returning = near(6 * PEERS, PEERS), near(TILES * PEERS, PEERS)
     dma = pltpu.SemaphoreType.DMA
-    line = pltpu.VMEM((6, 2, 8, 1024), f32)
+    square = pltpu.VMEM((PEERS, PEERS), f32)
 
     def make_dip(carry, sent, *operands):
         spec = lambda space, count: [pl.BlockSpec(memory_space=space)] * count
-        scratch = [square] * 4 + [pltpu.VMEM((6, 8, 1024), f32), line, dma((6, 2))]
-        outs, out_specs = returning, spec(pltpu.VMEM, 1)[0]
-        if carry:
-            scratch += [pltpu.VMEM((2, 8, 1024), f32), line, dma((7, 2))]
-            outs = [returning, far(6, 8, 1024), far(6, 8, 1024)]
-            out_specs = spec(pltpu.VMEM, 1) + spec(pltpu.HBM, 2)
+        pairs = pltpu.VMEM((6, 2, 8, 1024), f32)
+        outs = [returning] + [near(12, 8, 1024)] * carry
         return pl.pallas_call(
             functools.partial(dip_kernel, carry),
             in_specs=spec(pltpu.VMEM, 4) + spec(pltpu.HBM, len(operands)),
-            out_specs=out_specs,
+            out_specs=spec(pltpu.VMEM, len(outs)),
             out_shape=outs,
-            scratch_shapes=scratch,
+            scratch_shapes=[square] * 4 + [pltpu.VMEM((6, 8, 1024), f32), pairs, dma((6, 2))],
             compiler_params=room(8),
         )(*held((sent, my, twist, ahead), pltpu.VMEM), *held(operands, pltpu.HBM))
 
-    square = pltpu.VMEM((PEERS, PEERS), f32)
-
-    def make_early(velocity, stress, west, south, mark):
-        outs = [far(3, 4, 64, PEERS), far(64, PEERS), far(16, PEERS)]
-        return call(early_kernel, outs, velocity, stress, west, south, coef, mark, close=False)
-
-    def make_cells(rims, *operands):
+    def make_carry(spectrum, memory, later):
+        whole = lambda *dims: pl.BlockSpec(dims, lambda i: (0,) * len(dims))
+        wave = whole(6, 8, 1024)
+        return pl.pallas_call(
+            carry_kernel,
+            grid=(1,),
+            in_specs=[whole(12, 8, 1024), whole(2, 1, 8, 1024), wave, wave],
+            out_specs=[wave, wave],
+            out_shape=[far(6, 8, 1024)] * 2,
+            compiler_params=room(8),
+            name="carry",
+        )(spectrum, *held((memory, *later), pltpu.HBM))
+
+    def make_early(velocity, stress, west, south, name):
+        outs = [(far if name == "early0" else near)(3, 4, 64, PEERS), far(64, PEERS), far(16, PEERS)]
+        velocity, stress, coef_far = held((velocity, stress, coef), pltpu.HBM)
+        return call(early_kernel, outs, velocity, stress, west, south, coef_far, close=False)
+
+    def make_cells(rims, early, east, north, traction, *fields):
         outs = [shape(3, 4, 64, PEERS), shape(3, 3, 4, 64, PEERS)]
         if rims:
             outs = [far(3, 4, 64, PEERS), far(3, 3, 4, 64, PEERS), far(64, PEERS), far(16, PEERS)]
+            early, *fields = held((early, *fields), pltpu.VMEM)
+        operands = (early, east, north, traction, *fields)
         return call(functools.partial(cells_kernel, rims), outs, *operands, close=not rims)
 
     rows = exchange_row(pack(zone_table, velocity, stress, zones))
@@ -582,10 +584,11 @@
     now, later = zip(tails_of(history, memory, 0), tails_of(history, memory, 1))
     sent = exchange_all(call(forward_kernel, sending, rows, mx, twist, scratch=WORK))
     onward = [((GX - 1) * GY + h, (h + 1) % GY) for h in range(GY)]
-    above = lax.ppermute(rows[:, 160:168], both, onward)
-    early, east, north = make_early(velocity, stress, west, south, south)
+    above = lax.ppermute(rows[:, 120:], both, onward)
+    early, east, north = make_early(velocity, stress, west, south, "early0")
     east, north = shifted(east, "gx", -1), shifted(north, "gy", -1)
-    lines, *later = make_dip(True, sent, impedance, *now, memory, *later)
+    lines, spectrum = make_dip(True, sent, impedance, *now)
+    later = make_carry(spectrum, memory, later)
     lines = exchange_all(lines)
     feed = call(feed_kernel, near(GX, 64, PEERS), rows, above)
     sending1, traction = call(
@@ -596,12 +599,11 @@
     )
     sent = exchange_all(sending1)
     traction = exchange_row(traction)
-    lines = make_dip(False, sent, impedance, *later)
+    (lines,) = make_dip(False, sent, impedance, *later)
     lines = exchange_all(lines)
     velocity, stress, west, south = make_cells(True, early, east, north, traction, coef, stress, face_mask)
     west, south = shifted(west, "gx", 1), shifted(south, "gy", 1)
-    mark = call(mark_kernel, shape(8, PEERS), coef, close=False)
-    early, east, north = make_early(velocity, stress, west, south, mark)
+    early, east, north = make_early(velocity, stress, west, south, "early1")
     east, north = shifted(east, "gx", -1), shifted(north, "gy", -1)
     traction = call(inverse_kernel, near(GX, 64, PEERS), lines, mx, twist, scratch=[square] * 2)
     traction = exchange_row(traction)

time: 165 us -> 159 us (0.964)
  blocking collectives: 51.2 us -> 32.8 us
  waiting for transfers between devices: 38.8 us -> 48.9 us
  starting transfers between devices: 34.2 us -> 41 us
  local copies, waits for them, and re-layouts: 4.16 us -> 1.04 us
    all_to_all x2 -> x1, blocking collectives: 33.2 us -> 16.9 us  [exchange_all(): lax.all_to_all(blocks, both, split_axis=0, concat_axis=0, tiled=True)]
    all_to_all x2 -> x3, waiting for transfers between devices: 10.5 us -> 19 us  [exchange_all(): lax.all_to_all(blocks, both, split_axis=0, concat_axis=0, tiled=True)]
    all_to_all x2 -> x3, starting transfers between devices: 17.2 us -> 24 us  [exchange_all(): lax.all_to_all(blocks, both, split_axis=0, concat_axis=0, tiled=True)]
    unnamed x36 -> x20, local copies, waits for them, and re-layouts: 4.15 us -> 1.03 us
    pallas_call x9 -> x8, Pallas kernels: 14.9 us -> 12.4 us  [call(): pl.pallas_call(kernel, out_shape=outs, scratch_shapes=list(scratch), comp...]
    all_to_all x1, blocking collectives: 18 us -> 15.9 us  [exchange_row(): return lax.all_to_all(value, 'gx', split_axis=0, concat_axis=0, tiled=True)]
    pallas_call x0 -> x1, Pallas kernels: none -> 1.83 us  [make_carry(): pl.pallas_call(carry_kernel, grid=(1,), in_specs=[whole(12, 8, 1024), who...]
    ppermute x8, waiting for transfers between devices: 22.6 us -> 24.3 us  [shifted(): lax.ppermute(value, axis, [(source, (source + steps) % count) for source...]
  transfers between devices with their start and end apart: 13 -> 14, of which waited for: 9 -> 10; matrix products, arithmetic and copies ran while one was open for 0% -> 0% of each run, Pallas kernels for 14% -> 14%
where the time goes in v3:
time: 159 us; the launch traced here: 158 us
  waiting for transfers between devices  48.9 us (31%)
  starting transfers between devices  41 us (26%)
  Pallas kernels  33.9 us (21%)
  blocking collectives  32.8 us (21%)
    ppermute x8, waiting for transfers between devices, shifted(): lax.ppermute(value, axis, [(source, (source + steps) % count) for source...  24.3 us
    all_to_all x3, starting transfers between devices, exchange_all(): lax.all_to_all(blocks, both, split_axis=0, concat_axis=0, tiled=True)  24 us
    all_to_all x3, waiting for transfers between devices, exchange_all(): lax.all_to_all(blocks, both, split_axis=0, concat_axis=0, tiled=True)  19 us
    all_to_all x1, blocking collectives, exchange_all(): lax.all_to_all(blocks, both, split_axis=0, concat_axis=0, tiled=True)  16.9 us
    all_to_all x1, blocking collectives, exchange_row(): return lax.all_to_all(value, 'gx', split_axis=0, concat_axis=0, tiled=True)  15.9 us
    pallas_call x8, Pallas kernels, call(): pl.pallas_call(kernel, out_shape=outs, scratch_shapes=list(scratch), comp...  12.4 us
    all_to_all x2, starting transfers between devices, exchange_row(): return lax.all_to_all(value, 'gx', split_axis=0, concat_axis=0, tiled=True)  11.2 us
    pallas_call x2, Pallas kernels, tails_of(): pl.pallas_call(history_kernel, grid=(3,), in_specs=[pl.BlockSpec((1, 1, 3...  9.82 us
  transfers between devices with their start and end apart: 14, of which 10 were waited for; matrix products, arithmetic and copies ran while one was open for 0% of the time, Pallas kernels for 14%

profile of v3, /device:TPU:96, one launch (start us, length us, event | category | flops | bytes accessed | tf_op | source)
XLA Modules:
  0.0 158.5 jit_solution(16532294446045041759)
XLA Ops:
  0.6 0.0 copy-start.4
  0.6 0.0 copy-start.5
  0.7 2.3 %pack.1 = f32[8,128,128]{2,1,0:T(8,128)S(1)} custom-call(f32[3,8]{1,0:T(4,128)} %table_ref.3, f32[3,4,64,128]{3,2,1,0:T(8,128)} %velocity_ref.3, f32[3,3,4,64,128]{4,3,2,1,0:T(8,128)} %stress_ref.5, s32[4,64,128]{2,1,0:T(8,128)} %zones_ref.3), custom_call_target="tpu_custom_call" | custom-call | tf_op jit(solution)/shard_map/pack/pallas_call | solution.py:492
  3.0 15.9 %all_to_all.35.x_ref.rows_ref = f32[8,128,128]{2,1,0:T(8,128)S(1)} all-to-all(f32[8,128,128]{2,1,0:T(8,128)S(1)} %pack.1), channel_id=1, replica_groups=mesh['gx'=8,'gy'=16] {'gx'}, dimensions={0} | all-to-all | bytes 1048576 | tf_op jit(solution)/shard_map/all_to_all | solution.py:481
  18.9 1.2 shard_map.150
  20.1 8.1 %all-to-all-start.1 = ((f32[128,1,768]{2,1,0:T(1,128)}), f32[128,1,768]{2,1,0:T(1,128)S(1)}, u32[]{:S(2)}, u32[]{:S(2)}) async-start(f32[128,1,768]{2,1,0:T(1,128)} %bitcast), calls=%async_computation.1 | async-start | bytes 786432 | tf_op jit(solution)/shard_map/all_to_all | solution.py:476
  28.2 4.9 %shard_map.152 = (f32[6,8,1024]{2,1,0:T(8,128)}, f32[6,8,1024]{2,1,0:T(8,128)}) custom-call(f32[2,3,31,2,8,1024]{5,4,3,2,1,0:T(8,128)} %history_ref.3, f32[2,31,8,1024]{3,2,1,0:T(8,128)} %memory_ref.5), custom_call_target="tpu_custom_call" | custom-call | tf_op jit(solution)/shard_map/pallas_call | solution.py:522
  33.1 4.9 %shard_map.151 = (f32[6,8,1024]{2,1,0:T(8,128)}, f32[6,8,1024]{2,1,0:T(8,128)}) custom-call(f32[2,3,31,2,8,1024]{5,4,3,2,1,0:T(8,128)} %history_ref.3, f32[2,31,8,1024]{3,2,1,0:T(8,128)} %memory_ref.5), custom_call_target="tpu_custom_call" | custom-call | tf_op jit(solution)/shard_map/pallas_call | solution.py:522
  38.0 0.4 all-to-all-done.1
  38.4 3.1 %shard_map.153 = (f32[896,128]{1,0:T(8,128)}, f32[12,8,1024]{2,1,0:T(8,128)S(1)}) custom-call(f32[768,128]{1,0:T(8,128)S(1)} %bitcast.13, bf16[2,256,256]{2,1,0:T(8,128)(2,1)S(1)} %copy-done.7, f32[2,8,8,128]{3,2,1,0:T(8,128)S(1)} %copy-done.5, f32[2,8,128]{2,1,0:T(8,128)S(1)} %copy-done.9, f32[6,8,1024]{2,1,0:T(8,128)} %bitcast.14, ...), custom_call_target="tpu_custom_call" | custom-call | tf_op jit(solution)/shard_map/pallas_call | solution.py:546
  41.6 9.4 %all-to-all-start.2 = ((f32[128,1,896]{2,1,0:T(1,128)}), f32[128,1,896]{2,1,0:T(1,128)S(1)}, u32[]{:S(2)}, u32[]{:S(2)}) async-start(f32[128,1,896]{2,1,0:T(1,128)} %bitcast.3), calls=%async_computation.2 | async-start | bytes 917504 | tf_op jit(solution)/shard_map/all_to_all | solution.py:476
  50.9 0.7 collective-permute-start.4
  51.6 0.0 collective-permute-done.4.south_ref
  51.6 0.1 shard_map.154.early_ref
  51.7 10.1 %all-to-all-done.2 = f32[128,1,896]{2,1,0:T(1,128)S(1)} async-done(((f32[128,1,896]{2,1,0:T(1,128)}), f32[128,1,896]{2,1,0:T(1,128)S(1)}, u32[]{:S(2)}, u32[]{:S(2)}) %all-to-all-start.2) | async-done | bytes 458784 | tf_op jit(solution)/shard_map/all_to_all | solution.py:476
  61.9 1.7 %shard_map.155 = (f32[768,128]{1,0:T(8,128)}, f32[8,64,128]{2,1,0:T(8,128)}) custom-call(f32[896,128]{1,0:T(8,128)S(1)} %bitcast.9, f32[8,64,128]{2,1,0:T(8,128)S(1)} %shard_map.154.early_ref, bf16[2,256,256]{2,1,0:T(8,128)(2,1)S(1)} %copy-done.4, f32[2,8,8,128]{3,2,1,0:T(8,128)S(1)} %copy-done.5), custom_call_target="tpu_custom_call" | custom-call | tf_op jit(solution)/shard_map/pallas_call | solution.py:470
  63.6 6.6 %all-to-all-start.4 = ((f32[128,1,768]{2,1,0:T(1,128)}), f32[128,1,768]{2,1,0:T(1,128)S(1)}, u32[]{:S(2)}, u32[]{:S(2)}) async-start(f32[128,1,768]{2,1,0:T(1,128)} %bitcast.5), calls=%async_computation.4 | async-start | bytes 786432 | tf_op jit(solution)/shard_map/all_to_all | solution.py:476
  70.2 1.8 %carry.1 = (f32[6,8,1024]{2,1,0:T(8,128)}, f32[6,8,1024]{2,1,0:T(8,128)}) custom-call(f32[12,8,1024]{2,1,0:T(8,128)S(1)} %get-tuple-element.43.spectrum_ref, f32[2,31,8,1024]{3,2,1,0:T(8,128)} %memory_ref.5, f32[6,8,1024]{2,1,0:T(8,128)} %get-tuple-element.44.refs_0_, f32[6,8,1024]{2,1,0:T(8,128)} %get-tuple-element.45.refs_1_), custom_call_target="tpu_custom_call" | custom-call | tf_op jit(solution)/shard_map/carry/pallas_call | solution.py:558
  72.0 8.4 %all-to-all-done.4 = f32[128,1,768]{2,1,0:T(1,128)S(1)} async-done(((f32[128,1,768]{2,1,0:T(1,128)}), f32[128,1,768]{2,1,0:T(1,128)S(1)}, u32[]{:S(2)}, u32[]{:S(2)}) %all-to-all-start.4) | async-done | bytes 393248 | tf_op jit(solution)/shard_map/all_to_all | solution.py:476
  80.4 2.3 %shard_map.158 = f32[896,128]{1,0:T(8,128)S(1)} custom-call(f32[768,128]{1,0:T(8,128)S(1)} %bitcast.12, bf16[2,256,256]{2,1,0:T(8,128)(2,1)S(1)} %copy-done.7, f32[2,8,8,128]{3,2,1,0:T(8,128)S(1)} %copy-done.5, f32[2,8,128]{2,1,0:T(8,128)S(1)} %copy-done.9, f32[6,8,1024]{2,1,0:T(8,128)} %bitcast.15, f32[6,8,1024]{2,1,0:T(8,128)} %get-tuple-element.46.refs_0_, ...), custom_call_target="tpu_custom_call" | custom-call | tf_op jit(solution)/shard_map/pallas_call | solution.py:546
  82.8 16.9 %all_to_all.36 = f32[128,1,896]{2,1,0:T(1,128)S(1)} all-to-all(f32[128,1,896]{2,1,0:T(1,128)S(1)} %bitcast.11), channel_id=1, replica_groups=mesh['gx'=8,'gy'=16] {'gx','gy'}, dimensions={0} | all-to-all | bytes 917504 | tf_op jit(solution)/shard_map/all_to_all | solution.py:476
  99.7 5.6 %all-to-all-start.3 = ((f32[8,64,128]{2,1,0:T(8,128)}), f32[8,64,128]{2,1,0:T(8,128)S(1)}, u32[]{:S(2)}, u32[]{:S(2)}) async-start(f32[8,64,128]{2,1,0:T(8,128)} %get-tuple-element.34), calls=%async_computation.3 | async-start | bytes 524288 | tf_op jit(solution)/shard_map/all_to_all | solution.py:481
  105.2 1.2 shard_map.159
  106.5 5.7 %all-to-all-done.3.d_ref = f32[8,64,128]{2,1,0:T(8,128)S(1)} async-done(((f32[8,64,128]{2,1,0:T(8,128)}), f32[8,64,128]{2,1,0:T(8,128)S(1)}, u32[]{:S(2)}, u32[]{:S(2)}) %all-to-all-start.3) | async-done | bytes 262176 | tf_op jit(solution)/shard_map/all_to_all | solution.py:481
  112.1 5.7 %all-to-all-start.6 = ((f32[8,64,128]{2,1,0:T(8,128)}), f32[8,64,128]{2,1,0:T(8,128)S(1)}, u32[]{:S(2)}, u32[]{:S(2)}) async-start(f32[8,64,128]{2,1,0:T(8,128)} %shard_map.159), calls=%async_computation.6 | async-start | bytes 524288 | tf_op jit(solution)/shard_map/all_to_all | solution.py:481
  117.8 2.1 %zones.1 = (f32[3,4,64,128]{3,2,1,0:T(8,128)}, f32[64,128]{1,0:T(8,128)}, f32[16,128]{1,0:T(8,128)}) custom-call(f32[3,8]{1,0:T(4,128)} %table_ref.3, s32[4,64,128]{2,1,0:T(8,128)} %zones_ref.3, f32[3,3,4,64,128]{4,3,2,1,0:T(8,128)} %stress_ref.5, f32[3,3,4,64,128]{4,3,2,1,0:T(8,128)} %stress_ref.5), custom_call_target="tpu_custom_call" | custom-call | tf_op jit(solution)/shard_map/zones/pallas_call | solution.py:504
  119.9 3.0 %collective-permute-start = (f32[64,128]{1,0:T(8,128)}, f32[64,128]{1,0:T(8,128)S(1)}, u32[]{:S(2)}, u32[]{:S(2)}) collective-permute-start(f32[64,128]{1,0:T(8,128)} %get-tuple-element.25), channel_id=1, source_target_pairs={{0,16},{16,32},{32,48},{48,64},{64,80},{80,96},{96,112},{112,0},{1... | collective-permute-start | bytes 98312 | tf_op jit(solution)/shard_map/ppermute | solution.py:486
  122.9 0.0 collective-permute-start.1
  123.0 5.4 %collective-permute-done.1.south_ref = f32[16,128]{1,0:T(8,128)S(1)} collective-permute-done((f32[16,128]{1,0:T(8,128)}, f32[16,128]{1,0:T(8,128)S(1)}, u32[]{:S(2)}, u32[]{:S(2)}) %collective-permute-start.1) | collective-permute-done | bytes 8224 | tf_op jit(solution)/shard_map/ppermute | solution.py:486
  128.3 0.0 collective-permute-done.west_ref
  128.3 2.5 %shard_map.149 = (f32[3,4,64,128]{3,2,1,0:T(8,128)}, f32[64,128]{1,0:T(8,128)}, f32[16,128]{1,0:T(8,128)}) custom-call(f32[3,4,64,128]{3,2,1,0:T(8,128)} %velocity_ref.3, f32[3,3,4,64,128]{4,3,2,1,0:T(8,128)} %stress_ref.5, f32[64,128]{1,0:T(8,128)S(1)} %collective-permute-done.west_ref, f32[16,128]{1,0:T(8,128)S(1)} %collective-permute-done.1.south_ref, ...), custom_call_target="tpu_custom_call" | custom-call | tf_op jit(solution)/shard_map/pallas_call | solution.py:470
  130.9 0.0 collective-permute-start.2
  130.9 0.0 collective-permute-start.3
  130.9 1.6 collective-permute-done.3.north_ref
  132.4 6.2 %collective-permute-done.2.east_ref = f32[64,128]{1,0:T(8,128)S(1)} collective-permute-done((f32[64,128]{1,0:T(8,128)}, f32[64,128]{1,0:T(8,128)S(1)}, u32[]{:S(2)}, u32[]{:S(2)}) %collective-permute-start.2) | collective-permute-done | bytes 32800 | tf_op jit(solution)/shard_map/ppermute | solution.py:486
  138.6 0.0 copy-start.8
  138.6 1.0 copy-done.8
  139.6 1.7 %shard_map.156 = (f32[3,4,64,128]{3,2,1,0:T(8,128)}, f32[3,3,4,64,128]{4,3,2,1,0:T(8,128)}, f32[64,128]{1,0:T(8,128)}, f32[16,128]{1,0:T(8,128)}) custom-call(f32[3,4,64,128]{3,2,1,0:T(8,128)S(1)} %copy-done.8, f32[64,128]{1,0:T(8,128)S(1)} %collective-permute-done.2.east_ref, f32[16,128]{1,0:T(8,128)S(1)} %collective-permute-done.3.north_ref, ...), custom_call_target="tpu_custom_call" | custom-call | tf_op jit(solution)/shard_map/pallas_call | solution.py:470
  141.3 0.0 collective-permute-start.5
  141.3 0.1 collective-permute-start.6
  141.4 5.4 %collective-permute-done.6.south_ref = f32[16,128]{1,0:T(8,128)S(1)} collective-permute-done((f32[16,128]{1,0:T(8,128)}, f32[16,128]{1,0:T(8,128)S(1)}, u32[]{:S(2)}, u32[]{:S(2)}) %collective-permute-start.6) | collective-permute-done | bytes 8224 | tf_op jit(solution)/shard_map/ppermute | solution.py:486
  146.7 0.0 collective-permute-done.5.west_ref
  146.8 2.5 %shard_map.157 = (f32[3,4,64,128]{3,2,1,0:T(8,128)S(1)}, f32[64,128]{1,0:T(8,128)}, f32[16,128]{1,0:T(8,128)}) custom-call(f32[3,4,64,128]{3,2,1,0:T(8,128)} %get-tuple-element.35.velocity_ref, f32[3,3,4,64,128]{4,3,2,1,0:T(8,128)} %get-tuple-element.36.stress_ref, f32[64,128]{1,0:T(8,128)S(1)} %collective-permute-done.5.west_ref, ...), custom_call_target="tpu_custom_call" | custom-call | tf_op jit(solution)/shard_map/pallas_call | solution.py:470
  149.2 1.9 %collective-permute-start.7 = (f32[64,128]{1,0:T(8,128)}, f32[64,128]{1,0:T(8,128)S(1)}, u32[]{:S(2)}, u32[]{:S(2)}) collective-permute-start(f32[64,128]{1,0:T(8,128)} %get-tuple-element.40), channel_id=1, source_target_pairs={{0,112},{16,0},{32,16},{48,32},{64,48},{80,64},{96,80},{112,96},{1... | collective-permute-start | bytes 98312 | tf_op jit(solution)/shard_map/ppermute | solution.py:486
  151.2 1.6 collective-permute-done.8.north_ref
  152.8 4.2 %collective-permute-done.7.east_ref = f32[64,128]{1,0:T(8,128)S(1)} collective-permute-done((f32[64,128]{1,0:T(8,128)}, f32[64,128]{1,0:T(8,128)S(1)}, u32[]{:S(2)}, u32[]{:S(2)}) %collective-permute-start.7) | collective-permute-done | bytes 32800 | tf_op jit(solution)/shard_map/ppermute | solution.py:486
  157.0 0.0 all-to-all-done.6.d_ref
  157.0 1.5 shard_map.160
  (18 shorter events, 0.0 us)
Async XLA Ops:
  0.6 18.2 %copy-start.4 = (bf16[2,256,256]{2,1,0:T(8,128)(2,1)S(1)}, bf16[2,256,256]{2,1,0:T(8,128)(2,1)}, u32[]{:S(2)}) copy-start(bf16[2,256,256]{2,1,0:T(8,128)(2,1)} %constant.21.mx_ref) | copy-start | bytes 786436
  0.6 18.2 %copy-start.5 = (f32[2,8,8,128]{3,2,1,0:T(8,128)S(1)}, f32[2,8,8,128]{3,2,1,0:T(8,128)}, u32[]{:S(2)}) copy-start(f32[2,8,8,128]{3,2,1,0:T(8,128)} %constant.10.clone.twist_ref) | copy-start | bytes 196612
  20.1 18.4 %all-to-all-start.1 = ((f32[128,1,768]{2,1,0:T(1,128)}), f32[128,1,768]{2,1,0:T(1,128)S(1)}, u32[]{:S(2)}, u32[]{:S(2)}) async-start(f32[128,1,768]{2,1,0:T(1,128)} %bitcast), calls=%async_computation.1 | async-start | bytes 786432 | tf_op jit(solution)/shard_map/all_to_all | solution.py:476
  33.1 5.4 %copy-start.7 = (bf16[2,256,256]{2,1,0:T(8,128)(2,1)S(1)}, bf16[2,256,256]{2,1,0:T(8,128)(2,1)}, u32[]{:S(2)}) copy-start(bf16[2,256,256]{2,1,0:T(8,128)(2,1)} %constant.28.my_ref) | copy-start | bytes 786436
  33.1 5.4 %copy-start.9 = (f32[2,8,128]{2,1,0:T(8,128)S(1)}, f32[2,8,128]{2,1,0:T(8,128)}, u32[]{:S(2)}) copy-start(f32[2,8,128]{2,1,0:T(8,128)} %constant.11.clone.ahead_ref) | copy-start | bytes 24580
  41.6 20.3 %all-to-all-start.2 = ((f32[128,1,896]{2,1,0:T(1,128)}), f32[128,1,896]{2,1,0:T(1,128)S(1)}, u32[]{:S(2)}, u32[]{:S(2)}) async-start(f32[128,1,896]{2,1,0:T(1,128)} %bitcast.3), calls=%async_computation.2 | async-start | bytes 917504 | tf_op jit(solution)/shard_map/all_to_all | solution.py:476
  50.9 0.7 collective-permute-start.4
  63.6 16.9 %all-to-all-start.4 = ((f32[128,1,768]{2,1,0:T(1,128)}), f32[128,1,768]{2,1,0:T(1,128)S(1)}, u32[]{:S(2)}, u32[]{:S(2)}) async-start(f32[128,1,768]{2,1,0:T(1,128)} %bitcast.5), calls=%async_computation.4 | async-start | bytes 786432 | tf_op jit(solution)/shard_map/all_to_all | solution.py:476
  99.7 12.4 %all-to-all-start.3 = ((f32[8,64,128]{2,1,0:T(8,128)}), f32[8,64,128]{2,1,0:T(8,128)S(1)}, u32[]{:S(2)}, u32[]{:S(2)}) async-start(f32[8,64,128]{2,1,0:T(8,128)} %get-tuple-element.34), calls=%async_computation.3 | async-start | bytes 524288 | tf_op jit(solution)/shard_map/all_to_all | solution.py:481
  112.1 44.8 %all-to-all-start.6 = ((f32[8,64,128]{2,1,0:T(8,128)}), f32[8,64,128]{2,1,0:T(8,128)S(1)}, u32[]{:S(2)}, u32[]{:S(2)}) async-start(f32[8,64,128]{2,1,0:T(8,128)} %shard_map.159), calls=%async_computation.6 | async-start | bytes 524288 | tf_op jit(solution)/shard_map/all_to_all | solution.py:481
  119.9 18.7 %copy-start = (f32[3,3,4,64,128]{4,3,2,1,0:T(8,128)S(1)}, f32[3,3,4,64,128]{4,3,2,1,0:T(8,128)}, u32[]{:S(2)}) copy-start(f32[3,3,4,64,128]{4,3,2,1,0:T(8,128)} %stress_ref.5) | copy-start | bytes 3538948
  119.9 18.7 %copy-start.1 = (f32[3,4,64,128]{3,2,1,0:T(8,128)S(1)}, f32[3,4,64,128]{3,2,1,0:T(8,128)}, u32[]{:S(2)}) copy-start(f32[3,4,64,128]{3,2,1,0:T(8,128)} %get-tuple-element.27.coef_ref) | copy-start | bytes 1179652
  119.9 18.7 %copy-start.6 = (s32[3,4,64,128]{3,2,1,0:T(8,128)S(1)}, s32[3,4,64,128]{3,2,1,0:T(8,128)}, u32[]{:S(2)}) copy-start(s32[3,4,64,128]{3,2,1,0:T(8,128)} %mask_ref.3) | copy-start | bytes 1179652
  119.9 8.4 %collective-permute-start = (f32[64,128]{1,0:T(8,128)}, f32[64,128]{1,0:T(8,128)S(1)}, u32[]{:S(2)}, u32[]{:S(2)}) collective-permute-start(f32[64,128]{1,0:T(8,128)} %get-tuple-element.25), channel_id=1, source_target_pairs={{0,16},{16,32},{32,48},{48,64},{64,80},{80,96},{96,112},{112,0},{1... | collective-permute-start | bytes 98312 | tf_op jit(solution)/shard_map/ppermute | solution.py:486
  122.9 5.4 %collective-permute-start.1 = (f32[16,128]{1,0:T(8,128)}, f32[16,128]{1,0:T(8,128)S(1)}, u32[]{:S(2)}, u32[]{:S(2)}) collective-permute-start(f32[16,128]{1,0:T(8,128)} %get-tuple-element.26), channel_id=1, source_target_pairs={{0,1},{1,2},{2,3},{3,4},{4,5},{5,6},{6,7},{7,8},{8,9},{9,10},{10,1... | collective-permute-start | bytes 24584 | tf_op jit(solution)/shard_map/ppermute | solution.py:486
  130.9 7.7 %collective-permute-start.2 = (f32[64,128]{1,0:T(8,128)}, f32[64,128]{1,0:T(8,128)S(1)}, u32[]{:S(2)}, u32[]{:S(2)}) collective-permute-start(f32[64,128]{1,0:T(8,128)} %get-tuple-element.29), channel_id=1, source_target_pairs={{0,112},{16,0},{32,16},{48,32},{64,48},{80,64},{96,80},{112,96},{1... | collective-permute-start | bytes 98312 | tf_op jit(solution)/shard_map/ppermute | solution.py:486
  130.9 1.6 collective-permute-start.3
  138.6 1.0 copy-start.8
  141.3 15.7 %copy-start.2 = (f32[3,4,64,128]{3,2,1,0:T(8,128)S(1)}, f32[3,4,64,128]{3,2,1,0:T(8,128)}, u32[]{:S(2)}) copy-start(f32[3,4,64,128]{3,2,1,0:T(8,128)} %get-tuple-element.27.coef_ref) | copy-start | bytes 1179652
  141.3 15.7 %copy-start.3 = (f32[3,3,4,64,128]{4,3,2,1,0:T(8,128)S(1)}, f32[3,3,4,64,128]{4,3,2,1,0:T(8,128)}, u32[]{:S(2)}) copy-start(f32[3,3,4,64,128]{4,3,2,1,0:T(8,128)} %get-tuple-element.36.stress_ref) | copy-start | bytes 3538948
  141.3 5.5 %collective-permute-start.5 = (f32[64,128]{1,0:T(8,128)}, f32[64,128]{1,0:T(8,128)S(1)}, u32[]{:S(2)}, u32[]{:S(2)}) collective-permute-start(f32[64,128]{1,0:T(8,128)} %get-tuple-element.37), channel_id=1, source_target_pairs={{0,16},{16,32},{32,48},{48,64},{64,80},{80,96},{96,112},{112,0},{1... | collective-permute-start | bytes 98312 | tf_op jit(solution)/shard_map/ppermute | solution.py:486
  141.3 5.5 %collective-permute-start.6 = (f32[16,128]{1,0:T(8,128)}, f32[16,128]{1,0:T(8,128)S(1)}, u32[]{:S(2)}, u32[]{:S(2)}) collective-permute-start(f32[16,128]{1,0:T(8,128)} %get-tuple-element.38), channel_id=1, source_target_pairs={{0,1},{1,2},{2,3},{3,4},{4,5},{5,6},{6,7},{7,8},{8,9},{9,10},{10,1... | collective-permute-start | bytes 24584 | tf_op jit(solution)/shard_map/ppermute | solution.py:486
  149.2 7.7 %collective-permute-start.7 = (f32[64,128]{1,0:T(8,128)}, f32[64,128]{1,0:T(8,128)S(1)}, u32[]{:S(2)}, u32[]{:S(2)}) collective-permute-start(f32[64,128]{1,0:T(8,128)} %get-tuple-element.40), channel_id=1, source_target_pairs={{0,112},{16,0},{32,16},{48,32},{64,48},{80,64},{96,80},{112,96},{1... | collective-permute-start | bytes 98312 | tf_op jit(solution)/shard_map/ppermute | solution.py:486
  151.2 1.6 collective-permute-start.8

commit v4 on v3

--- a/solution.py
+++ b/solution.py
@@ -121,7 +121,7 @@
                 rows = pl.ds(member * 64 + k * 8, 8)
                 re_ref[rows, :] = re
                 im_ref[rows, :] = im
-        to_peers(o_ref, pair, matrix, re_ref, im_ref, 6)
+        to_peers(o_ref, pair, matrix, re_ref, im_ref, TILES)
 
 
 def strike_inverse(x_ref, twist_ref, matrix, d_ref, re_ref, im_ref, put):
@@ -186,7 +186,7 @@
     im2_ref[...] = jnp.zeros((PEERS, PEERS), f32)
     c8, s8 = ahead_ref[0], ahead_ref[1]
     for pair in range(3):
-        from_peers(x_ref, pair, matrix, re_ref, im_ref, 6)
+        from_peers(x_ref, pair, matrix, re_ref, im_ref, TILES)
         for copy in arriving[pair]:
             copy.wait()
         for member in range(2):
@@ -248,20 +248,35 @@
     strike_inverse(x_ref, twist_ref, matrix, d_ref, re_ref, im_ref, lambda plane, tile, value: None)
 
 
-def history_kernel(history_ref, memory_ref, now_ref, next_ref):
-    lags = history_ref.shape[2]
-    for tile in range(8):
-        lanes = pl.ds(tile * PEERS, PEERS)
-        for part in range(2):
-            now = jnp.zeros((8, PEERS), f32)
-            later = jnp.zeros((8, PEERS), f32)
-            for lag in range(lags):
-                value = history_ref[0, 0, lag, part, :, lanes]
-                now = now + memory_ref[0, lag, :, lanes] * value
-                if lag + 1 < lags:
-                    later = later + memory_ref[0, lag + 1, :, lanes] * value
-            now_ref[part, :, lanes] = now
-            next_ref[part, :, lanes] = later
+def history_kernel(side, history_ref, memory_ref, now_ref, next_ref, h_ref, m_ref, sems):
+    lags = h_ref.shape[1]
+    chunks = [(0, 11), (11, 11), (22, 9)]
+    copies = [pltpu.make_async_copy(memory_ref.at[side], m_ref, sems.at[9])]
+    for c in range(3):
+        for number, (begin, count) in enumerate(chunks):
+            span = pl.ds(begin, count)
+            copies.append(
+                pltpu.make_async_copy(history_ref.at[side, c, span], h_ref.at[c, span], sems.at[3 * c + number])
+            )
+    for copy in copies:
+        copy.start()
+    copies[0].wait()
+    for c in range(3):
+        for number, (begin, count) in enumerate(chunks):
+            copies[1 + 3 * c + number].wait()
+            for tile in range(8):
+                lanes = pl.ds(tile * PEERS, PEERS)
+                for part in range(2):
+                    row = 2 * c + part
+                    now = now_ref[row, :, lanes] if begin else jnp.zeros((8, PEERS), f32)
+                    later = next_ref[row, :, lanes] if begin else jnp.zeros((8, PEERS), f32)
+                    for lag in range(begin, begin + count):
+                        value = h_ref[c, lag, part, :, lanes]
+                        now = now + m_ref[lag, :, lanes] * value
+                        if lag + 1 < lags:
+                            later = later + m_ref[lag + 1, :, lanes] * value
+                    now_ref[row, :, lanes] = now
+                    next_ref[row, :, lanes] = later
 
 
 def pack_kernel(table_ref, velocity_ref, stress_ref, zones_ref, o_ref, v_ref, x_ref, y_ref, z_ref, zone_ref, sems):
@@ -518,16 +533,17 @@
 
 
 def tails_of(history, memory, plane):
-    out_spec = pl.BlockSpec((2, 8, 1024), lambda c: (c, 0, 0))
+    whole = pl.BlockSpec(memory_space=pltpu.HBM)
     return pl.pallas_call(
-        history_kernel,
-        grid=(3,),
-        in_specs=[
-            pl.BlockSpec((1, 1, 31, 2, 8, 1024), lambda c: (plane, c, 0, 0, 0, 0)),
-            pl.BlockSpec((1, 31, 8, 1024), lambda c: (plane, 0, 0, 0)),
+        functools.partial(history_kernel, plane),
+        in_specs=[whole, whole],
+        out_shape=[far(6, 8, 1024)] * 2,
+        scratch_shapes=[
+            pltpu.VMEM((3, 31, 2, 8, 1024), f32),
+            pltpu.VMEM((31, 8, 1024), f32),
+            pltpu.SemaphoreType.DMA((10,)),
         ],
-        out_specs=[out_spec, out_spec],
-        out_shape=[far(6, 8, 1024)] * 2,
+        out_specs=[pl.BlockSpec((6, 8, 1024), lambda: (0, 0, 0))] * 2,
         compiler_params=room(16),
     )(*held((history, memory), pltpu.HBM))
 
@@ -535,7 +551,7 @@
 def steps(velocity, stress, face_mask, zones, zone_table, impedance, memory, history):
     mx, my, twist, ahead = tables()
     impedance = impedance.reshape(6, 8, 1024)
-    sending, returning = near(6 * PEERS, PEERS), near(TILES * PEERS, PEERS)
+    sending, returning = near(TILES * PEERS, PEERS), near(TILES * PEERS, PEERS)
     dma = pltpu.SemaphoreType.DMA
     square = pltpu.VMEM((PEERS, PEERS), f32)
 
@@ -567,14 +583,14 @@
 
     def make_early(velocity, stress, west, south, name):
         outs = [(far if name == "early0" else near)(3, 4, 64, PEERS), far(64, PEERS), far(16, PEERS)]
-        velocity, stress, coef_far = held((velocity, stress, coef), pltpu.HBM)
+        velocity, stress, coef_far = held((velocity, stress, coef), pltpu.HBM if name == "early0" else pltpu.VMEM)
         return call(early_kernel, outs, velocity, stress, west, south, coef_far, close=False)
 
     def make_cells(rims, early, east, north, traction, *fields):
         outs = [shape(3, 4, 64, PEERS), shape(3, 3, 4, 64, PEERS)]
         if rims:
-            outs = [far(3, 4, 64, PEERS), far(3, 3, 4, 64, PEERS), far(64, PEERS), far(16, PEERS)]
-            early, *fields = held((early, *fields), pltpu.VMEM)
+            outs = [near(3, 4, 64, PEERS), near(3, 3, 4, 64, PEERS), far(64, PEERS), far(16, PEERS)]
+            early, *fields = held((early, *fields), pltpu.HBM)
         operands = (early, east, north, traction, *fields)
         return call(functools.partial(cells_kernel, rims), outs, *operands, close=not rims)
 

time: 159 us -> 157 us (0.987)
  waiting for transfers between devices: 48.9 us -> 52.2 us
  starting transfers between devices: 41 us -> 38.4 us
  Pallas kernels: 33.9 us -> 31.8 us
    all_to_all x3, waiting for transfers between devices: 19 us -> 22.2 us  [exchange_all(): lax.all_to_all(blocks, both, split_axis=0, concat_axis=0, tiled=True)]
    all_to_all x3, starting transfers between devices: 24 us -> 21.5 us  [exchange_all(): lax.all_to_all(blocks, both, split_axis=0, concat_axis=0, tiled=True)]
    pallas_call x2, Pallas kernels: 9.82 us -> 7.87 us  [tails_of(): pl.pallas_call(functools.partial(history_kernel, plane), in_specs=[whole,...]
  transfers between devices with their start and end apart: 14 -> 14, of which waited for: 10 -> 10; matrix products, arithmetic and copies ran while one was open for 0% -> 0% of each run, Pallas kernels for 14% -> 13%
where the time goes in v4:
time: 157 us; the launch traced here: 156 us
  waiting for transfers between devices  52.2 us (33%)
  starting transfers between devices  38.4 us (24%)
  blocking collectives  32.7 us (21%)
  Pallas kernels  31.8 us (20%)
    ppermute x8, waiting for transfers between devices, shifted(): lax.ppermute(value, axis, [(source, (source + steps) % count) for source...  24.3 us
    all_to_all x3, waiting for transfers between devices, exchange_all(): lax.all_to_all(blocks, both, split_axis=0, concat_axis=0, tiled=True)  22.2 us
    all_to_all x3, starting transfers between devices, exchange_all(): lax.all_to_all(blocks, both, split_axis=0, concat_axis=0, tiled=True)  21.5 us
    all_to_all x1, blocking collectives, exchange_all(): lax.all_to_all(blocks, both, split_axis=0, concat_axis=0, tiled=True)  16.9 us
    all_to_all x1, blocking collectives, exchange_row(): return lax.all_to_all(value, 'gx', split_axis=0, concat_axis=0, tiled=True)  15.9 us
    pallas_call x8, Pallas kernels, call(): pl.pallas_call(kernel, out_shape=outs, scratch_shapes=list(scratch), comp...  12.3 us
    all_to_all x2, starting transfers between devices, exchange_row(): return lax.all_to_all(value, 'gx', split_axis=0, concat_axis=0, tiled=True)  11.2 us
    pallas_call x2, Pallas kernels, tails_of(): pl.pallas_call(functools.partial(history_kernel, plane), in_specs=[whole,...  7.87 us
  transfers between devices with their start and end apart: 14, of which 10 were waited for; matrix products, arithmetic and copies ran while one was open for 0% of the time, Pallas kernels for 13%

profile of v4, /device:TPU:96, one launch (start us, length us, event | category | flops | bytes accessed | tf_op | source)
XLA Modules:
  0.0 156.0 jit_solution(1622736128496104590)
XLA Ops:
  0.6 0.0 copy-start.1
  0.6 0.0 copy-start.2
  0.7 2.3 %pack.1 = f32[8,128,128]{2,1,0:T(8,128)S(1)} custom-call(f32[3,8]{1,0:T(4,128)} %table_ref.3, f32[3,4,64,128]{3,2,1,0:T(8,128)} %velocity_ref.3, f32[3,3,4,64,128]{4,3,2,1,0:T(8,128)} %stress_ref.5, s32[4,64,128]{2,1,0:T(8,128)} %zones_ref.3), custom_call_target="tpu_custom_call" | custom-call | tf_op jit(solution)/shard_map/pack/pallas_call | solution.py:507
  3.0 15.9 %all_to_all.35.x_ref.rows_ref = f32[8,128,128]{2,1,0:T(8,128)S(1)} all-to-all(f32[8,128,128]{2,1,0:T(8,128)S(1)} %pack.1), channel_id=1, replica_groups=mesh['gx'=8,'gy'=16] {'gx'}, dimensions={0} | all-to-all | bytes 1048576 | tf_op jit(solution)/shard_map/all_to_all | solution.py:496
  18.9 1.3 shard_map.150
  20.1 8.1 %all-to-all-start.1 = ((f32[128,1,896]{2,1,0:T(1,128)}), f32[128,1,896]{2,1,0:T(1,128)S(1)}, u32[]{:S(2)}, u32[]{:S(2)}) async-start(f32[128,1,896]{2,1,0:T(1,128)} %bitcast), calls=%async_computation.1 | async-start | bytes 917504 | tf_op jit(solution)/shard_map/all_to_all | solution.py:491
  28.2 3.9 %shard_map.152 = (f32[6,8,1024]{2,1,0:T(8,128)}, f32[6,8,1024]{2,1,0:T(8,128)}) custom-call(f32[2,3,31,2,8,1024]{5,4,3,2,1,0:T(8,128)} %history_ref.3, f32[2,31,8,1024]{3,2,1,0:T(8,128)} %memory_ref.5), custom_call_target="tpu_custom_call" | custom-call | tf_op jit(solution)/shard_map/pallas_call | solution.py:537
  32.1 0.0 copy-start.4
  32.1 0.0 copy-start.5
  32.2 4.0 %shard_map.151 = (f32[6,8,1024]{2,1,0:T(8,128)}, f32[6,8,1024]{2,1,0:T(8,128)}) custom-call(f32[2,3,31,2,8,1024]{5,4,3,2,1,0:T(8,128)} %history_ref.3, f32[2,31,8,1024]{3,2,1,0:T(8,128)} %memory_ref.5), custom_call_target="tpu_custom_call" | custom-call | tf_op jit(solution)/shard_map/pallas_call | solution.py:537
  36.1 3.0 %all-to-all-done.1 = f32[128,1,896]{2,1,0:T(1,128)S(1)} async-done(((f32[128,1,896]{2,1,0:T(1,128)}), f32[128,1,896]{2,1,0:T(1,128)S(1)}, u32[]{:S(2)}, u32[]{:S(2)}) %all-to-all-start.1) | async-done | bytes 458784 | tf_op jit(solution)/shard_map/all_to_all | solution.py:491
  39.1 3.1 %shard_map.153 = (f32[896,128]{1,0:T(8,128)}, f32[12,8,1024]{2,1,0:T(8,128)S(1)}) custom-call(f32[896,128]{1,0:T(8,128)S(1)} %bitcast.13, bf16[2,256,256]{2,1,0:T(8,128)(2,1)S(1)} %copy-done.4, f32[2,8,8,128]{3,2,1,0:T(8,128)S(1)} %copy-done.2, f32[2,8,128]{2,1,0:T(8,128)S(1)} %copy-done.5, f32[6,8,1024]{2,1,0:T(8,128)} %bitcast.14, ...), custom_call_target="tpu_custom_call" | custom-call | tf_op jit(solution)/shard_map/pallas_call | solution.py:562
  42.3 6.8 %all-to-all-start.2 = ((f32[128,1,896]{2,1,0:T(1,128)}), f32[128,1,896]{2,1,0:T(1,128)S(1)}, u32[]{:S(2)}, u32[]{:S(2)}) async-start(f32[128,1,896]{2,1,0:T(1,128)} %bitcast.3), calls=%async_computation.2 | async-start | bytes 917504 | tf_op jit(solution)/shard_map/all_to_all | solution.py:491
  49.1 0.7 collective-permute-start.4
  49.7 0.0 collective-permute-done.4.south_ref
  49.7 0.1 shard_map.154.early_ref
  49.9 10.1 %all-to-all-done.2 = f32[128,1,896]{2,1,0:T(1,128)S(1)} async-done(((f32[128,1,896]{2,1,0:T(1,128)}), f32[128,1,896]{2,1,0:T(1,128)S(1)}, u32[]{:S(2)}, u32[]{:S(2)}) %all-to-all-start.2) | async-done | bytes 458784 | tf_op jit(solution)/shard_map/all_to_all | solution.py:491
  60.0 1.7 %shard_map.155 = (f32[896,128]{1,0:T(8,128)}, f32[8,64,128]{2,1,0:T(8,128)}) custom-call(f32[896,128]{1,0:T(8,128)S(1)} %bitcast.11, f32[8,64,128]{2,1,0:T(8,128)S(1)} %shard_map.154.early_ref, bf16[2,256,256]{2,1,0:T(8,128)(2,1)S(1)} %copy-done.1, f32[2,8,8,128]{3,2,1,0:T(8,128)S(1)} %copy-done.2), custom_call_target="tpu_custom_call" | custom-call | tf_op jit(solution)/shard_map/pallas_call | solution.py:485
  61.7 6.6 %all-to-all-start.4 = ((f32[128,1,896]{2,1,0:T(1,128)}), f32[128,1,896]{2,1,0:T(1,128)S(1)}, u32[]{:S(2)}, u32[]{:S(2)}) async-start(f32[128,1,896]{2,1,0:T(1,128)} %bitcast.5), calls=%async_computation.4 | async-start | bytes 917504 | tf_op jit(solution)/shard_map/all_to_all | solution.py:491
  68.3 1.8 %carry.1 = (f32[6,8,1024]{2,1,0:T(8,128)}, f32[6,8,1024]{2,1,0:T(8,128)}) custom-call(f32[12,8,1024]{2,1,0:T(8,128)S(1)} %get-tuple-element.43.spectrum_ref, f32[2,31,8,1024]{3,2,1,0:T(8,128)} %memory_ref.5, f32[6,8,1024]{2,1,0:T(8,128)} %get-tuple-element.44.refs_0_, f32[6,8,1024]{2,1,0:T(8,128)} %get-tuple-element.45.refs_1_), custom_call_target="tpu_custom_call" | custom-call | tf_op jit(solution)/shard_map/carry/pallas_call | solution.py:574
  70.2 9.1 %all-to-all-done.4 = f32[128,1,896]{2,1,0:T(1,128)S(1)} async-done(((f32[128,1,896]{2,1,0:T(1,128)}), f32[128,1,896]{2,1,0:T(1,128)S(1)}, u32[]{:S(2)}, u32[]{:S(2)}) %all-to-all-start.4) | async-done | bytes 458784 | tf_op jit(solution)/shard_map/all_to_all | solution.py:491
  79.3 2.3 %shard_map.158 = f32[896,128]{1,0:T(8,128)S(1)} custom-call(f32[896,128]{1,0:T(8,128)S(1)} %bitcast.9, bf16[2,256,256]{2,1,0:T(8,128)(2,1)S(1)} %copy-done.4, f32[2,8,8,128]{3,2,1,0:T(8,128)S(1)} %copy-done.2, f32[2,8,128]{2,1,0:T(8,128)S(1)} %copy-done.5, f32[6,8,1024]{2,1,0:T(8,128)} %bitcast.15, f32[6,8,1024]{2,1,0:T(8,128)} %get-tuple-element.46.refs_0_, ...), custom_call_target="tpu_custom_call" | custom-call | tf_op jit(solution)/shard_map/pallas_call | solution.py:562
  81.6 16.9 %all_to_all.36 = f32[128,1,896]{2,1,0:T(1,128)S(1)} all-to-all(f32[128,1,896]{2,1,0:T(1,128)S(1)} %bitcast.10), channel_id=1, replica_groups=mesh['gx'=8,'gy'=16] {'gx','gy'}, dimensions={0} | all-to-all | bytes 917504 | tf_op jit(solution)/shard_map/all_to_all | solution.py:491
  98.5 5.6 %all-to-all-start.3 = ((f32[8,64,128]{2,1,0:T(8,128)}), f32[8,64,128]{2,1,0:T(8,128)S(1)}, u32[]{:S(2)}, u32[]{:S(2)}) async-start(f32[8,64,128]{2,1,0:T(8,128)} %get-tuple-element.34), calls=%async_computation.3 | async-start | bytes 524288 | tf_op jit(solution)/shard_map/all_to_all | solution.py:496
  104.0 1.2 shard_map.159
  105.2 5.7 %all-to-all-done.3.d_ref = f32[8,64,128]{2,1,0:T(8,128)S(1)} async-done(((f32[8,64,128]{2,1,0:T(8,128)}), f32[8,64,128]{2,1,0:T(8,128)S(1)}, u32[]{:S(2)}, u32[]{:S(2)}) %all-to-all-start.3) | async-done | bytes 262176 | tf_op jit(solution)/shard_map/all_to_all | solution.py:496
  110.9 5.7 %all-to-all-start.6 = ((f32[8,64,128]{2,1,0:T(8,128)}), f32[8,64,128]{2,1,0:T(8,128)S(1)}, u32[]{:S(2)}, u32[]{:S(2)}) async-start(f32[8,64,128]{2,1,0:T(8,128)} %shard_map.159), calls=%async_computation.6 | async-start | bytes 524288 | tf_op jit(solution)/shard_map/all_to_all | solution.py:496
  116.6 2.1 %zones.1 = (f32[3,4,64,128]{3,2,1,0:T(8,128)}, f32[64,128]{1,0:T(8,128)}, f32[16,128]{1,0:T(8,128)}) custom-call(f32[3,8]{1,0:T(4,128)} %table_ref.3, s32[4,64,128]{2,1,0:T(8,128)} %zones_ref.3, f32[3,3,4,64,128]{4,3,2,1,0:T(8,128)} %stress_ref.5, f32[3,3,4,64,128]{4,3,2,1,0:T(8,128)} %stress_ref.5), custom_call_target="tpu_custom_call" | custom-call | tf_op jit(solution)/shard_map/zones/pallas_call | solution.py:519
  118.7 3.0 %collective-permute-start = (f32[64,128]{1,0:T(8,128)}, f32[64,128]{1,0:T(8,128)S(1)}, u32[]{:S(2)}, u32[]{:S(2)}) collective-permute-start(f32[64,128]{1,0:T(8,128)} %get-tuple-element.25), channel_id=1, source_target_pairs={{0,16},{16,32},{32,48},{48,64},{64,80},{80,96},{96,112},{112,0},{1... | collective-permute-start | bytes 98312 | tf_op jit(solution)/shard_map/ppermute | solution.py:501
  121.6 0.0 collective-permute-start.1
  121.6 5.4 %collective-permute-done.1.south_ref = f32[16,128]{1,0:T(8,128)S(1)} collective-permute-done((f32[16,128]{1,0:T(8,128)}, f32[16,128]{1,0:T(8,128)S(1)}, u32[]{:S(2)}, u32[]{:S(2)}) %collective-permute-start.1) | collective-permute-done | bytes 8224 | tf_op jit(solution)/shard_map/ppermute | solution.py:501
  127.0 0.0 collective-permute-done.west_ref
  127.0 2.5 %shard_map.149 = (f32[3,4,64,128]{3,2,1,0:T(8,128)}, f32[64,128]{1,0:T(8,128)}, f32[16,128]{1,0:T(8,128)}) custom-call(f32[3,4,64,128]{3,2,1,0:T(8,128)} %velocity_ref.3, f32[3,3,4,64,128]{4,3,2,1,0:T(8,128)} %stress_ref.5, f32[64,128]{1,0:T(8,128)S(1)} %collective-permute-done.west_ref, f32[16,128]{1,0:T(8,128)S(1)} %collective-permute-done.1.south_ref, ...), custom_call_target="tpu_custom_call" | custom-call | tf_op jit(solution)/shard_map/pallas_call | solution.py:485
  129.5 0.0 collective-permute-start.2
  129.5 0.0 collective-permute-start.3
  129.5 1.6 %collective-permute-done.3.north_ref = f32[16,128]{1,0:T(8,128)S(1)} collective-permute-done((f32[16,128]{1,0:T(8,128)}, f32[16,128]{1,0:T(8,128)S(1)}, u32[]{:S(2)}, u32[]{:S(2)}) %collective-permute-start.3) | collective-permute-done | bytes 8224 | tf_op jit(solution)/shard_map/ppermute | solution.py:501
  131.1 6.2 %collective-permute-done.2.east_ref = f32[64,128]{1,0:T(8,128)S(1)} collective-permute-done((f32[64,128]{1,0:T(8,128)}, f32[64,128]{1,0:T(8,128)S(1)}, u32[]{:S(2)}, u32[]{:S(2)}) %collective-permute-start.2) | collective-permute-done | bytes 32800 | tf_op jit(solution)/shard_map/ppermute | solution.py:501
  137.3 2.9 %shard_map.156 = (f32[3,4,64,128]{3,2,1,0:T(8,128)S(1)}, f32[3,3,4,64,128]{4,3,2,1,0:T(8,128)S(1)}, f32[64,128]{1,0:T(8,128)}, f32[16,128]{1,0:T(8,128)}) custom-call(f32[3,4,64,128]{3,2,1,0:T(8,128)} %get-tuple-element.28.early_ref, f32[64,128]{1,0:T(8,128)S(1)} %collective-permute-done.2.east_ref, f32[16,128]{1,0:T(8,128)S(1)} %collective-permute-done.3.north_ref, ...), custom_call_target="tpu_custom_call" | custom-call | tf_op jit(solution)/shard_map/pallas_call | solution.py:485
  140.2 0.0 collective-permute-start.5
  140.2 0.1 collective-permute-start.6
  140.3 5.4 %collective-permute-done.6.south_ref = f32[16,128]{1,0:T(8,128)S(1)} collective-permute-done((f32[16,128]{1,0:T(8,128)}, f32[16,128]{1,0:T(8,128)S(1)}, u32[]{:S(2)}, u32[]{:S(2)}) %collective-permute-start.6) | collective-permute-done | bytes 8224 | tf_op jit(solution)/shard_map/ppermute | solution.py:501
  145.7 0.0 collective-permute-done.5.west_ref
  145.7 1.0 shard_map.157
  146.7 2.0 %collective-permute-start.7 = (f32[64,128]{1,0:T(8,128)}, f32[64,128]{1,0:T(8,128)S(1)}, u32[]{:S(2)}, u32[]{:S(2)}) collective-permute-start(f32[64,128]{1,0:T(8,128)} %get-tuple-element.40), channel_id=1, source_target_pairs={{0,112},{16,0},{32,16},{48,32},{64,48},{80,64},{96,80},{112,96},{1... | collective-permute-start | bytes 98312 | tf_op jit(solution)/shard_map/ppermute | solution.py:501
  148.6 0.0 collective-permute-start.8
  148.6 1.6 %collective-permute-done.8.north_ref = f32[16,128]{1,0:T(8,128)S(1)} collective-permute-done((f32[16,128]{1,0:T(8,128)}, f32[16,128]{1,0:T(8,128)S(1)}, u32[]{:S(2)}, u32[]{:S(2)}) %collective-permute-start.8) | collective-permute-done | bytes 8224 | tf_op jit(solution)/shard_map/ppermute | solution.py:501
  150.2 4.2 %collective-permute-done.7.east_ref = f32[64,128]{1,0:T(8,128)S(1)} collective-permute-done((f32[64,128]{1,0:T(8,128)}, f32[64,128]{1,0:T(8,128)S(1)}, u32[]{:S(2)}, u32[]{:S(2)}) %collective-permute-start.7) | collective-permute-done | bytes 32800 | tf_op jit(solution)/shard_map/ppermute | solution.py:501
  154.4 1.5 shard_map.160
  (10 shorter events, 0.0 us)
Async XLA Ops:
  0.6 18.2 %copy-start.1 = (bf16[2,256,256]{2,1,0:T(8,128)(2,1)S(1)}, bf16[2,256,256]{2,1,0:T(8,128)(2,1)}, u32[]{:S(2)}) copy-start(bf16[2,256,256]{2,1,0:T(8,128)(2,1)} %constant.21.mx_ref) | copy-start | bytes 786436
  0.6 18.2 %copy-start.2 = (f32[2,8,8,128]{3,2,1,0:T(8,128)S(1)}, f32[2,8,8,128]{3,2,1,0:T(8,128)}, u32[]{:S(2)}) copy-start(f32[2,8,8,128]{3,2,1,0:T(8,128)} %constant.10.clone.twist_ref) | copy-start | bytes 196612
  20.1 19.0 %all-to-all-start.1 = ((f32[128,1,896]{2,1,0:T(1,128)}), f32[128,1,896]{2,1,0:T(1,128)S(1)}, u32[]{:S(2)}, u32[]{:S(2)}) async-start(f32[128,1,896]{2,1,0:T(1,128)} %bitcast), calls=%async_computation.1 | async-start | bytes 917504 | tf_op jit(solution)/shard_map/all_to_all | solution.py:491
  32.1 7.0 %copy-start.4 = (bf16[2,256,256]{2,1,0:T(8,128)(2,1)S(1)}, bf16[2,256,256]{2,1,0:T(8,128)(2,1)}, u32[]{:S(2)}) copy-start(bf16[2,256,256]{2,1,0:T(8,128)(2,1)} %constant.28.my_ref) | copy-start | bytes 786436
  32.1 7.0 %copy-start.5 = (f32[2,8,128]{2,1,0:T(8,128)S(1)}, f32[2,8,128]{2,1,0:T(8,128)}, u32[]{:S(2)}) copy-start(f32[2,8,128]{2,1,0:T(8,128)} %constant.11.clone.ahead_ref) | copy-start | bytes 24580
  42.3 17.7 %all-to-all-start.2 = ((f32[128,1,896]{2,1,0:T(1,128)}), f32[128,1,896]{2,1,0:T(1,128)S(1)}, u32[]{:S(2)}, u32[]{:S(2)}) async-start(f32[128,1,896]{2,1,0:T(1,128)} %bitcast.3), calls=%async_computation.2 | async-start | bytes 917504 | tf_op jit(solution)/shard_map/all_to_all | solution.py:491
  49.1 0.7 collective-permute-start.4
  61.7 17.5 %all-to-all-start.4 = ((f32[128,1,896]{2,1,0:T(1,128)}), f32[128,1,896]{2,1,0:T(1,128)S(1)}, u32[]{:S(2)}, u32[]{:S(2)}) async-start(f32[128,1,896]{2,1,0:T(1,128)} %bitcast.5), calls=%async_computation.4 | async-start | bytes 917504 | tf_op jit(solution)/shard_map/all_to_all | solution.py:491
  98.5 12.4 %all-to-all-start.3 = ((f32[8,64,128]{2,1,0:T(8,128)}), f32[8,64,128]{2,1,0:T(8,128)S(1)}, u32[]{:S(2)}, u32[]{:S(2)}) async-start(f32[8,64,128]{2,1,0:T(8,128)} %get-tuple-element.34), calls=%async_computation.3 | async-start | bytes 524288 | tf_op jit(solution)/shard_map/all_to_all | solution.py:496
  110.9 43.5 %all-to-all-start.6 = ((f32[8,64,128]{2,1,0:T(8,128)}), f32[8,64,128]{2,1,0:T(8,128)S(1)}, u32[]{:S(2)}, u32[]{:S(2)}) async-start(f32[8,64,128]{2,1,0:T(8,128)} %shard_map.159), calls=%async_computation.6 | async-start | bytes 524288 | tf_op jit(solution)/shard_map/all_to_all | solution.py:496
  118.7 8.4 %collective-permute-start = (f32[64,128]{1,0:T(8,128)}, f32[64,128]{1,0:T(8,128)S(1)}, u32[]{:S(2)}, u32[]{:S(2)}) collective-permute-start(f32[64,128]{1,0:T(8,128)} %get-tuple-element.25), channel_id=1, source_target_pairs={{0,16},{16,32},{32,48},{48,64},{64,80},{80,96},{96,112},{112,0},{1... | collective-permute-start | bytes 98312 | tf_op jit(solution)/shard_map/ppermute | solution.py:501
  121.6 5.4 %collective-permute-start.1 = (f32[16,128]{1,0:T(8,128)}, f32[16,128]{1,0:T(8,128)S(1)}, u32[]{:S(2)}, u32[]{:S(2)}) collective-permute-start(f32[16,128]{1,0:T(8,128)} %get-tuple-element.26), channel_id=1, source_target_pairs={{0,1},{1,2},{2,3},{3,4},{4,5},{5,6},{6,7},{7,8},{8,9},{9,10},{10,1... | collective-permute-start | bytes 24584 | tf_op jit(solution)/shard_map/ppermute | solution.py:501
  129.5 7.7 %collective-permute-start.2 = (f32[64,128]{1,0:T(8,128)}, f32[64,128]{1,0:T(8,128)S(1)}, u32[]{:S(2)}, u32[]{:S(2)}) collective-permute-start(f32[64,128]{1,0:T(8,128)} %get-tuple-element.29), channel_id=1, source_target_pairs={{0,112},{16,0},{32,16},{48,32},{64,48},{80,64},{96,80},{112,96},{1... | collective-permute-start | bytes 98312 | tf_op jit(solution)/shard_map/ppermute | solution.py:501
  129.5 1.6 %collective-permute-start.3 = (f32[16,128]{1,0:T(8,128)}, f32[16,128]{1,0:T(8,128)S(1)}, u32[]{:S(2)}, u32[]{:S(2)}) collective-permute-start(f32[16,128]{1,0:T(8,128)} %get-tuple-element.30), channel_id=1, source_target_pairs={{0,15},{1,0},{2,1},{3,2},{4,3},{5,4},{6,5},{7,6},{8,7},{9,8},{10,9... | collective-permute-start | bytes 24584 | tf_op jit(solution)/shard_map/ppermute | solution.py:501
  137.3 8.4 %copy-start = (f32[3,4,64,128]{3,2,1,0:T(8,128)S(1)}, f32[3,4,64,128]{3,2,1,0:T(8,128)}, u32[]{:S(2)}) copy-start(f32[3,4,64,128]{3,2,1,0:T(8,128)} %get-tuple-element.27.coef_ref) | copy-start | bytes 1179652
  140.2 14.2 %copy-start.3 = (s32[3,4,64,128]{3,2,1,0:T(8,128)S(1)}, s32[3,4,64,128]{3,2,1,0:T(8,128)}, u32[]{:S(2)}) copy-start(s32[3,4,64,128]{3,2,1,0:T(8,128)} %mask_ref.3) | copy-start | bytes 1179652
  140.2 5.5 %collective-permute-start.5 = (f32[64,128]{1,0:T(8,128)}, f32[64,128]{1,0:T(8,128)S(1)}, u32[]{:S(2)}, u32[]{:S(2)}) collective-permute-start(f32[64,128]{1,0:T(8,128)} %get-tuple-element.37), channel_id=1, source_target_pairs={{0,16},{16,32},{32,48},{48,64},{64,80},{80,96},{96,112},{112,0},{1... | collective-permute-start | bytes 98312 | tf_op jit(solution)/shard_map/ppermute | solution.py:501
  140.2 5.5 %collective-permute-start.6 = (f32[16,128]{1,0:T(8,128)}, f32[16,128]{1,0:T(8,128)S(1)}, u32[]{:S(2)}, u32[]{:S(2)}) collective-permute-start(f32[16,128]{1,0:T(8,128)} %get-tuple-element.38), channel_id=1, source_target_pairs={{0,1},{1,2},{2,3},{3,4},{4,5},{5,6},{6,7},{7,8},{8,9},{9,10},{10,1... | collective-permute-start | bytes 24584 | tf_op jit(solution)/shard_map/ppermute | solution.py:501
  146.7 7.7 %collective-permute-start.7 = (f32[64,128]{1,0:T(8,128)}, f32[64,128]{1,0:T(8,128)S(1)}, u32[]{:S(2)}, u32[]{:S(2)}) collective-permute-start(f32[64,128]{1,0:T(8,128)} %get-tuple-element.40), channel_id=1, source_target_pairs={{0,112},{16,0},{32,16},{48,32},{64,48},{80,64},{96,80},{112,96},{1... | collective-permute-start | bytes 98312 | tf_op jit(solution)/shard_map/ppermute | solution.py:501
  148.6 1.6 %collective-permute-start.8 = (f32[16,128]{1,0:T(8,128)}, f32[16,128]{1,0:T(8,128)S(1)}, u32[]{:S(2)}, u32[]{:S(2)}) collective-permute-start(f32[16,128]{1,0:T(8,128)} %get-tuple-element.41), channel_id=1, source_target_pairs={{0,15},{1,0},{2,1},{3,2},{4,3},{5,4},{6,5},{7,6},{8,7},{9,8},{10,9... | collective-permute-start | bytes 24584 | tf_op jit(solution)/shard_map/ppermute | solution.py:501
